TPU v7x, 32 devices: a whole 2x2x4 slice. The times are simulated.
32 devices in a mesh: head: 2 (over x), blk: 16 (over z, y, core).
Axes of the slice: x: 2, y: 2, z: 4, core: 2. Of those that a mesh axis runs over, the one named last changes fastest.
Arguments:
- queries: bfloat16 [12288, 2560], P(('blk', 'head')), may hold values from -100 to 100
- key_rows: bfloat16 [12288, 2560], P(('blk', 'head')), may hold values from -4.5 to 4.5
- value_rows: bfloat16 [12288, 2560], P(('blk', 'head')), may hold values from -6 to 6
- key_tiles: int32 [96, 16], replicated, may hold values from 0 to 95, as said below
- tile_count: int32 [96], replicated, may hold values from 8 to 16, as said below
Outputs:
- attended: bfloat16 [12288, 2560], P(('blk', 'head'))
Inputs may be any that keep to these rules, and one draw needn't show every extreme that they name: `key_tiles`: tile ids. Row q lists tile_count[q] distinct tiles first, the first being q itself; later entries equal q. With s = q // 6, every listed tile lies in slab s, in the upper half of slab s - 1, in the lower half of slab s + 1, or in slab s - 16 // 2**k or s + 16 // 2**k for k = 1 to 3; all query tiles of one slab that list a tile of such a distant slab list the same tile of it. `tile_count`: 16 is reached in every draw.
All inputs are finite; a program needn't handle non-finite values.
Results may differ from a plain program's by a relative error of at most 0.0034.
Values may be sent and summed in bfloat16 or wider, within the bound.
No kernel may reach another device: no remote copies, remote signals or barrier semaphores. Data moves between devices by JAX's collectives and lax.ppermute only.
A program may use at most 128 MiB of HBM per device.

v0:
```python
import functools
import math

import jax
import jax.numpy as jnp
from jax import lax
from jax.experimental import pallas as pl
from jax.experimental.pallas import tpu as pltpu
from jax.sharding import PartitionSpec as P


HD = 128
TILE = 128
FAR = 3


masked_value = -1e30
exp2_scale = math.log2(math.e) / math.sqrt(HD)
across = (((1,), (1,)), ((), ()))
anywhere = pl.BlockSpec(memory_space=pl.ANY)


def columns_of(array, side, low, width):
    half = array.shape[1] // 2
    first = lax.slice_in_dim(array, low, low + width, axis=1)
    second = lax.slice_in_dim(array, half + low, half + low + width, axis=1)
    return jnp.where(side == 0, first, second)


def distant_kernel(half, low_col, width, meta, key, value, received, *rest):
    outs, sems = rest[:-1], rest[-1]
    first = pl.multiple_of(meta[0] * width_of(key) + low_col, HD)
    copies = []
    for i, out in enumerate(outs):
        slot = meta[1 + i]
        own = slot < half
        rows = pl.ds(pl.multiple_of(lax.rem(slot, half) * TILE, TILE), TILE)
        cols = pl.ds(first, width)
        for j, source in enumerate((key, value)):
            sem = sems.at[i, j]
            mine = pltpu.make_async_copy(source.at[rows, cols], out.at[j], sem)
            theirs = pltpu.make_async_copy(received.at[j, rows, :], out.at[j], sem)
            pl.when(own)(mine.start)
            pl.when(jnp.logical_not(own))(theirs.start)
            copies.append(theirs)
    for copy in copies:
        copy.wait()


def width_of(ref):
    return ref.shape[1] // 2


def select_distant(meta, key, value, received, low_col, count, half):
    width = received.shape[2]
    shape = jax.ShapeDtypeStruct((2, TILE, width), key.dtype)
    return pl.pallas_call(
        functools.partial(distant_kernel, half, low_col, width),
        out_shape=[shape] * count,
        grid_spec=pltpu.PrefetchScalarGridSpec(
            num_scalar_prefetch=1,
            grid=(),
            in_specs=[anywhere] * 3,
            out_specs=[pl.BlockSpec(memory_space=pltpu.VMEM)] * count,
            scratch_shapes=[pltpu.SemaphoreType.DMA((count, 2))],
        ),
    )(meta, key, value, received)


def attend_kernel(allowed, where, q_own, q_rec, k_own, v_own, kv_rec, rim_a, rim_b, *rest):
    far, (o_own, o_send) = rest[:-2], rest[-2:]
    tiles = q_own.shape[0] // TILE
    keys = jnp.concatenate([k_own[...], kv_rec[0], rim_a[0], rim_b[0]] + [d[0] for d in far], 0)
    values = jnp.concatenate([v_own[...], kv_rec[1], rim_a[1], rim_b[1]] + [d[1] for d in far], 0)
    slots = keys.shape[0] // TILE
    for q_ref, o_ref, base in ((q_own, o_own, 0), (q_rec, o_send, tiles)):
        scores = lax.dot_general(q_ref[...], keys, across, preferred_element_type=jnp.float32)
        rounded, totals = [], []
        for t in range(tiles):
            rows = slice(t * TILE, (t + 1) * TILE)
            cells = [
                jnp.where(
                    allowed[base + t, j] > 0,
                    scores[rows, j * TILE : (j + 1) * TILE],
                    masked_value,
                )
                for j in range(slots)
            ]
            largest = jnp.max(functools.reduce(jnp.maximum, cells), -1, keepdims=True)
            weights = [jnp.exp2((cell - largest) * exp2_scale) for cell in cells]
            totals.append(jnp.sum(functools.reduce(jnp.add, weights), -1, keepdims=True))
            rounded.append(jnp.concatenate([w.astype(jnp.bfloat16) for w in weights], 1))
        mixture = jnp.dot(
            jnp.concatenate(rounded, 0), values, preferred_element_type=jnp.float32
        )
        o_ref[...] = (mixture / jnp.concatenate(totals, 0)).astype(o_ref.dtype)


def attend(allowed, where, arrays, result, chunk_low, low, high, heads_here):
    queries, q_rec, key, value, kv_rec, rim_a, rim_b, far = arrays
    rows = queries.shape[0]
    own = pl.BlockSpec((rows, HD), lambda i, a, w: (0, w[0] * heads_here + low + i))
    flat = pl.BlockSpec((rows, HD), lambda i, a, w: (0, low + i))
    whole = pl.BlockSpec((2, rows, HD), lambda i, a, w: (0, 0, low + i))
    part = pl.BlockSpec((2, rows, HD), lambda i, a, w: (0, 0, low - chunk_low + i))
    tile = pl.BlockSpec((2, TILE, HD), lambda i, a, w: (0, 0, low - chunk_low + i))
    out = pl.BlockSpec((rows, HD), lambda i, a, w: (0, i))
    shape = jax.ShapeDtypeStruct((rows, (high - low) * HD), queries.dtype)
    inputs = [queries, q_rec, key, value, kv_rec, rim_a, rim_b, *far]
    specs = [own, flat, own, own, part, whole, part] + [tile] * len(far)
    aliases = {}
    kernel = attend_kernel
    if result is not None:
        kernel = functools.partial(skip_operand, attend_kernel, 2 + len(inputs))
        aliases = {2 + len(inputs): 0}
        inputs, specs = inputs + [result], specs + [anywhere]
    return pl.pallas_call(
        kernel,
        out_shape=[jax.ShapeDtypeStruct(queries.shape, queries.dtype), shape],
        grid_spec=pltpu.PrefetchScalarGridSpec(
            num_scalar_prefetch=2,
            grid=(high - low,),
            in_specs=specs,
            out_specs=[own, out],
        ),
        input_output_aliases=aliases,
    )(allowed, where, *inputs)


def skip_operand(kernel, index, *refs):
    kernel(*refs[:index], *refs[index + 1 :])


def place_kernel(lows, heads_here, where, *refs):
    count = len(lows)
    pieces, out, held, sems = refs[:count], refs[count + 1], refs[count + 2 : -1], refs[-1]
    loads, stores = [], []
    for i, low in enumerate(lows):
        cols = pl.ds(pl.multiple_of(((1 - where[0]) * heads_here + low) * HD, HD), held[i].shape[1])
        loads.append(pltpu.make_async_copy(pieces[i], held[i], sems.at[0, i]))
        stores.append(pltpu.make_async_copy(held[i], out.at[:, cols], sems.at[1, i]))
    for load in loads:
        load.start()
    for load, store in zip(loads, stores):
        load.wait()
        store.start()
    for store in stores:
        store.wait()


def place(where, pieces, lows, result, heads_here):
    return pl.pallas_call(
        functools.partial(place_kernel, lows, heads_here),
        out_shape=jax.ShapeDtypeStruct(result.shape, result.dtype),
        grid_spec=pltpu.PrefetchScalarGridSpec(
            num_scalar_prefetch=1,
            grid=(),
            in_specs=[anywhere] * (len(pieces) + 1),
            out_specs=anywhere,
            scratch_shapes=[pltpu.VMEM(piece.shape, piece.dtype) for piece in pieces]
            + [pltpu.SemaphoreType.DMA((2, len(pieces)))],
        ),
        input_output_aliases={1 + len(pieces): 0},
    )(where, *pieces, result)


def on_device(queries, key_rows, value_rows, key_tiles, tile_count):
    tok_rows, row_width = queries.shape
    side = lax.axis_index("head")
    slab = lax.axis_index("blk")
    slabs = lax.axis_size("blk")
    group_width = row_width // 2
    heads_here = group_width // HD
    half = tok_rows // TILE
    slab_tiles = 2 * half

    shifts = [(0, slabs // 2)]
    for level in range(2, FAR + 1):
        shifts += [(1, slabs // 2**level), (-1, slabs // 2**level)]
    live = jnp.arange(key_tiles.shape[1], dtype=jnp.int32)[None, :] < tile_count[:, None]
    listed_slab = key_tiles // slab_tiles
    within = key_tiles % slab_tiles
    turned = (within + half * side) % slab_tiles
    mine = jnp.where(live & (listed_slab == slab), turned, 0)
    chosen = jnp.max(mine.reshape(slabs, -1), axis=1)
    readers = [
        (slab + shifts[0][1]) % slabs if direction == 0 else jnp.clip(slab + direction * far, 0, slabs - 1)
        for direction, far in shifts
    ]
    sent_slots = chosen[jnp.stack(readers)]
    where = side.astype(jnp.int32)[None]
    meta = jnp.concatenate([where, sent_slots])

    offset = listed_slab - slab
    slots = jnp.where(offset == 0, turned, -1)
    slots = jnp.where(offset == -1, 2 * half + half * (1 - side) + within - half, slots)
    slots = jnp.where(offset == 1, 2 * half + half * side + within, slots)
    for i, (direction, far) in enumerate(shifts):
        hit = (jnp.abs(offset) == far) if direction == 0 else (offset == -direction * far)
        slots = jnp.where(hit, 4 * half + i, slots)
    slots = jnp.where(live, slots, -1)
    slots = lax.dynamic_slice_in_dim(slots, slab * slab_tiles, slab_tiles, 0)
    slots = jnp.where(side == 0, slots, jnp.roll(slots, half, axis=0))
    slot_total = 4 * half + len(shifts)
    allowed = jnp.any(
        slots[:, :, None] == jnp.arange(slot_total, dtype=jnp.int32)[None, None, :], axis=1
    ).astype(jnp.int32)

    swap = [(0, 1), (1, 0)]
    chunks = chunk_bounds(heads_here)

    def outward(direction):
        return [
            (g * slabs + s, g * slabs + s + step)
            for g, step in ((0, -direction), (1, direction))
            for s in range(slabs)
            if 0 <= s + step < slabs
        ]

    kv_rec = []
    rim_a = None
    for c, (low, high) in enumerate(chunks):
        width = (high - low) * HD
        packed = jnp.stack(
            [columns_of(array, 1 - side, low * HD, width) for array in (key_rows, value_rows)]
        )
        kv_rec.append(lax.ppermute(packed, "head", swap))
        if c == 0:
            rim_a = lax.ppermute(
                jnp.stack(
                    [columns_of(array, side, 0, group_width) for array in (key_rows, value_rows)]
                ),
                ("head", "blk"),
                outward(1),
            )
    q_rec = lax.ppermute(columns_of(queries, 1 - side, 0, group_width), "head", swap)

    gathered = []
    for c, (low, high) in enumerate(chunks):
        rim_b = lax.ppermute(kv_rec[c], ("head", "blk"), outward(-1))
        tiles = select_distant(meta, key_rows, value_rows, kv_rec[c], low * HD, len(shifts), half)
        far = []
        for (direction, distance), tile in zip(shifts, tiles):
            if direction == 0:
                pairs = [(s, (s + distance) % slabs) for s in range(slabs)]
            else:
                step = direction * distance
                pairs = [(s, s + step) for s in range(slabs) if 0 <= s + step < slabs]
            far.append(lax.ppermute(tile, "blk", pairs))
        gathered.append((rim_b, far))
    result, returned = None, []
    for c, a, b in head_runs(heads_here):
        rim_b, far = gathered[c]
        arrays = (queries, q_rec, key_rows, value_rows, kv_rec[c], rim_a, rim_b, far)
        result, sent = attend(allowed, where, arrays, result, chunks[c][0], a, b, heads_here)
        returned.append((a, lax.ppermute(sent, "head", swap)))
    result = place(
        where, [p for _, p in returned[:-1]], [a for a, _ in returned[:-1]], result, heads_here
    )
    result = place(where, [returned[-1][1]], [returned[-1][0]], result, heads_here)
    return result


def chunk_bounds(heads):
    cuts = [0, heads * 3 // 10, heads * 7 // 10, heads]
    return list(zip(cuts[:-1], cuts[1:]))


def head_runs(heads):
    runs = []
    for c, (low, high) in enumerate(chunk_bounds(heads)):
        cuts = [low, high] if c == 0 else [low, low + (high - low + 1) // 2, high]
        runs += [(c, a, b) for a, b in zip(cuts[:-1], cuts[1:])]
    return runs


def solution(mesh):
    placed = (
        P(("blk", "head"), None),
        P(("blk", "head"), None),
        P(("blk", "head"), None),
        P(),
        P(),
    )

    return jax.shard_map(
        on_device, mesh=mesh, in_specs=placed, out_specs=P(("blk", "head"), None), check_vma=False
    )
```

profile of v0, /device:TPU:12, one launch (start us, length us, event | category | flops | bytes accessed | tf_op | source)
XLA Modules:
  0.0 235.2 jit_solution(4900949795481839152)
XLA Ops:
  0.0 2.7 %select_bitcast_fusion.4 = (bf16[1,384,384]{2,1,0:T(8,128)(2,1)S(1)}, bf16[1,384,384]{2,1,0:T(8,128)(2,1)}, bf16[1,384,384]{2,1,0:T(8,128)(2,1)}, bf16[1,384,384]{2,1,0:T(8,128)(2,1)S(1)}) fusion(bf16[384,2560]{1,0:T(8,128)(2,1)} %refs_5_.7, pred[]{:T(512)S(6)} %eq.95, bf16[384,2560]{1,0:T(8,128)(2,1)} %refs_4_.7), kind=kLoop, calls=%fused_computation.10 | loop fusion | flops 589824 | bytes 3538945 | tf_op jit(solution)/shard_map/stack | solution.py:224
  2.7 0.9 pad_maximum_fusion.3
  3.6 1.5 collective-permute-start.16
  5.1 1.7 select_bitcast_fusion
  6.8 1.4 pad_maximum_fusion
  8.3 1.9 collective-permute-start.2
  10.2 1.1 slice_select_fusion
  11.8 1.2 select_bitcast_fusion.2
  13.0 1.0 pad_maximum_fusion.1
  14.0 1.5 collective-permute-start.9
  15.5 0.9 pad_maximum_fusion.2
  18.6 1.4 collective-permute-done.16.received.kv_rec
  20.9 3.0 %shard_map.57 = (bf16[2,128,384]{2,1,0:T(8,128)(2,1)}, bf16[2,128,384]{2,1,0:T(8,128)(2,1)}, bf16[2,128,384]{2,1,0:T(8,128)(2,1)}, bf16[2,128,384]{2,1,0:T(8,128)(2,1)}, bf16[2,128,384]{2,1,0:T(8,128)(2,1)}) custom-call(s32[6]{0:T(128)} %pad_add_fusion.meta, bf16[384,2560]{1,0:T(8,128)(2,1)} %refs_4_.7, bf16[384,2560]{1,0:T(8,128)(2,1)} %refs_5_.7, ...), custom_call_target="tpu_custom_call" | custom-call | tf_op jit(solution)/shard_map/pallas_call | solution.py:57
  23.9 2.7 %collective-permute-start.18 = (bf16[2,128,384]{2,1,0:T(8,128)(2,1)}, bf16[2,128,384]{2,1,0:T(8,128)(2,1)S(1)}, u32[]{:S(2)}, u32[]{:S(2)}) collective-permute-start(bf16[2,128,384]{2,1,0:T(8,128)(2,1)} %get-tuple-element.40), channel_id=1, source_target_pairs={{0,8},{1,9},{2,10},{3,11},{4,12},{5,13},{6,14},{7,15},{8,0},{9,1},... | collective-permute-start | bytes 589832 | tf_op jit(solution)/shard_map/ppermute | solution.py:249
  26.6 42.9 %collective-permute-done.1.received.refs_6_ = bf16[2,384,384]{2,1,0:T(8,128)(2,1)S(1)} collective-permute-done((bf16[2,384,384]{2,1,0:T(8,128)(2,1)}, bf16[2,384,384]{2,1,0:T(8,128)(2,1)S(1)}, u32[]{:S(2)}, u32[]{:S(2)}) %collective-permute-start.1) | collective-permute-done | bytes 589856 | tf_op jit(solution)/shard_map/ppermute | solution.py:227
  69.5 3.5 %collective-permute-start.19 = (bf16[2,128,384]{2,1,0:T(8,128)(2,1)}, bf16[2,128,384]{2,1,0:T(8,128)(2,1)S(1)}, u32[]{:S(2)}, u32[]{:S(2)}) collective-permute-start(bf16[2,128,384]{2,1,0:T(8,128)(2,1)} %get-tuple-element.41), channel_id=1, source_target_pairs={{0,4},{1,5},{2,6},{3,7},{4,8},{5,9},{6,10},{7,11},{8,12},{9,13},{1... | collective-permute-start | bytes 589832 | tf_op jit(solution)/shard_map/ppermute | solution.py:249
  73.0 2.4 %collective-permute-start.20 = (bf16[2,128,384]{2,1,0:T(8,128)(2,1)}, bf16[2,128,384]{2,1,0:T(8,128)(2,1)}, u32[]{:S(2)}, u32[]{:S(2)}) collective-permute-start(bf16[2,128,384]{2,1,0:T(8,128)(2,1)} %get-tuple-element.42), channel_id=1, source_target_pairs={{4,0},{5,1},{6,2},{7,3},{8,4},{9,5},{10,6},{11,7},{12,8},{13,9},{1... | collective-permute-start | bytes 589832 | tf_op jit(solution)/shard_map/ppermute | solution.py:249
  75.3 2.0 collective-permute-done.19.rest_1_
  77.4 3.4 %collective-permute-start.21 = (bf16[2,128,384]{2,1,0:T(8,128)(2,1)}, bf16[2,128,384]{2,1,0:T(8,128)(2,1)}, u32[]{:S(2)}, u32[]{:S(2)}) collective-permute-start(bf16[2,128,384]{2,1,0:T(8,128)(2,1)} %get-tuple-element.43), channel_id=1, source_target_pairs={{0,2},{1,3},{2,4},{3,5},{4,6},{5,7},{6,8},{7,9},{8,10},{9,11},{10,... | collective-permute-start | bytes 589832 | tf_op jit(solution)/shard_map/ppermute | solution.py:249
  80.9 2.4 %collective-permute-start.22 = (bf16[2,128,384]{2,1,0:T(8,128)(2,1)}, bf16[2,128,384]{2,1,0:T(8,128)(2,1)}, u32[]{:S(2)}, u32[]{:S(2)}) collective-permute-start(bf16[2,128,384]{2,1,0:T(8,128)(2,1)} %get-tuple-element.44), channel_id=1, source_target_pairs={{2,0},{3,1},{4,2},{5,3},{6,4},{7,5},{8,6},{9,7},{10,8},{11,9},{12,... | collective-permute-start | bytes 589832 | tf_op jit(solution)/shard_map/ppermute | solution.py:249
  83.3 3.1 %shard_map.55 = (bf16[2,128,384]{2,1,0:T(8,128)(2,1)}, bf16[2,128,384]{2,1,0:T(8,128)(2,1)}, bf16[2,128,384]{2,1,0:T(8,128)(2,1)}, bf16[2,128,384]{2,1,0:T(8,128)(2,1)}, bf16[2,128,384]{2,1,0:T(8,128)(2,1)}) custom-call(s32[6]{0:T(128)} %pad_add_fusion.meta, bf16[384,2560]{1,0:T(8,128)(2,1)} %refs_4_.7, bf16[384,2560]{1,0:T(8,128)(2,1)} %refs_5_.7, ...), custom_call_target="tpu_custom_call" | custom-call | tf_op jit(solution)/shard_map/pallas_call | solution.py:57
  86.4 3.3 %collective-permute-start.4 = (bf16[2,128,384]{2,1,0:T(8,128)(2,1)}, bf16[2,128,384]{2,1,0:T(8,128)(2,1)}, u32[]{:S(2)}, u32[]{:S(2)}) collective-permute-start(bf16[2,128,384]{2,1,0:T(8,128)(2,1)} %get-tuple-element.30), channel_id=1, source_target_pairs={{0,8},{1,9},{2,10},{3,11},{4,12},{5,13},{6,14},{7,15},{8,0},{9,1},... | collective-permute-start | bytes 589832 | tf_op jit(solution)/shard_map/ppermute | solution.py:249
  89.7 3.2 %shard_map.56 = (bf16[2,128,512]{2,1,0:T(8,128)(2,1)}, bf16[2,128,512]{2,1,0:T(8,128)(2,1)}, bf16[2,128,512]{2,1,0:T(8,128)(2,1)}, bf16[2,128,512]{2,1,0:T(8,128)(2,1)}, bf16[2,128,512]{2,1,0:T(8,128)(2,1)}) custom-call(s32[6]{0:T(128)} %pad_add_fusion.meta, bf16[384,2560]{1,0:T(8,128)(2,1)} %refs_4_.7, bf16[384,2560]{1,0:T(8,128)(2,1)} %refs_5_.7, ...), custom_call_target="tpu_custom_call" | custom-call | tf_op jit(solution)/shard_map/pallas_call | solution.py:57
  93.8 7.7 %collective-permute-done.22.rest_4_ = bf16[2,128,384]{2,1,0:T(8,128)(2,1)} collective-permute-done((bf16[2,128,384]{2,1,0:T(8,128)(2,1)}, bf16[2,128,384]{2,1,0:T(8,128)(2,1)}, u32[]{:S(2)}, u32[]{:S(2)}) %collective-permute-start.22) | collective-permute-done | bytes 196640 | tf_op jit(solution)/shard_map/ppermute | solution.py:249
  101.5 1.9 collective-permute-start.12
  103.4 1.9 collective-permute-start.5
  105.3 11.1 %collective-permute-done.5.refs_10_ = bf16[2,128,384]{2,1,0:T(8,128)(2,1)S(1)} collective-permute-done((bf16[2,128,384]{2,1,0:T(8,128)(2,1)}, bf16[2,128,384]{2,1,0:T(8,128)(2,1)S(1)}, u32[]{:S(2)}, u32[]{:S(2)}) %collective-permute-start.5) | collective-permute-done | bytes 196640 | tf_op jit(solution)/shard_map/ppermute | solution.py:249
  116.4 1.9 collective-permute-start.17
  118.4 1.9 collective-permute-start.13
  120.3 5.1 %collective-permute-start.14 = (bf16[2,128,512]{2,1,0:T(8,128)(2,1)}, bf16[2,128,512]{2,1,0:T(8,128)(2,1)}, u32[]{:S(2)}, u32[]{:S(2)}) collective-permute-start(bf16[2,128,512]{2,1,0:T(8,128)(2,1)} %get-tuple-element.38), channel_id=1, source_target_pairs={{0,2},{1,3},{2,4},{3,5},{4,6},{5,7},{6,8},{7,9},{8,10},{9,11},{10,... | collective-permute-start | bytes 786440 | tf_op jit(solution)/shard_map/ppermute | solution.py:249
  125.5 2.4 %collective-permute-start.10 = (bf16[2,384,512]{2,1,0:T(8,128)(2,1)}, bf16[2,384,512]{2,1,0:T(8,128)(2,1)S(1)}, u32[]{:S(2)}, u32[]{:S(2)}) collective-permute-start(bf16[2,384,512]{2,1,0:T(8,128)(2,1)} %copy-done.3), channel_id=1, source_target_pairs={{0,1},{1,2},{2,3},{3,4},{4,5},{5,6},{6,7},{7,8},{8,9},{9,10},{10,1... | collective-permute-start | bytes 2359304 | tf_op jit(solution)/shard_map/ppermute | solution.py:240
  128.2 4.0 %collective-permute-start.3 = (bf16[2,384,384]{2,1,0:T(8,128)(2,1)S(1)}, bf16[2,384,384]{2,1,0:T(8,128)(2,1)}, u32[]{:S(2)}, u32[]{:S(2)}) collective-permute-start(bf16[2,384,384]{2,1,0:T(8,128)(2,1)S(1)} %copy-done.5), channel_id=1, source_target_pairs={{0,1},{1,2},{2,3},{3,4},{4,5},{5,6},{6,7},{7,8},{8,9},{9,10},{10,1... | collective-permute-start | bytes 1769480 | tf_op jit(solution)/shard_map/ppermute | solution.py:240
  132.5 3.5 %collective-permute-start.15 = (bf16[2,128,512]{2,1,0:T(8,128)(2,1)}, bf16[2,128,512]{2,1,0:T(8,128)(2,1)}, u32[]{:S(2)}, u32[]{:S(2)}) collective-permute-start(bf16[2,128,512]{2,1,0:T(8,128)(2,1)} %get-tuple-element.39), channel_id=1, source_target_pairs={{2,0},{3,1},{4,2},{5,3},{6,4},{7,5},{8,6},{9,7},{10,8},{11,9},{12,... | collective-permute-start | bytes 786440 | tf_op jit(solution)/shard_map/ppermute | solution.py:249
  136.2 17.3 %collective-permute-done.15.refs_13_ = bf16[2,128,512]{2,1,0:T(8,128)(2,1)} collective-permute-done((bf16[2,128,512]{2,1,0:T(8,128)(2,1)}, bf16[2,128,512]{2,1,0:T(8,128)(2,1)}, u32[]{:S(2)}, u32[]{:S(2)}) %collective-permute-start.15) | collective-permute-done | bytes 262176 | tf_op jit(solution)/shard_map/ppermute | solution.py:249
  153.5 1.9 collective-permute-start.6
  155.4 6.2 %collective-permute-start.7 = (bf16[2,128,384]{2,1,0:T(8,128)(2,1)}, bf16[2,128,384]{2,1,0:T(8,128)(2,1)S(1)}, u32[]{:S(2)}, u32[]{:S(2)}) collective-permute-start(bf16[2,128,384]{2,1,0:T(8,128)(2,1)} %get-tuple-element.33), channel_id=1, source_target_pairs={{0,2},{1,3},{2,4},{3,5},{4,6},{5,7},{6,8},{7,9},{8,10},{9,11},{10,... | collective-permute-start | bytes 589832 | tf_op jit(solution)/shard_map/ppermute | solution.py:249
  161.7 2.1 collective-permute-start.8
  164.5 14.0 %shard_map.58 = (bf16[384,2560]{1,0:T(8,128)(2,1)}, bf16[384,384]{1,0:T(8,128)(2,1)}) custom-call(s32[6,17]{1,0:T(8,128)} %convert_element_type.3.allowed.refs_0_, s32[1]{0:T(128)} %bitcast.where.refs_1_, bf16[384,2560]{1,0:T(8,128)(2,1)} %refs_2_.7, bf16[384,1280]{1,0:T(8,128)(2,1)} %copy-done.2, bf16[384,2560]{1,0:T(8,128)(2,1)} %refs_4_.7, ...), custom_call_target="tpu_custom_call" | custom-call | tf_op jit(solution)/shard_map/pallas_call | solution.py:117
  178.5 8.2 %collective-permute-start.24 = (bf16[384,384]{1,0:T(8,128)(2,1)}, bf16[384,384]{1,0:T(8,128)(2,1)S(1)}, u32[]{:S(2)}, u32[]{:S(2)}) collective-permute-start(bf16[384,384]{1,0:T(8,128)(2,1)} %get-tuple-element.50), channel_id=1, source_target_pairs={{0,16},{16,0},{1,17},{17,1},{2,18},{18,2},{3,19},{19,3},{4,20},{20... | collective-permute-start | bytes 884744 | tf_op jit(solution)/shard_map/ppermute | solution.py:256
  186.6 10.2 %shard_map.59 = (bf16[384,2560]{1,0:T(8,128)(2,1)}, bf16[384,256]{1,0:T(8,128)(2,1)}) custom-call(s32[6,17]{1,0:T(8,128)} %convert_element_type.3.allowed.refs_0_, s32[1]{0:T(128)} %bitcast.where.refs_1_, bf16[384,2560]{1,0:T(8,128)(2,1)} %refs_2_.7, bf16[384,1280]{1,0:T(8,128)(2,1)} %copy-done.2, ...), custom_call_target="tpu_custom_call", output_to_operand_aliasing={{0}: (14, {})} | custom-call | tf_op jit(solution)/shard_map/pallas_call | solution.py:117
  196.8 10.2 %shard_map.60 = (bf16[384,2560]{1,0:T(8,128)(2,1)}, bf16[384,256]{1,0:T(8,128)(2,1)}) custom-call(s32[6,17]{1,0:T(8,128)} %convert_element_type.3.allowed.refs_0_, s32[1]{0:T(128)} %bitcast.where.refs_1_, bf16[384,2560]{1,0:T(8,128)(2,1)} %refs_2_.7, bf16[384,1280]{1,0:T(8,128)(2,1)} %copy-done.2, ...), custom_call_target="tpu_custom_call", output_to_operand_aliasing={{0}: (14, {})} | custom-call | tf_op jit(solution)/shard_map/pallas_call | solution.py:117
  207.9 10.6 %shard_map.61 = (bf16[384,2560]{1,0:T(8,128)(2,1)}, bf16[384,256]{1,0:T(8,128)(2,1)}) custom-call(s32[6,17]{1,0:T(8,128)} %convert_element_type.3.allowed.refs_0_, s32[1]{0:T(128)} %bitcast.where.refs_1_, bf16[384,2560]{1,0:T(8,128)(2,1)} %refs_2_.7, bf16[384,1280]{1,0:T(8,128)(2,1)} %copy-done.2, ...), custom_call_target="tpu_custom_call", output_to_operand_aliasing={{0}: (14, {})} | custom-call | tf_op jit(solution)/shard_map/pallas_call | solution.py:117
  219.3 1.2 collective-permute-start.26
  221.4 6.4 %shard_map.62 = (bf16[384,2560]{1,0:T(8,128)(2,1)}, bf16[384,128]{1,0:T(8,128)(2,1)}) custom-call(s32[6,17]{1,0:T(8,128)} %convert_element_type.3.allowed.refs_0_, s32[1]{0:T(128)} %bitcast.where.refs_1_, bf16[384,2560]{1,0:T(8,128)(2,1)} %refs_2_.7, bf16[384,1280]{1,0:T(8,128)(2,1)} %copy-done.2, ...), custom_call_target="tpu_custom_call", output_to_operand_aliasing={{0}: (14, {})} | custom-call | tf_op jit(solution)/shard_map/pallas_call | solution.py:117
  227.7 1.2 collective-permute-start.23
  229.0 1.2 collective-permute-done.25.refs_1_
  230.9 1.9 shard_map.63.refs_1_
  233.5 1.5 shard_map.64
  (95 shorter events, 10.0 us)
Async XLA Ops:
  0.0 5.1 %copy-start = (bf16[384,2560]{1,0:T(8,128)(2,1)S(1)}, bf16[384,2560]{1,0:T(8,128)(2,1)}, u32[]{:S(2)}) copy-start(bf16[384,2560]{1,0:T(8,128)(2,1)} %refs_4_.7) | copy-start | bytes 5898244
  3.6 16.4 %collective-permute-start.16 = (bf16[2,384,384]{2,1,0:T(8,128)(2,1)}, bf16[2,384,384]{2,1,0:T(8,128)(2,1)S(1)}, u32[]{:S(2)}, u32[]{:S(2)}) collective-permute-start(bf16[2,384,384]{2,1,0:T(8,128)(2,1)} %pad_maximum_fusion.3), channel_id=1, source_target_pairs={{0,16},{16,0},{1,17},{17,1},{2,18},{18,2},{3,19},{19,3},{4,20},{20... | collective-permute-start | bytes 1769480 | tf_op jit(solution)/shard_map/ppermute | solution.py:227
  6.8 3.4 %copy-start.1 = (bf16[384,2560]{1,0:T(8,128)(2,1)S(1)}, bf16[384,2560]{1,0:T(8,128)(2,1)}, u32[]{:S(2)}) copy-start(bf16[384,2560]{1,0:T(8,128)(2,1)} %refs_2_.7) | copy-start | bytes 5898244
  8.3 153.4 %collective-permute-start.2 = (bf16[2,384,1280]{2,1,0:T(8,128)(2,1)}, bf16[2,384,1280]{2,1,0:T(8,128)(2,1)}, u32[]{:S(2)}, u32[]{:S(2)}) collective-permute-start(bf16[2,384,1280]{2,1,0:T(8,128)(2,1)} %pad_maximum_fusion), channel_id=1, source_target_pairs={{1,0},{2,1},{3,2},{4,3},{5,4},{6,5},{7,6},{8,7},{9,8},{10,9},{11,1... | collective-permute-start | bytes 5898248 | tf_op jit(solution)/shard_map/ppermute | solution.py:229
  11.3 4.2 %copy-start.9 = (bf16[1,384,384]{2,1,0:T(8,128)(2,1)S(1)}, bf16[1,384,384]{2,1,0:T(8,128)(2,1)}, u32[]{:S(2)}) copy-start(bf16[1,384,384]{2,1,0:T(8,128)(2,1)} %get-tuple-element.58) | copy-start | bytes 884740
  11.3 4.2 %copy-start.10 = (bf16[1,384,384]{2,1,0:T(8,128)(2,1)S(1)}, bf16[1,384,384]{2,1,0:T(8,128)(2,1)}, u32[]{:S(2)}) copy-start(bf16[1,384,384]{2,1,0:T(8,128)(2,1)} %get-tuple-element.70) | copy-start | bytes 884740
  11.3 107.1 %collective-permute-start = (bf16[384,1280]{1,0:T(8,128)(2,1)}, bf16[384,1280]{1,0:T(8,128)(2,1)S(1)}, u32[]{:S(2)}, u32[]{:S(2)}) collective-permute-start(bf16[384,1280]{1,0:T(8,128)(2,1)} %slice_select_fusion), channel_id=1, source_target_pairs={{0,16},{16,0},{1,17},{17,1},{2,18},{18,2},{3,19},{19,3},{4,20},{20... | collective-permute-start | bytes 2949128 | tf_op jit(solution)/shard_map/ppermute | solution.py:236
  13.0 4.0 %copy-start.23 = (s32[96,16]{0,1:T(8,128)S(1)}, s32[96,16]{0,1:T(8,128)}, u32[]{:S(2)}) copy-start(s32[96,16]{0,1:T(8,128)} %param.8) | copy-start | bytes 18436
  13.0 4.0 %copy-start.24 = (s32[96]{0:T(128)S(1)}, s32[96]{0:T(128)}, u32[]{:S(2)}) copy-start(s32[96]{0:T(128)} %param.9) | copy-start | bytes 1156
  14.0 72.4 %collective-permute-start.9 = (bf16[2,384,512]{2,1,0:T(8,128)(2,1)}, bf16[2,384,512]{2,1,0:T(8,128)(2,1)S(1)}, u32[]{:S(2)}, u32[]{:S(2)}) collective-permute-start(bf16[2,384,512]{2,1,0:T(8,128)(2,1)} %pad_maximum_fusion.1), channel_id=1, source_target_pairs={{0,16},{16,0},{1,17},{17,1},{2,18},{18,2},{3,19},{19,3},{4,20},{20... | collective-permute-start | bytes 2359304 | tf_op jit(solution)/shard_map/ppermute | solution.py:227
  16.4 53.1 %collective-permute-start.1 = (bf16[2,384,384]{2,1,0:T(8,128)(2,1)}, bf16[2,384,384]{2,1,0:T(8,128)(2,1)S(1)}, u32[]{:S(2)}, u32[]{:S(2)}) collective-permute-start(bf16[2,384,384]{2,1,0:T(8,128)(2,1)} %pad_maximum_fusion.2), channel_id=1, source_target_pairs={{0,16},{16,0},{1,17},{17,1},{2,18},{18,2},{3,19},{19,3},{4,20},{20... | collective-permute-start | bytes 1769480 | tf_op jit(solution)/shard_map/ppermute | solution.py:227
  23.9 49.1 %collective-permute-start.18 = (bf16[2,128,384]{2,1,0:T(8,128)(2,1)}, bf16[2,128,384]{2,1,0:T(8,128)(2,1)S(1)}, u32[]{:S(2)}, u32[]{:S(2)}) collective-permute-start(bf16[2,128,384]{2,1,0:T(8,128)(2,1)} %get-tuple-element.40), channel_id=1, source_target_pairs={{0,8},{1,9},{2,10},{3,11},{4,12},{5,13},{6,14},{7,15},{8,0},{9,1},... | collective-permute-start | bytes 589832 | tf_op jit(solution)/shard_map/ppermute | solution.py:249
  69.5 13.8 %copy-start.4 = (bf16[2,384,384]{2,1,0:T(8,128)(2,1)}, bf16[2,384,384]{2,1,0:T(8,128)(2,1)S(1)}, u32[]{:S(2)}) copy-start(bf16[2,384,384]{2,1,0:T(8,128)(2,1)S(1)} %collective-permute-done.1.received.refs_6_) | copy-start | bytes 1769476
  69.5 7.9 %collective-permute-start.19 = (bf16[2,128,384]{2,1,0:T(8,128)(2,1)}, bf16[2,128,384]{2,1,0:T(8,128)(2,1)S(1)}, u32[]{:S(2)}, u32[]{:S(2)}) collective-permute-start(bf16[2,128,384]{2,1,0:T(8,128)(2,1)} %get-tuple-element.41), channel_id=1, source_target_pairs={{0,4},{1,5},{2,6},{3,7},{4,8},{5,9},{6,10},{7,11},{8,12},{9,13},{1... | collective-permute-start | bytes 589832 | tf_op jit(solution)/shard_map/ppermute | solution.py:249
  73.0 13.4 %copy-start.20 = (bf16[2,128,384]{2,1,0:T(8,128)(2,1)}, bf16[2,128,384]{2,1,0:T(8,128)(2,1)S(1)}, u32[]{:S(2)}) copy-start(bf16[2,128,384]{2,1,0:T(8,128)(2,1)S(1)} %collective-permute-done.18.rest_0_) | copy-start | bytes 589828
  73.0 7.9 %collective-permute-start.20 = (bf16[2,128,384]{2,1,0:T(8,128)(2,1)}, bf16[2,128,384]{2,1,0:T(8,128)(2,1)}, u32[]{:S(2)}, u32[]{:S(2)}) collective-permute-start(bf16[2,128,384]{2,1,0:T(8,128)(2,1)} %get-tuple-element.42), channel_id=1, source_target_pairs={{4,0},{5,1},{6,2},{7,3},{8,4},{9,5},{10,6},{11,7},{12,8},{13,9},{1... | collective-permute-start | bytes 589832 | tf_op jit(solution)/shard_map/ppermute | solution.py:249
  77.3 9.0 %copy-start.21 = (bf16[2,128,384]{2,1,0:T(8,128)(2,1)}, bf16[2,128,384]{2,1,0:T(8,128)(2,1)S(1)}, u32[]{:S(2)}) copy-start(bf16[2,128,384]{2,1,0:T(8,128)(2,1)S(1)} %collective-permute-done.19.rest_1_) | copy-start | bytes 589828
  77.4 15.6 %collective-permute-start.21 = (bf16[2,128,384]{2,1,0:T(8,128)(2,1)}, bf16[2,128,384]{2,1,0:T(8,128)(2,1)}, u32[]{:S(2)}, u32[]{:S(2)}) collective-permute-start(bf16[2,128,384]{2,1,0:T(8,128)(2,1)} %get-tuple-element.43), channel_id=1, source_target_pairs={{0,2},{1,3},{2,4},{3,5},{4,6},{5,7},{6,8},{7,9},{8,10},{9,11},{10,... | collective-permute-start | bytes 589832 | tf_op jit(solution)/shard_map/ppermute | solution.py:249
  80.9 20.6 %collective-permute-start.22 = (bf16[2,128,384]{2,1,0:T(8,128)(2,1)}, bf16[2,128,384]{2,1,0:T(8,128)(2,1)}, u32[]{:S(2)}, u32[]{:S(2)}) collective-permute-start(bf16[2,128,384]{2,1,0:T(8,128)(2,1)} %get-tuple-element.44), channel_id=1, source_target_pairs={{2,0},{3,1},{4,2},{5,3},{6,4},{7,5},{8,6},{9,7},{10,8},{11,9},{12,... | collective-permute-start | bytes 589832 | tf_op jit(solution)/shard_map/ppermute | solution.py:249
  86.4 3.3 %copy-start.3 = (bf16[2,384,512]{2,1,0:T(8,128)(2,1)}, bf16[2,384,512]{2,1,0:T(8,128)(2,1)S(1)}, u32[]{:S(2)}) copy-start(bf16[2,384,512]{2,1,0:T(8,128)(2,1)S(1)} %collective-permute-done.9.received.refs_6_) | copy-start | bytes 2359300
  86.4 30.0 %copy-start.8 = (bf16[2,384,384]{2,1,0:T(8,128)(2,1)S(1)}, bf16[2,384,384]{2,1,0:T(8,128)(2,1)}, u32[]{:S(2)}) copy-start(bf16[2,384,384]{2,1,0:T(8,128)(2,1)} %copy-done.7) | copy-start | bytes 1769476
  86.4 41.7 %copy-start.5 = (bf16[2,384,384]{2,1,0:T(8,128)(2,1)S(1)}, bf16[2,384,384]{2,1,0:T(8,128)(2,1)}, u32[]{:S(2)}) copy-start(bf16[2,384,384]{2,1,0:T(8,128)(2,1)} %copy-done.4) | copy-start | bytes 1769476
  86.4 17.0 %collective-permute-start.4 = (bf16[2,128,384]{2,1,0:T(8,128)(2,1)}, bf16[2,128,384]{2,1,0:T(8,128)(2,1)}, u32[]{:S(2)}, u32[]{:S(2)}) collective-permute-start(bf16[2,128,384]{2,1,0:T(8,128)(2,1)} %get-tuple-element.30), channel_id=1, source_target_pairs={{0,8},{1,9},{2,10},{3,11},{4,12},{5,13},{6,14},{7,15},{8,0},{9,1},... | collective-permute-start | bytes 589832 | tf_op jit(solution)/shard_map/ppermute | solution.py:249
  92.9 27.4 %collective-permute-start.11 = (bf16[2,128,512]{2,1,0:T(8,128)(2,1)}, bf16[2,128,512]{2,1,0:T(8,128)(2,1)S(1)}, u32[]{:S(2)}, u32[]{:S(2)}) collective-permute-start(bf16[2,128,512]{2,1,0:T(8,128)(2,1)} %get-tuple-element.35), channel_id=1, source_target_pairs={{0,8},{1,9},{2,10},{3,11},{4,12},{5,13},{6,14},{7,15},{8,0},{9,1},... | collective-permute-start | bytes 786440 | tf_op jit(solution)/shard_map/ppermute | solution.py:249
  101.5 24.0 %collective-permute-start.12 = (bf16[2,128,512]{2,1,0:T(8,128)(2,1)}, bf16[2,128,512]{2,1,0:T(8,128)(2,1)S(1)}, u32[]{:S(2)}, u32[]{:S(2)}) collective-permute-start(bf16[2,128,512]{2,1,0:T(8,128)(2,1)} %get-tuple-element.36), channel_id=1, source_target_pairs={{0,4},{1,5},{2,6},{3,7},{4,8},{5,9},{6,10},{7,11},{8,12},{9,13},{1... | collective-permute-start | bytes 786440 | tf_op jit(solution)/shard_map/ppermute | solution.py:249
  103.4 13.0 %collective-permute-start.5 = (bf16[2,128,384]{2,1,0:T(8,128)(2,1)}, bf16[2,128,384]{2,1,0:T(8,128)(2,1)S(1)}, u32[]{:S(2)}, u32[]{:S(2)}) collective-permute-start(bf16[2,128,384]{2,1,0:T(8,128)(2,1)} %get-tuple-element.31), channel_id=1, source_target_pairs={{0,4},{1,5},{2,6},{3,7},{4,8},{5,9},{6,10},{7,11},{8,12},{9,13},{1... | collective-permute-start | bytes 589832 | tf_op jit(solution)/shard_map/ppermute | solution.py:249
  116.4 9.0 %copy-start.13 = (bf16[2,128,384]{2,1,0:T(8,128)(2,1)}, bf16[2,128,384]{2,1,0:T(8,128)(2,1)S(1)}, u32[]{:S(2)}) copy-start(bf16[2,128,384]{2,1,0:T(8,128)(2,1)S(1)} %collective-permute-done.5.refs_10_) | copy-start | bytes 589828
  116.4 39.0 %collective-permute-start.17 = (bf16[2,384,384]{2,1,0:T(8,128)(2,1)S(1)}, bf16[2,384,384]{2,1,0:T(8,128)(2,1)}, u32[]{:S(2)}, u32[]{:S(2)}) collective-permute-start(bf16[2,384,384]{2,1,0:T(8,128)(2,1)S(1)} %copy-done.8), channel_id=1, source_target_pairs={{0,1},{1,2},{2,3},{3,4},{4,5},{5,6},{6,7},{7,8},{8,9},{9,10},{10,1... | collective-permute-start | bytes 1769480 | tf_op jit(solution)/shard_map/ppermute | solution.py:240
  118.4 46.1 %copy-start.2 = (bf16[384,1280]{1,0:T(8,128)(2,1)}, bf16[384,1280]{1,0:T(8,128)(2,1)S(1)}, u32[]{:S(2)}) copy-start(bf16[384,1280]{1,0:T(8,128)(2,1)S(1)} %collective-permute-done.q_rec.refs_3_) | copy-start | bytes 2949124
  118.4 9.8 %collective-permute-start.13 = (bf16[2,128,512]{2,1,0:T(8,128)(2,1)}, bf16[2,128,512]{2,1,0:T(8,128)(2,1)}, u32[]{:S(2)}, u32[]{:S(2)}) collective-permute-start(bf16[2,128,512]{2,1,0:T(8,128)(2,1)} %get-tuple-element.37), channel_id=1, source_target_pairs={{4,0},{5,1},{6,2},{7,3},{8,4},{9,5},{10,6},{11,7},{12,8},{13,9},{1... | collective-permute-start | bytes 786440 | tf_op jit(solution)/shard_map/ppermute | solution.py:249
  120.3 58.1 %copy-start.11 = (bf16[2,128,512]{2,1,0:T(8,128)(2,1)}, bf16[2,128,512]{2,1,0:T(8,128)(2,1)S(1)}, u32[]{:S(2)}) copy-start(bf16[2,128,512]{2,1,0:T(8,128)(2,1)S(1)} %collective-permute-done.11.refs_9_) | copy-start | bytes 786436
  120.3 12.1 %collective-permute-start.14 = (bf16[2,128,512]{2,1,0:T(8,128)(2,1)}, bf16[2,128,512]{2,1,0:T(8,128)(2,1)}, u32[]{:S(2)}, u32[]{:S(2)}) collective-permute-start(bf16[2,128,512]{2,1,0:T(8,128)(2,1)} %get-tuple-element.38), channel_id=1, source_target_pairs={{0,2},{1,3},{2,4},{3,5},{4,6},{5,7},{6,8},{7,9},{8,10},{9,11},{10,... | collective-permute-start | bytes 786440 | tf_op jit(solution)/shard_map/ppermute | solution.py:249
  125.5 52.9 %copy-start.12 = (bf16[2,128,512]{2,1,0:T(8,128)(2,1)}, bf16[2,128,512]{2,1,0:T(8,128)(2,1)S(1)}, u32[]{:S(2)}) copy-start(bf16[2,128,512]{2,1,0:T(8,128)(2,1)S(1)} %collective-permute-done.12.refs_10_) | copy-start | bytes 786436
  125.5 52.9 %collective-permute-start.10 = (bf16[2,384,512]{2,1,0:T(8,128)(2,1)}, bf16[2,384,512]{2,1,0:T(8,128)(2,1)S(1)}, u32[]{:S(2)}, u32[]{:S(2)}) collective-permute-start(bf16[2,384,512]{2,1,0:T(8,128)(2,1)} %copy-done.3), channel_id=1, source_target_pairs={{0,1},{1,2},{2,3},{3,4},{4,5},{5,6},{6,7},{7,8},{8,9},{9,10},{10,1... | collective-permute-start | bytes 2359304 | tf_op jit(solution)/shard_map/ppermute | solution.py:240
  128.2 79.0 %collective-permute-start.3 = (bf16[2,384,384]{2,1,0:T(8,128)(2,1)S(1)}, bf16[2,384,384]{2,1,0:T(8,128)(2,1)}, u32[]{:S(2)}, u32[]{:S(2)}) collective-permute-start(bf16[2,384,384]{2,1,0:T(8,128)(2,1)S(1)} %copy-done.5), channel_id=1, source_target_pairs={{0,1},{1,2},{2,3},{3,4},{4,5},{5,6},{6,7},{7,8},{8,9},{9,10},{10,1... | collective-permute-start | bytes 1769480 | tf_op jit(solution)/shard_map/ppermute | solution.py:240
  132.5 21.0 %collective-permute-start.15 = (bf16[2,128,512]{2,1,0:T(8,128)(2,1)}, bf16[2,128,512]{2,1,0:T(8,128)(2,1)}, u32[]{:S(2)}, u32[]{:S(2)}) collective-permute-start(bf16[2,128,512]{2,1,0:T(8,128)(2,1)} %get-tuple-element.39), channel_id=1, source_target_pairs={{2,0},{3,1},{4,2},{5,3},{6,4},{7,5},{8,6},{9,7},{10,8},{11,9},{12,... | collective-permute-start | bytes 786440 | tf_op jit(solution)/shard_map/ppermute | solution.py:249
  153.5 53.6 %collective-permute-start.6 = (bf16[2,128,384]{2,1,0:T(8,128)(2,1)}, bf16[2,128,384]{2,1,0:T(8,128)(2,1)}, u32[]{:S(2)}, u32[]{:S(2)}) collective-permute-start(bf16[2,128,384]{2,1,0:T(8,128)(2,1)} %get-tuple-element.32), channel_id=1, source_target_pairs={{4,0},{5,1},{6,2},{7,3},{8,4},{9,5},{10,6},{11,7},{12,8},{13,9},{1... | collective-permute-start | bytes 589832 | tf_op jit(solution)/shard_map/ppermute | solution.py:249
  155.4 51.7 %collective-permute-start.7 = (bf16[2,128,384]{2,1,0:T(8,128)(2,1)}, bf16[2,128,384]{2,1,0:T(8,128)(2,1)S(1)}, u32[]{:S(2)}, u32[]{:S(2)}) collective-permute-start(bf16[2,128,384]{2,1,0:T(8,128)(2,1)} %get-tuple-element.33), channel_id=1, source_target_pairs={{0,2},{1,3},{2,4},{3,5},{4,6},{5,7},{6,8},{7,9},{8,10},{9,11},{10,... | collective-permute-start | bytes 589832 | tf_op jit(solution)/shard_map/ppermute | solution.py:249
  161.7 45.5 %collective-permute-start.8 = (bf16[2,128,384]{2,1,0:T(8,128)(2,1)}, bf16[2,128,384]{2,1,0:T(8,128)(2,1)S(1)}, u32[]{:S(2)}, u32[]{:S(2)}) collective-permute-start(bf16[2,128,384]{2,1,0:T(8,128)(2,1)} %get-tuple-element.34), channel_id=1, source_target_pairs={{2,0},{3,1},{4,2},{5,3},{6,4},{7,5},{8,6},{9,7},{10,8},{11,9},{12,... | collective-permute-start | bytes 589832 | tf_op jit(solution)/shard_map/ppermute | solution.py:249
  178.5 8.2 %copy-start.6 = (bf16[2,384,512]{2,1,0:T(8,128)(2,1)}, bf16[2,384,512]{2,1,0:T(8,128)(2,1)S(1)}, u32[]{:S(2)}) copy-start(bf16[2,384,512]{2,1,0:T(8,128)(2,1)S(1)} %collective-permute-done.10.refs_8_) | copy-start | bytes 2359300
  178.5 51.7 %collective-permute-start.24 = (bf16[384,384]{1,0:T(8,128)(2,1)}, bf16[384,384]{1,0:T(8,128)(2,1)S(1)}, u32[]{:S(2)}, u32[]{:S(2)}) collective-permute-start(bf16[384,384]{1,0:T(8,128)(2,1)} %get-tuple-element.50), channel_id=1, source_target_pairs={{0,16},{16,0},{1,17},{17,1},{2,18},{18,2},{3,19},{19,3},{4,20},{20... | collective-permute-start | bytes 884744 | tf_op jit(solution)/shard_map/ppermute | solution.py:256
  207.9 11.5 %copy-start.26 = (bf16[384,256]{1,0:T(8,128)(2,1)S(1)}, bf16[384,256]{1,0:T(8,128)(2,1)}, u32[]{:S(2)}) copy-start(bf16[384,256]{1,0:T(8,128)(2,1)} %get-tuple-element.52) | copy-start | bytes 589828
  207.9 12.7 %copy-start.25 = (bf16[384,256]{1,0:T(8,128)(2,1)S(1)}, bf16[384,256]{1,0:T(8,128)(2,1)}, u32[]{:S(2)}) copy-start(bf16[384,256]{1,0:T(8,128)(2,1)} %get-tuple-element.51) | copy-start | bytes 589828
  218.4 10.5 %collective-permute-start.27 = (bf16[384,256]{1,0:T(8,128)(2,1)}, bf16[384,256]{1,0:T(8,128)(2,1)S(1)}, u32[]{:S(2)}, u32[]{:S(2)}) collective-permute-start(bf16[384,256]{1,0:T(8,128)(2,1)} %get-tuple-element.53), channel_id=1, source_target_pairs={{0,16},{16,0},{1,17},{17,1},{2,18},{18,2},{3,19},{19,3},{4,20},{20... | collective-permute-start | bytes 589832 | tf_op jit(solution)/shard_map/ppermute | solution.py:256
  219.3 9.6 %collective-permute-start.26 = (bf16[384,256]{1,0:T(8,128)(2,1)S(1)}, bf16[384,256]{1,0:T(8,128)(2,1)S(1)}, u32[]{:S(2)}, u32[]{:S(2)}) collective-permute-start(bf16[384,256]{1,0:T(8,128)(2,1)S(1)} %copy-done.26), channel_id=1, source_target_pairs={{0,16},{16,0},{1,17},{17,1},{2,18},{18,2},{3,19},{19,3},{4,20},{20... | collective-permute-start | bytes 589832 | tf_op jit(solution)/shard_map/ppermute | solution.py:256
  220.5 9.6 %collective-permute-start.25 = (bf16[384,256]{1,0:T(8,128)(2,1)S(1)}, bf16[384,256]{1,0:T(8,128)(2,1)S(1)}, u32[]{:S(2)}, u32[]{:S(2)}) collective-permute-start(bf16[384,256]{1,0:T(8,128)(2,1)S(1)} %copy-done.25), channel_id=1, source_target_pairs={{0,16},{16,0},{1,17},{17,1},{2,18},{18,2},{3,19},{19,3},{4,20},{20... | collective-permute-start | bytes 589832 | tf_op jit(solution)/shard_map/ppermute | solution.py:256
  227.7 5.1 %collective-permute-start.23 = (bf16[384,128]{1,0:T(8,128)(2,1)}, bf16[384,128]{1,0:T(8,128)(2,1)S(1)}, u32[]{:S(2)}, u32[]{:S(2)}) collective-permute-start(bf16[384,128]{1,0:T(8,128)(2,1)} %get-tuple-element.49), channel_id=1, source_target_pairs={{0,16},{16,0},{1,17},{17,1},{2,18},{18,2},{3,19},{19,3},{4,20},{20... | collective-permute-start | bytes 294920 | tf_op jit(solution)/shard_map/ppermute | solution.py:256
  228.9 1.2 copy-start.17
  (7 other events, 5.6 us)
where the time goes:
time: 238 us; the launch traced here: 235 us
  waiting for transfers between devices  84.3 us (35%)
  starting transfers between devices  69.5 us (29%)
  Pallas kernels  64.1 us (27%)
  other arithmetic  12.6 us (5%)
  local copies, waits for them, and re-layouts  4.02 us (2%)
    pallas_call x5, Pallas kernels, attend(): pl.pallas_call(kernel, out_shape=[jax.ShapeDtypeStruct(queries.shape, que...  51.3 us
    ppermute x3, waiting for transfers between devices, on_device(): kv_rec.append(lax.ppermute(packed, 'head', swap))  44.3 us
    ppermute x15, starting transfers between devices, on_device(): far.append(lax.ppermute(tile, 'blk', pairs))  43 us
    ppermute x15, waiting for transfers between devices, on_device(): far.append(lax.ppermute(tile, 'blk', pairs))  38.7 us
    ppermute x5, starting transfers between devices, on_device(): returned.append((a, lax.ppermute(sent, 'head', swap)))  12.3 us
    pallas_call x3, Pallas kernels, select_distant(): pl.pallas_call(functools.partial(distant_kernel, half, low_col, width), o...  9.32 us
    ppermute x3, starting transfers between devices, on_device(): rim_b = lax.ppermute(kv_rec[c], ('head', 'blk'), outward(-1))  8.27 us
    another operation x5, other arithmetic, on_device(): jnp.stack([columns_of(array, 1 - side, low * HD, width) for array in (key...  6.69 us
  transfers between devices with their start and end apart: 28, of which 10 were waited for; matrix products, arithmetic and copies ran while one was open for 4% of the time, Pallas kernels for 27%

commit v1 on v0

--- a/solution.py
+++ b/solution.py
@@ -27,83 +27,130 @@
     return jnp.where(side == 0, first, second)
 
 
-def distant_kernel(half, low_col, width, meta, key, value, received, *rest):
-    outs, sems = rest[:-1], rest[-1]
-    first = pl.multiple_of(meta[0] * width_of(key) + low_col, HD)
-    copies = []
+def distant_kernel(half, low_col, meta, key, value, *rest):
+    count = meta.shape[0] - 1
+    received, outs, sems = rest[: -count - 1], rest[-count - 1 : -1], rest[-1]
+    side_col = meta[0] * (key.shape[1] // 2) + low_col
+    waits = []
     for i, out in enumerate(outs):
         slot = meta[1 + i]
         own = slot < half
         rows = pl.ds(pl.multiple_of(lax.rem(slot, half) * TILE, TILE), TILE)
-        cols = pl.ds(first, width)
-        for j, source in enumerate((key, value)):
-            sem = sems.at[i, j]
-            mine = pltpu.make_async_copy(source.at[rows, cols], out.at[j], sem)
-            theirs = pltpu.make_async_copy(received.at[j, rows, :], out.at[j], sem)
-            pl.when(own)(mine.start)
-            pl.when(jnp.logical_not(own))(theirs.start)
-            copies.append(theirs)
-    for copy in copies:
+        first = 0
+        for p, part in enumerate(received):
+            width = part.shape[2]
+            cols = pl.ds(pl.multiple_of(side_col + first, HD), width)
+            for j, source in enumerate((key, value)):
+                target, sem = out.at[j, :, first : first + width], sems.at[i, j, p]
+                mine = pltpu.make_async_copy(source.at[rows, cols], target, sem)
+                theirs = pltpu.make_async_copy(part.at[j, rows, :], target, sem)
+                pl.when(own)(mine.start)
+                pl.when(jnp.logical_not(own))(theirs.start)
+                waits.append(theirs)
+            first += width
+    for copy in waits:
         copy.wait()
 
 
-def width_of(ref):
-    return ref.shape[1] // 2
-
-
-def select_distant(meta, key, value, received, low_col, count, half):
-    width = received.shape[2]
-    shape = jax.ShapeDtypeStruct((2, TILE, width), key.dtype)
+def select_distant(meta, key, value, received, low_col, half):
+    count = meta.shape[0] - 1
+    width = sum(part.shape[2] for part in received)
+    shape = pltpu.VMEM((2, TILE, width), key.dtype)
     return pl.pallas_call(
-        functools.partial(distant_kernel, half, low_col, width),
+        functools.partial(distant_kernel, half, low_col),
         out_shape=[shape] * count,
         grid_spec=pltpu.PrefetchScalarGridSpec(
             num_scalar_prefetch=1,
             grid=(),
-            in_specs=[anywhere] * 3,
+            in_specs=[anywhere] * (2 + len(received)),
             out_specs=[pl.BlockSpec(memory_space=pltpu.VMEM)] * count,
-            scratch_shapes=[pltpu.SemaphoreType.DMA((count, 2))],
+            scratch_shapes=[pltpu.SemaphoreType.DMA((count, 2, len(received)))],
         ),
-    )(meta, key, value, received)
+    )(meta, key, value, *received)
 
 
 def attend_kernel(allowed, where, q_own, q_rec, k_own, v_own, kv_rec, rim_a, rim_b, *rest):
-    far, (o_own, o_send) = rest[:-2], rest[-2:]
-    tiles = q_own.shape[0] // TILE
-    keys = jnp.concatenate([k_own[...], kv_rec[0], rim_a[0], rim_b[0]] + [d[0] for d in far], 0)
-    values = jnp.concatenate([v_own[...], kv_rec[1], rim_a[1], rim_b[1]] + [d[1] for d in far], 0)
+    far, (o_own, o_send, keys, values, scores, tops) = rest[:-6], rest[-6:]
+    rows = q_own.shape[0]
+    tiles = rows // TILE
     slots = keys.shape[0] // TILE
-    for q_ref, o_ref, base in ((q_own, o_own, 0), (q_rec, o_send, tiles)):
-        scores = lax.dot_general(q_ref[...], keys, across, preferred_element_type=jnp.float32)
-        rounded, totals = [], []
-        for t in range(tiles):
-            rows = slice(t * TILE, (t + 1) * TILE)
-            cells = [
-                jnp.where(
-                    allowed[base + t, j] > 0,
-                    scores[rows, j * TILE : (j + 1) * TILE],
-                    masked_value,
-                )
-                for j in range(slots)
-            ]
-            largest = jnp.max(functools.reduce(jnp.maximum, cells), -1, keepdims=True)
-            weights = [jnp.exp2((cell - largest) * exp2_scale) for cell in cells]
-            totals.append(jnp.sum(functools.reduce(jnp.add, weights), -1, keepdims=True))
-            rounded.append(jnp.concatenate([w.astype(jnp.bfloat16) for w in weights], 1))
-        mixture = jnp.dot(
-            jnp.concatenate(rounded, 0), values, preferred_element_type=jnp.float32
-        )
-        o_ref[...] = (mixture / jnp.concatenate(totals, 0)).astype(o_ref.dtype)
-
-
-def attend(allowed, where, arrays, result, chunk_low, low, high, heads_here):
+
+    @pl.when(pl.program_id(0) == 0)
+    def fill_ones():
+        values[:, HD:] = jnp.ones((slots * TILE, HD), values.dtype)
+
+    first = 0
+    sources = [(k_own[...], v_own[...])]
+    sources += [(ref[0], ref[1]) for ref in (kv_rec, rim_a, rim_b, *far)]
+    for key_part, value_part in sources:
+        last = first + key_part.shape[0]
+        keys[first:last, :] = key_part
+        values[first:last, :HD] = value_part
+        first = last
+
+    pairs = [(j, min(j + 2, slots)) for j in range(0, slots, 2)]
+    blocks = [(q_own, o_own, t, t) for t in range(tiles)]
+    blocks += [(q_rec, o_send, t, tiles + t) for t in range(tiles)]
+    largest, mixed = {}, {}
+
+    def score(b, pair):
+        q_ref, _, t, row = blocks[b]
+        low, high = pair
+        cells = lax.dot_general(
+            q_ref[t * TILE : (t + 1) * TILE, :],
+            keys[low * TILE : high * TILE, :],
+            across,
+            preferred_element_type=jnp.float32,
+        )
+        for j in range(low, high):
+            cell = cells[:, (j - low) * TILE : (j - low + 1) * TILE]
+            cell = jnp.where(allowed[row, j] > 0, cell, masked_value)
+            scores[b % 2, :, j * TILE : (j + 1) * TILE] = cell
+            largest[b] = cell if b not in largest else jnp.maximum(largest[b], cell)
+
+    def settle(b):
+        top = jnp.max(largest[b], axis=-1, keepdims=True)
+        tops[b % 2] = jnp.broadcast_to(top, (TILE, TILE))
+
+    def mix(b, pair):
+        low, high = pair
+        rounded = [
+            jnp.exp2(
+                (scores[b % 2, :, j * TILE : (j + 1) * TILE] - tops[b % 2]) * exp2_scale
+            ).astype(values.dtype)
+            for j in range(low, high)
+        ]
+        part = jnp.dot(
+            jnp.concatenate(rounded, 1),
+            values[low * TILE : high * TILE, :],
+            preferred_element_type=jnp.float32,
+        )
+        mixed[b] = part if b not in mixed else mixed[b] + part
+
+    for pair in pairs:
+        score(0, pair)
+    settle(0)
+    for b, (_, o_ref, t, _) in enumerate(blocks):
+        for pair in pairs:
+            if b + 1 < len(blocks):
+                score(b + 1, pair)
+            mix(b, pair)
+        o_ref[t * TILE : (t + 1) * TILE, :] = (mixed[b][:, :HD] / mixed[b][:, HD:]).astype(
+            o_ref.dtype
+        )
+        if b + 1 < len(blocks):
+            settle(b + 1)
+
+
+def attend(allowed, where, arrays, result, chunk_low, far_low, low, high, heads_here):
     queries, q_rec, key, value, kv_rec, rim_a, rim_b, far = arrays
     rows = queries.shape[0]
+    slots = allowed.shape[1]
     own = pl.BlockSpec((rows, HD), lambda i, a, w: (0, w[0] * heads_here + low + i))
     flat = pl.BlockSpec((rows, HD), lambda i, a, w: (0, low + i))
     whole = pl.BlockSpec((2, rows, HD), lambda i, a, w: (0, 0, low + i))
     part = pl.BlockSpec((2, rows, HD), lambda i, a, w: (0, 0, low - chunk_low + i))
-    tile = pl.BlockSpec((2, TILE, HD), lambda i, a, w: (0, 0, low - chunk_low + i))
+    tile = pl.BlockSpec((2, TILE, HD), lambda i, a, w: (0, 0, low - far_low + i))
     out = pl.BlockSpec((rows, HD), lambda i, a, w: (0, i))
     shape = jax.ShapeDtypeStruct((rows, (high - low) * HD), queries.dtype)
     inputs = [queries, q_rec, key, value, kv_rec, rim_a, rim_b, *far]
@@ -122,6 +169,12 @@
             grid=(high - low,),
             in_specs=specs,
             out_specs=[own, out],
+            scratch_shapes=[
+                pltpu.VMEM((slots * TILE, HD), queries.dtype),
+                pltpu.VMEM((slots * TILE, 2 * HD), queries.dtype),
+                pltpu.VMEM((2, TILE, slots * TILE), jnp.float32),
+                pltpu.VMEM((2, TILE, TILE), jnp.float32),
+            ],
         ),
         input_output_aliases=aliases,
     )(allowed, where, *inputs)
@@ -155,7 +208,7 @@
         grid_spec=pltpu.PrefetchScalarGridSpec(
             num_scalar_prefetch=1,
             grid=(),
-            in_specs=[anywhere] * (len(pieces) + 1),
+            in_specs=[pl.BlockSpec(memory_space=pltpu.HBM)] * (len(pieces) + 1),
             out_specs=anywhere,
             scratch_shapes=[pltpu.VMEM(piece.shape, piece.dtype) for piece in pieces]
             + [pltpu.SemaphoreType.DMA((2, len(pieces)))],
@@ -235,24 +288,31 @@
             )
     q_rec = lax.ppermute(columns_of(queries, 1 - side, 0, group_width), "head", swap)
 
-    gathered = []
-    for c, (low, high) in enumerate(chunks):
-        rim_b = lax.ppermute(kv_rec[c], ("head", "blk"), outward(-1))
-        tiles = select_distant(meta, key_rows, value_rows, kv_rec[c], low * HD, len(shifts), half)
-        far = []
+    rim_b = []
+    for c in range(len(chunks)):
+        rim_b.append(lax.ppermute(kv_rec[c], ("head", "blk"), outward(-1)))
+    far = []
+    for members in far_groups:
+        low = chunks[members[0]][0]
+        tiles = select_distant(
+            meta, key_rows, value_rows, [kv_rec[c] for c in members], low * HD, half
+        )
+        arrived = []
         for (direction, distance), tile in zip(shifts, tiles):
             if direction == 0:
                 pairs = [(s, (s + distance) % slabs) for s in range(slabs)]
             else:
                 step = direction * distance
                 pairs = [(s, s + step) for s in range(slabs) if 0 <= s + step < slabs]
-            far.append(lax.ppermute(tile, "blk", pairs))
-        gathered.append((rim_b, far))
+            arrived.append(lax.ppermute(tile, "blk", pairs))
+        far += [(low, arrived)] * len(members)
     result, returned = None, []
     for c, a, b in head_runs(heads_here):
-        rim_b, far = gathered[c]
-        arrays = (queries, q_rec, key_rows, value_rows, kv_rec[c], rim_a, rim_b, far)
-        result, sent = attend(allowed, where, arrays, result, chunks[c][0], a, b, heads_here)
+        far_low, arrived = far[c]
+        arrays = (queries, q_rec, key_rows, value_rows, kv_rec[c], rim_a, rim_b[c], arrived)
+        result, sent = attend(
+            allowed, where, arrays, result, chunks[c][0], far_low, a, b, heads_here
+        )
         returned.append((a, lax.ppermute(sent, "head", swap)))
     result = place(
         where, [p for _, p in returned[:-1]], [a for a, _ in returned[:-1]], result, heads_here
@@ -261,17 +321,16 @@
     return result
 
 
+far_groups = ((0,), (1,), (2,))
+
+
 def chunk_bounds(heads):
     cuts = [0, heads * 3 // 10, heads * 7 // 10, heads]
     return list(zip(cuts[:-1], cuts[1:]))
 
 
 def head_runs(heads):
-    runs = []
-    for c, (low, high) in enumerate(chunk_bounds(heads)):
-        cuts = [low, high] if c == 0 else [low, low + (high - low + 1) // 2, high]
-        runs += [(c, a, b) for a, b in zip(cuts[:-1], cuts[1:])]
-    return runs
+    return [(c, low, high) for c, (low, high) in enumerate(chunk_bounds(heads))]
 
 
 def solution(mesh):

time: 238 us -> 217 us (0.912)
  Pallas kernels: 64.1 us -> 44.5 us
  starting transfers between devices: 69.5 us -> 66.8 us
    pallas_call x5 -> x3, Pallas kernels: 51.3 us -> 34.7 us  [attend(): pl.pallas_call(kernel, out_shape=[jax.ShapeDtypeStruct(queries.shape, que...]
    ppermute x5 -> x3, starting transfers between devices: 12.3 us -> 2.23 us  [on_device(): returned.append((a, lax.ppermute(sent, 'head', swap)))]
    ppermute x18, starting transfers between devices: 51.3 us -> 58.7 us  [the longest x15 43.2 us: on_device(): arrived.append(lax.ppermute(tile, 'blk', pairs))]
    ppermute x5 -> x3, waiting for transfers between devices: 1.19 us -> 7.06 us  [on_device(): returned.append((a, lax.ppermute(sent, 'head', swap)))]
    ppermute x18, waiting for transfers between devices: 38.7 us -> 32.9 us  [the longest x15 32.9 us: on_device(): arrived.append(lax.ppermute(tile, 'blk', pairs))]
    pallas_call x3, Pallas kernels: 9.32 us -> 6.22 us  [select_distant(): pl.pallas_call(functools.partial(distant_kernel, half, low_col), out_shap...]
  transfers between devices with their start and end apart: 28 -> 26, of which waited for: 10 -> 9; matrix products, arithmetic and copies ran while one was open for 4% -> 5% of each run, Pallas kernels for 27% -> 20%
where the time goes in v1:
time: 217 us; the launch traced here: 215 us
  waiting for transfers between devices  86.3 us (40%)
  starting transfers between devices  66.8 us (31%)
  Pallas kernels  44.5 us (21%)
  other arithmetic  11.6 us (5%)
  local copies, waits for them, and re-layouts  4.75 us (2%)
    ppermute x3, waiting for transfers between devices, on_device(): kv_rec.append(lax.ppermute(packed, 'head', swap))  46.4 us
    ppermute x15, starting transfers between devices, on_device(): arrived.append(lax.ppermute(tile, 'blk', pairs))  43.2 us
    pallas_call x3, Pallas kernels, attend(): pl.pallas_call(kernel, out_shape=[jax.ShapeDtypeStruct(queries.shape, que...  34.7 us
    ppermute x15, waiting for transfers between devices, on_device(): arrived.append(lax.ppermute(tile, 'blk', pairs))  32.9 us
    ppermute x3, starting transfers between devices, on_device(): rim_b.append(lax.ppermute(kv_rec[c], ('head', 'blk'), outward(-1)))  15.4 us
    ppermute x3, waiting for transfers between devices, on_device(): returned.append((a, lax.ppermute(sent, 'head', swap)))  7.06 us
    pallas_call x3, Pallas kernels, select_distant(): pl.pallas_call(functools.partial(distant_kernel, half, low_col), out_shap...  6.22 us
    another operation x5, other arithmetic, on_device(): jnp.stack([columns_of(array, 1 - side, low * HD, width) for array in (key...  5.8 us
  transfers between devices with their start and end apart: 26, of which 9 were waited for; matrix products, arithmetic and copies ran while one was open for 5% of the time, Pallas kernels for 20%

profile of v1, /device:TPU:12, one launch (start us, length us, event | category | flops | bytes accessed | tf_op | source)
XLA Modules:
  0.0 214.7 jit_solution(2805600264725034793)
XLA Ops:
  0.0 1.9 select_bitcast_fusion.4
  1.9 0.9 pad_maximum_fusion.3
  2.8 1.5 collective-permute-start.16
  4.3 1.7 select_bitcast_fusion
  6.0 1.4 pad_maximum_fusion
  7.4 1.9 collective-permute-start.2
  9.3 1.1 slice_select_fusion
  11.0 1.2 select_bitcast_fusion.2
  12.2 0.9 pad_maximum_fusion.1
  13.1 1.5 collective-permute-start.9
  14.6 0.9 pad_maximum_fusion.2
  17.6 1.6 collective-permute-done.16.rest_0_.kv_rec
  19.3 2.0 shard_map.57
  21.3 2.7 %collective-permute-start.18 = (bf16[2,128,384]{2,1,0:T(8,128)(2,1)S(1)}, bf16[2,128,384]{2,1,0:T(8,128)(2,1)S(1)}, u32[]{:S(2)}, u32[]{:S(2)}) collective-permute-start(bf16[2,128,384]{2,1,0:T(8,128)(2,1)S(1)} %get-tuple-element.36), channel_id=1, source_target_pairs={{0,8},{1,9},{2,10},{3,11},{4,12},{5,13},{6,14},{7,15},{8,0},{9,1},... | collective-permute-start | bytes 589832 | tf_op jit(solution)/shard_map/ppermute | solution.py:307
  24.0 44.7 %collective-permute-done.1.rest_0_.refs_6_ = bf16[2,384,384]{2,1,0:T(8,128)(2,1)} collective-permute-done((bf16[2,384,384]{2,1,0:T(8,128)(2,1)}, bf16[2,384,384]{2,1,0:T(8,128)(2,1)}, u32[]{:S(2)}, u32[]{:S(2)}) %collective-permute-start.1) | collective-permute-done | bytes 589856 | tf_op jit(solution)/shard_map/ppermute | solution.py:280
  68.7 3.5 %collective-permute-start.19 = (bf16[2,128,384]{2,1,0:T(8,128)(2,1)S(1)}, bf16[2,128,384]{2,1,0:T(8,128)(2,1)S(1)}, u32[]{:S(2)}, u32[]{:S(2)}) collective-permute-start(bf16[2,128,384]{2,1,0:T(8,128)(2,1)S(1)} %get-tuple-element.37), channel_id=1, source_target_pairs={{0,4},{1,5},{2,6},{3,7},{4,8},{5,9},{6,10},{7,11},{8,12},{9,13},{1... | collective-permute-start | bytes 589832 | tf_op jit(solution)/shard_map/ppermute | solution.py:307
  72.2 2.4 %collective-permute-start.20 = (bf16[2,128,384]{2,1,0:T(8,128)(2,1)S(1)}, bf16[2,128,384]{2,1,0:T(8,128)(2,1)S(1)}, u32[]{:S(2)}, u32[]{:S(2)}) collective-permute-start(bf16[2,128,384]{2,1,0:T(8,128)(2,1)S(1)} %get-tuple-element.38), channel_id=1, source_target_pairs={{4,0},{5,1},{6,2},{7,3},{8,4},{9,5},{10,6},{11,7},{12,8},{13,9},{1... | collective-permute-start | bytes 589832 | tf_op jit(solution)/shard_map/ppermute | solution.py:307
  74.6 1.8 collective-permute-done.19.rest_1_
  76.4 3.4 %collective-permute-start.21 = (bf16[2,128,384]{2,1,0:T(8,128)(2,1)S(1)}, bf16[2,128,384]{2,1,0:T(8,128)(2,1)S(1)}, u32[]{:S(2)}, u32[]{:S(2)}) collective-permute-start(bf16[2,128,384]{2,1,0:T(8,128)(2,1)S(1)} %get-tuple-element.39), channel_id=1, source_target_pairs={{0,2},{1,3},{2,4},{3,5},{4,6},{5,7},{6,8},{7,9},{8,10},{9,11},{10,... | collective-permute-start | bytes 589832 | tf_op jit(solution)/shard_map/ppermute | solution.py:307
  79.9 0.8 copy-done.3
  80.7 2.4 %collective-permute-start.22 = (bf16[2,128,384]{2,1,0:T(8,128)(2,1)S(1)}, bf16[2,128,384]{2,1,0:T(8,128)(2,1)}, u32[]{:S(2)}, u32[]{:S(2)}) collective-permute-start(bf16[2,128,384]{2,1,0:T(8,128)(2,1)S(1)} %get-tuple-element.40), channel_id=1, source_target_pairs={{2,0},{3,1},{4,2},{5,3},{6,4},{7,5},{8,6},{9,7},{10,8},{11,9},{12,... | collective-permute-start | bytes 589832 | tf_op jit(solution)/shard_map/ppermute | solution.py:307
  83.1 2.1 shard_map.56
  85.3 3.3 %collective-permute-start.11 = (bf16[2,128,512]{2,1,0:T(8,128)(2,1)S(1)}, bf16[2,128,512]{2,1,0:T(8,128)(2,1)}, u32[]{:S(2)}, u32[]{:S(2)}) collective-permute-start(bf16[2,128,512]{2,1,0:T(8,128)(2,1)S(1)} %get-tuple-element.31), channel_id=1, source_target_pairs={{0,8},{1,9},{2,10},{3,11},{4,12},{5,13},{6,14},{7,15},{8,0},{9,1},... | collective-permute-start | bytes 786440 | tf_op jit(solution)/shard_map/ppermute | solution.py:307
  89.3 1.9 collective-permute-start.12
  91.2 2.0 shard_map.55
  93.3 7.9 %collective-permute-done.22.rest_4_ = bf16[2,128,384]{2,1,0:T(8,128)(2,1)} collective-permute-done((bf16[2,128,384]{2,1,0:T(8,128)(2,1)S(1)}, bf16[2,128,384]{2,1,0:T(8,128)(2,1)}, u32[]{:S(2)}, u32[]{:S(2)}) %collective-permute-start.22) | collective-permute-done | bytes 196640 | tf_op jit(solution)/shard_map/ppermute | solution.py:307
  101.2 9.6 %collective-permute-done.4.refs_9_ = bf16[2,128,384]{2,1,0:T(8,128)(2,1)S(1)} collective-permute-done((bf16[2,128,384]{2,1,0:T(8,128)(2,1)S(1)}, bf16[2,128,384]{2,1,0:T(8,128)(2,1)S(1)}, u32[]{:S(2)}, u32[]{:S(2)}) %collective-permute-start.4) | collective-permute-done | bytes 196640 | tf_op jit(solution)/shard_map/ppermute | solution.py:307
  110.8 1.9 collective-permute-start.13
  112.8 1.9 collective-permute-start.17
  114.7 4.7 %collective-permute-start.14 = (bf16[2,128,512]{2,1,0:T(8,128)(2,1)S(1)}, bf16[2,128,512]{2,1,0:T(8,128)(2,1)}, u32[]{:S(2)}, u32[]{:S(2)}) collective-permute-start(bf16[2,128,512]{2,1,0:T(8,128)(2,1)S(1)} %get-tuple-element.34), channel_id=1, source_target_pairs={{0,2},{1,3},{2,4},{3,5},{4,6},{5,7},{6,8},{7,9},{8,10},{9,11},{10,... | collective-permute-start | bytes 786440 | tf_op jit(solution)/shard_map/ppermute | solution.py:307
  119.5 2.4 %collective-permute-start.10 = (bf16[2,384,512]{2,1,0:T(8,128)(2,1)}, bf16[2,384,512]{2,1,0:T(8,128)(2,1)S(1)}, u32[]{:S(2)}, u32[]{:S(2)}) collective-permute-start(bf16[2,384,512]{2,1,0:T(8,128)(2,1)} %copy-done.3), channel_id=1, source_target_pairs={{0,1},{1,2},{2,3},{3,4},{4,5},{5,6},{6,7},{7,8},{8,9},{9,10},{10,1... | collective-permute-start | bytes 2359304 | tf_op jit(solution)/shard_map/ppermute | solution.py:293
  121.9 3.3 %collective-permute-start.15 = (bf16[2,128,512]{2,1,0:T(8,128)(2,1)S(1)}, bf16[2,128,512]{2,1,0:T(8,128)(2,1)S(1)}, u32[]{:S(2)}, u32[]{:S(2)}) collective-permute-start(bf16[2,128,512]{2,1,0:T(8,128)(2,1)S(1)} %get-tuple-element.35), channel_id=1, source_target_pairs={{2,0},{3,1},{4,2},{5,3},{6,4},{7,5},{8,6},{9,7},{10,8},{11,9},{12,... | collective-permute-start | bytes 786440 | tf_op jit(solution)/shard_map/ppermute | solution.py:307
  125.3 0.9 collective-permute-done.14.refs_12_
  126.1 11.1 %collective-permute-start.3 = (bf16[2,384,384]{2,1,0:T(8,128)(2,1)}, bf16[2,384,384]{2,1,0:T(8,128)(2,1)}, u32[]{:S(2)}, u32[]{:S(2)}) collective-permute-start(bf16[2,384,384]{2,1,0:T(8,128)(2,1)} %collective-permute-done.1.rest_0_.refs_6_), channel_id=1, source_target_pairs={{0,1},{1,2},{2,3},{3,4},{4,5},{5,6},{6,7},{7,8},{8,9},{9,10},{10,1... | collective-permute-start | bytes 1769480 | tf_op jit(solution)/shard_map/ppermute | solution.py:293
  137.3 12.6 %collective-permute-done.15.refs_13_ = bf16[2,128,512]{2,1,0:T(8,128)(2,1)S(1)} collective-permute-done((bf16[2,128,512]{2,1,0:T(8,128)(2,1)S(1)}, bf16[2,128,512]{2,1,0:T(8,128)(2,1)S(1)}, u32[]{:S(2)}, u32[]{:S(2)}) %collective-permute-start.15) | collective-permute-done | bytes 262176 | tf_op jit(solution)/shard_map/ppermute | solution.py:307
  150.0 3.9 %collective-permute-start.5 = (bf16[2,128,384]{2,1,0:T(8,128)(2,1)S(1)}, bf16[2,128,384]{2,1,0:T(8,128)(2,1)S(1)}, u32[]{:S(2)}, u32[]{:S(2)}) collective-permute-start(bf16[2,128,384]{2,1,0:T(8,128)(2,1)S(1)} %get-tuple-element.27), channel_id=1, source_target_pairs={{0,4},{1,5},{2,6},{3,7},{4,8},{5,9},{6,10},{7,11},{8,12},{9,13},{1... | collective-permute-start | bytes 589832 | tf_op jit(solution)/shard_map/ppermute | solution.py:307
  154.0 1.9 collective-permute-start.6
  156.0 5.8 %collective-permute-start.7 = (bf16[2,128,384]{2,1,0:T(8,128)(2,1)S(1)}, bf16[2,128,384]{2,1,0:T(8,128)(2,1)S(1)}, u32[]{:S(2)}, u32[]{:S(2)}) collective-permute-start(bf16[2,128,384]{2,1,0:T(8,128)(2,1)S(1)} %get-tuple-element.29), channel_id=1, source_target_pairs={{0,2},{1,3},{2,4},{3,5},{4,6},{5,7},{6,8},{7,9},{8,10},{9,11},{10,... | collective-permute-start | bytes 589832 | tf_op jit(solution)/shard_map/ppermute | solution.py:307
  161.8 2.1 collective-permute-start.8
  164.6 10.6 %shard_map.58 = (bf16[384,2560]{1,0:T(8,128)(2,1)}, bf16[384,384]{1,0:T(8,128)(2,1)}) custom-call(s32[6,17]{1,0:T(8,128)} %convert_element_type.3.allowed.refs_0_, s32[1]{0:T(128)} %bitcast.where.refs_1_, bf16[384,2560]{1,0:T(8,128)(2,1)} %refs_2_.3, bf16[384,1280]{1,0:T(8,128)(2,1)} %copy-done.2, bf16[384,2560]{1,0:T(8,128)(2,1)} %refs_4_.3, ...), custom_call_target="tpu_custom_call" | custom-call | tf_op jit(solution)/shard_map/pallas_call | solution.py:164
  175.3 13.5 %shard_map.59 = (bf16[384,2560]{1,0:T(8,128)(2,1)}, bf16[384,512]{1,0:T(8,128)(2,1)}) custom-call(s32[6,17]{1,0:T(8,128)} %convert_element_type.3.allowed.refs_0_, s32[1]{0:T(128)} %bitcast.where.refs_1_, bf16[384,2560]{1,0:T(8,128)(2,1)} %refs_2_.3, bf16[384,1280]{1,0:T(8,128)(2,1)} %copy-done.2, ...), custom_call_target="tpu_custom_call", output_to_operand_aliasing={{0}: (14, {})} | custom-call | tf_op jit(solution)/shard_map/pallas_call | solution.py:164
  188.9 2.1 collective-permute-start.24
  191.6 10.7 %shard_map.60 = (bf16[384,2560]{1,0:T(8,128)(2,1)}, bf16[384,384]{1,0:T(8,128)(2,1)}) custom-call(s32[6,17]{1,0:T(8,128)} %convert_element_type.3.allowed.refs_0_, s32[1]{0:T(128)} %bitcast.where.refs_1_, bf16[384,2560]{1,0:T(8,128)(2,1)} %refs_2_.3, bf16[384,1280]{1,0:T(8,128)(2,1)} %copy-done.2, ...), custom_call_target="tpu_custom_call", output_to_operand_aliasing={{0}: (14, {})} | custom-call | tf_op jit(solution)/shard_map/pallas_call | solution.py:164
  202.4 5.0 %collective-permute-done.24.refs_0_ = bf16[384,384]{1,0:T(8,128)(2,1)S(1)} collective-permute-done((bf16[384,384]{1,0:T(8,128)(2,1)S(1)}, bf16[384,384]{1,0:T(8,128)(2,1)S(1)}, u32[]{:S(2)}, u32[]{:S(2)}) %collective-permute-start.24) | collective-permute-done | bytes 294944 | tf_op jit(solution)/shard_map/ppermute | solution.py:316
  208.2 1.9 shard_map.61.refs_1_
  210.1 2.1 collective-permute-done.23.refs_0_
  212.1 0.7 copy-done.7
  212.8 1.7 shard_map.62
  (75 shorter events, 6.1 us)
Async XLA Ops:
  0.0 4.3 %copy-start = (bf16[384,2560]{1,0:T(8,128)(2,1)S(1)}, bf16[384,2560]{1,0:T(8,128)(2,1)}, u32[]{:S(2)}) copy-start(bf16[384,2560]{1,0:T(8,128)(2,1)} %refs_4_.3) | copy-start | bytes 5898244
  2.8 16.5 %collective-permute-start.16 = (bf16[2,384,384]{2,1,0:T(8,128)(2,1)}, bf16[2,384,384]{2,1,0:T(8,128)(2,1)}, u32[]{:S(2)}, u32[]{:S(2)}) collective-permute-start(bf16[2,384,384]{2,1,0:T(8,128)(2,1)} %pad_maximum_fusion.3), channel_id=1, source_target_pairs={{0,16},{16,0},{1,17},{17,1},{2,18},{18,2},{3,19},{19,3},{4,20},{20... | collective-permute-start | bytes 1769480 | tf_op jit(solution)/shard_map/ppermute | solution.py:280
  6.0 3.4 %copy-start.1 = (bf16[384,2560]{1,0:T(8,128)(2,1)S(1)}, bf16[384,2560]{1,0:T(8,128)(2,1)}, u32[]{:S(2)}) copy-start(bf16[384,2560]{1,0:T(8,128)(2,1)} %refs_2_.3) | copy-start | bytes 5898244
  7.4 154.4 %collective-permute-start.2 = (bf16[2,384,1280]{2,1,0:T(8,128)(2,1)}, bf16[2,384,1280]{2,1,0:T(8,128)(2,1)}, u32[]{:S(2)}, u32[]{:S(2)}) collective-permute-start(bf16[2,384,1280]{2,1,0:T(8,128)(2,1)} %pad_maximum_fusion), channel_id=1, source_target_pairs={{1,0},{2,1},{3,2},{4,3},{5,4},{6,5},{7,6},{8,7},{9,8},{10,9},{11,1... | collective-permute-start | bytes 5898248 | tf_op jit(solution)/shard_map/ppermute | solution.py:282
  10.4 102.3 %collective-permute-start = (bf16[384,1280]{1,0:T(8,128)(2,1)}, bf16[384,1280]{1,0:T(8,128)(2,1)S(1)}, u32[]{:S(2)}, u32[]{:S(2)}) collective-permute-start(bf16[384,1280]{1,0:T(8,128)(2,1)} %slice_select_fusion), channel_id=1, source_target_pairs={{0,16},{16,0},{1,17},{17,1},{2,18},{18,2},{3,19},{19,3},{4,20},{20... | collective-permute-start | bytes 2949128 | tf_op jit(solution)/shard_map/ppermute | solution.py:289
  12.2 3.9 %copy-start.17 = (s32[96,16]{0,1:T(8,128)S(1)}, s32[96,16]{0,1:T(8,128)}, u32[]{:S(2)}) copy-start(s32[96,16]{0,1:T(8,128)} %param.8) | copy-start | bytes 18436
  12.2 3.9 %copy-start.18 = (s32[96]{0:T(128)S(1)}, s32[96]{0:T(128)}, u32[]{:S(2)}) copy-start(s32[96]{0:T(128)} %param.9) | copy-start | bytes 1156
  13.1 66.7 %collective-permute-start.9 = (bf16[2,384,512]{2,1,0:T(8,128)(2,1)}, bf16[2,384,512]{2,1,0:T(8,128)(2,1)S(1)}, u32[]{:S(2)}, u32[]{:S(2)}) collective-permute-start(bf16[2,384,512]{2,1,0:T(8,128)(2,1)} %pad_maximum_fusion.1), channel_id=1, source_target_pairs={{0,16},{16,0},{1,17},{17,1},{2,18},{18,2},{3,19},{19,3},{4,20},{20... | collective-permute-start | bytes 2359304 | tf_op jit(solution)/shard_map/ppermute | solution.py:280
  15.5 53.2 %collective-permute-start.1 = (bf16[2,384,384]{2,1,0:T(8,128)(2,1)}, bf16[2,384,384]{2,1,0:T(8,128)(2,1)}, u32[]{:S(2)}, u32[]{:S(2)}) collective-permute-start(bf16[2,384,384]{2,1,0:T(8,128)(2,1)} %pad_maximum_fusion.2), channel_id=1, source_target_pairs={{0,16},{16,0},{1,17},{17,1},{2,18},{18,2},{3,19},{19,3},{4,20},{20... | collective-permute-start | bytes 1769480 | tf_op jit(solution)/shard_map/ppermute | solution.py:280
  21.3 50.9 %collective-permute-start.18 = (bf16[2,128,384]{2,1,0:T(8,128)(2,1)S(1)}, bf16[2,128,384]{2,1,0:T(8,128)(2,1)S(1)}, u32[]{:S(2)}, u32[]{:S(2)}) collective-permute-start(bf16[2,128,384]{2,1,0:T(8,128)(2,1)S(1)} %get-tuple-element.36), channel_id=1, source_target_pairs={{0,8},{1,9},{2,10},{3,11},{4,12},{5,13},{6,14},{7,15},{8,0},{9,1},... | collective-permute-start | bytes 589832 | tf_op jit(solution)/shard_map/ppermute | solution.py:307
  68.7 7.7 %collective-permute-start.19 = (bf16[2,128,384]{2,1,0:T(8,128)(2,1)S(1)}, bf16[2,128,384]{2,1,0:T(8,128)(2,1)S(1)}, u32[]{:S(2)}, u32[]{:S(2)}) collective-permute-start(bf16[2,128,384]{2,1,0:T(8,128)(2,1)S(1)} %get-tuple-element.37), channel_id=1, source_target_pairs={{0,4},{1,5},{2,6},{3,7},{4,8},{5,9},{6,10},{7,11},{8,12},{9,13},{1... | collective-permute-start | bytes 589832 | tf_op jit(solution)/shard_map/ppermute | solution.py:307
  72.2 7.6 %copy-start.9 = (bf16[2,128,384]{2,1,0:T(8,128)(2,1)}, bf16[2,128,384]{2,1,0:T(8,128)(2,1)S(1)}, u32[]{:S(2)}) copy-start(bf16[2,128,384]{2,1,0:T(8,128)(2,1)S(1)} %collective-permute-done.18.rest_0_) | copy-start | bytes 589828
  72.2 13.0 %collective-permute-start.20 = (bf16[2,128,384]{2,1,0:T(8,128)(2,1)S(1)}, bf16[2,128,384]{2,1,0:T(8,128)(2,1)S(1)}, u32[]{:S(2)}, u32[]{:S(2)}) collective-permute-start(bf16[2,128,384]{2,1,0:T(8,128)(2,1)S(1)} %get-tuple-element.38), channel_id=1, source_target_pairs={{4,0},{5,1},{6,2},{7,3},{8,4},{9,5},{10,6},{11,7},{12,8},{13,9},{1... | collective-permute-start | bytes 589832 | tf_op jit(solution)/shard_map/ppermute | solution.py:307
  76.4 3.5 %copy-start.10 = (bf16[2,128,384]{2,1,0:T(8,128)(2,1)}, bf16[2,128,384]{2,1,0:T(8,128)(2,1)S(1)}, u32[]{:S(2)}) copy-start(bf16[2,128,384]{2,1,0:T(8,128)(2,1)S(1)} %collective-permute-done.19.rest_1_) | copy-start | bytes 589828
  76.4 12.2 %collective-permute-start.21 = (bf16[2,128,384]{2,1,0:T(8,128)(2,1)S(1)}, bf16[2,128,384]{2,1,0:T(8,128)(2,1)S(1)}, u32[]{:S(2)}, u32[]{:S(2)}) collective-permute-start(bf16[2,128,384]{2,1,0:T(8,128)(2,1)S(1)} %get-tuple-element.39), channel_id=1, source_target_pairs={{0,2},{1,3},{2,4},{3,5},{4,6},{5,7},{6,8},{7,9},{8,10},{9,11},{10,... | collective-permute-start | bytes 589832 | tf_op jit(solution)/shard_map/ppermute | solution.py:307
  79.8 0.9 copy-start.3
  80.7 20.5 %collective-permute-start.22 = (bf16[2,128,384]{2,1,0:T(8,128)(2,1)S(1)}, bf16[2,128,384]{2,1,0:T(8,128)(2,1)}, u32[]{:S(2)}, u32[]{:S(2)}) collective-permute-start(bf16[2,128,384]{2,1,0:T(8,128)(2,1)S(1)} %get-tuple-element.40), channel_id=1, source_target_pairs={{2,0},{3,1},{4,2},{5,3},{6,4},{7,5},{8,6},{9,7},{10,8},{11,9},{12,... | collective-permute-start | bytes 589832 | tf_op jit(solution)/shard_map/ppermute | solution.py:307
  85.3 3.3 %copy-start.11 = (bf16[2,128,384]{2,1,0:T(8,128)(2,1)}, bf16[2,128,384]{2,1,0:T(8,128)(2,1)S(1)}, u32[]{:S(2)}) copy-start(bf16[2,128,384]{2,1,0:T(8,128)(2,1)S(1)} %collective-permute-done.20.rest_2_) | copy-start | bytes 589828
  85.3 29.4 %collective-permute-start.11 = (bf16[2,128,512]{2,1,0:T(8,128)(2,1)S(1)}, bf16[2,128,512]{2,1,0:T(8,128)(2,1)}, u32[]{:S(2)}, u32[]{:S(2)}) collective-permute-start(bf16[2,128,512]{2,1,0:T(8,128)(2,1)S(1)} %get-tuple-element.31), channel_id=1, source_target_pairs={{0,8},{1,9},{2,10},{3,11},{4,12},{5,13},{6,14},{7,15},{8,0},{9,1},... | collective-permute-start | bytes 786440 | tf_op jit(solution)/shard_map/ppermute | solution.py:307
  88.6 0.7 copy-start.13
  89.3 30.2 %collective-permute-start.12 = (bf16[2,128,512]{2,1,0:T(8,128)(2,1)S(1)}, bf16[2,128,512]{2,1,0:T(8,128)(2,1)}, u32[]{:S(2)}, u32[]{:S(2)}) collective-permute-start(bf16[2,128,512]{2,1,0:T(8,128)(2,1)S(1)} %get-tuple-element.32), channel_id=1, source_target_pairs={{0,4},{1,5},{2,6},{3,7},{4,8},{5,9},{6,10},{7,11},{8,12},{9,13},{1... | collective-permute-start | bytes 786440 | tf_op jit(solution)/shard_map/ppermute | solution.py:307
  101.2 9.6 %collective-permute-start.4 = (bf16[2,128,384]{2,1,0:T(8,128)(2,1)S(1)}, bf16[2,128,384]{2,1,0:T(8,128)(2,1)S(1)}, u32[]{:S(2)}, u32[]{:S(2)}) collective-permute-start(bf16[2,128,384]{2,1,0:T(8,128)(2,1)S(1)} %get-tuple-element.26), channel_id=1, source_target_pairs={{0,8},{1,9},{2,10},{3,11},{4,12},{5,13},{6,14},{7,15},{8,0},{9,1},... | collective-permute-start | bytes 589832 | tf_op jit(solution)/shard_map/ppermute | solution.py:307
  110.8 8.6 %copy-start.12 = (bf16[2,128,384]{2,1,0:T(8,128)(2,1)}, bf16[2,128,384]{2,1,0:T(8,128)(2,1)S(1)}, u32[]{:S(2)}) copy-start(bf16[2,128,384]{2,1,0:T(8,128)(2,1)S(1)} %collective-permute-done.4.refs_9_) | copy-start | bytes 589828
  110.8 11.1 %collective-permute-start.13 = (bf16[2,128,512]{2,1,0:T(8,128)(2,1)S(1)}, bf16[2,128,512]{2,1,0:T(8,128)(2,1)}, u32[]{:S(2)}, u32[]{:S(2)}) collective-permute-start(bf16[2,128,512]{2,1,0:T(8,128)(2,1)S(1)} %get-tuple-element.33), channel_id=1, source_target_pairs={{4,0},{5,1},{6,2},{7,3},{8,4},{9,5},{10,6},{11,7},{12,8},{13,9},{1... | collective-permute-start | bytes 786440 | tf_op jit(solution)/shard_map/ppermute | solution.py:307
  112.8 51.9 %copy-start.2 = (bf16[384,1280]{1,0:T(8,128)(2,1)}, bf16[384,1280]{1,0:T(8,128)(2,1)S(1)}, u32[]{:S(2)}) copy-start(bf16[384,1280]{1,0:T(8,128)(2,1)S(1)} %collective-permute-done.q_rec.refs_3_) | copy-start | bytes 2949124
  112.8 41.3 %collective-permute-start.17 = (bf16[2,384,384]{2,1,0:T(8,128)(2,1)}, bf16[2,384,384]{2,1,0:T(8,128)(2,1)}, u32[]{:S(2)}, u32[]{:S(2)}) collective-permute-start(bf16[2,384,384]{2,1,0:T(8,128)(2,1)} %collective-permute-done.16.rest_0_.kv_rec), channel_id=1, source_target_pairs={{0,1},{1,2},{2,3},{3,4},{4,5},{5,6},{6,7},{7,8},{8,9},{9,10},{10,1... | collective-permute-start | bytes 1769480 | tf_op jit(solution)/shard_map/ppermute | solution.py:293
  114.7 11.4 %collective-permute-start.14 = (bf16[2,128,512]{2,1,0:T(8,128)(2,1)S(1)}, bf16[2,128,512]{2,1,0:T(8,128)(2,1)}, u32[]{:S(2)}, u32[]{:S(2)}) collective-permute-start(bf16[2,128,512]{2,1,0:T(8,128)(2,1)S(1)} %get-tuple-element.34), channel_id=1, source_target_pairs={{0,2},{1,3},{2,4},{3,5},{4,6},{5,7},{6,8},{7,9},{8,10},{9,11},{10,... | collective-permute-start | bytes 786440 | tf_op jit(solution)/shard_map/ppermute | solution.py:307
  119.5 36.5 %collective-permute-start.10 = (bf16[2,384,512]{2,1,0:T(8,128)(2,1)}, bf16[2,384,512]{2,1,0:T(8,128)(2,1)S(1)}, u32[]{:S(2)}, u32[]{:S(2)}) collective-permute-start(bf16[2,384,512]{2,1,0:T(8,128)(2,1)} %copy-done.3), channel_id=1, source_target_pairs={{0,1},{1,2},{2,3},{3,4},{4,5},{5,6},{6,7},{7,8},{8,9},{9,10},{10,1... | collective-permute-start | bytes 2359304 | tf_op jit(solution)/shard_map/ppermute | solution.py:293
  121.9 28.1 %collective-permute-start.15 = (bf16[2,128,512]{2,1,0:T(8,128)(2,1)S(1)}, bf16[2,128,512]{2,1,0:T(8,128)(2,1)S(1)}, u32[]{:S(2)}, u32[]{:S(2)}) collective-permute-start(bf16[2,128,512]{2,1,0:T(8,128)(2,1)S(1)} %get-tuple-element.35), channel_id=1, source_target_pairs={{2,0},{3,1},{4,2},{5,3},{6,4},{7,5},{8,6},{9,7},{10,8},{11,9},{12,... | collective-permute-start | bytes 786440 | tf_op jit(solution)/shard_map/ppermute | solution.py:307
  126.1 64.8 %collective-permute-start.3 = (bf16[2,384,384]{2,1,0:T(8,128)(2,1)}, bf16[2,384,384]{2,1,0:T(8,128)(2,1)}, u32[]{:S(2)}, u32[]{:S(2)}) collective-permute-start(bf16[2,384,384]{2,1,0:T(8,128)(2,1)} %collective-permute-done.1.rest_0_.refs_6_), channel_id=1, source_target_pairs={{0,1},{1,2},{2,3},{3,4},{4,5},{5,6},{6,7},{7,8},{8,9},{9,10},{10,1... | collective-permute-start | bytes 1769480 | tf_op jit(solution)/shard_map/ppermute | solution.py:293
  150.0 25.3 %copy-start.8 = (bf16[2,128,512]{2,1,0:T(8,128)(2,1)}, bf16[2,128,512]{2,1,0:T(8,128)(2,1)S(1)}, u32[]{:S(2)}) copy-start(bf16[2,128,512]{2,1,0:T(8,128)(2,1)S(1)} %collective-permute-done.15.refs_13_) | copy-start | bytes 786436
  150.0 38.8 %collective-permute-start.5 = (bf16[2,128,384]{2,1,0:T(8,128)(2,1)S(1)}, bf16[2,128,384]{2,1,0:T(8,128)(2,1)S(1)}, u32[]{:S(2)}, u32[]{:S(2)}) collective-permute-start(bf16[2,128,384]{2,1,0:T(8,128)(2,1)S(1)} %get-tuple-element.27), channel_id=1, source_target_pairs={{0,4},{1,5},{2,6},{3,7},{4,8},{5,9},{6,10},{7,11},{8,12},{9,13},{1... | collective-permute-start | bytes 589832 | tf_op jit(solution)/shard_map/ppermute | solution.py:307
  154.0 34.8 %collective-permute-start.6 = (bf16[2,128,384]{2,1,0:T(8,128)(2,1)S(1)}, bf16[2,128,384]{2,1,0:T(8,128)(2,1)S(1)}, u32[]{:S(2)}, u32[]{:S(2)}) collective-permute-start(bf16[2,128,384]{2,1,0:T(8,128)(2,1)S(1)} %get-tuple-element.28), channel_id=1, source_target_pairs={{4,0},{5,1},{6,2},{7,3},{8,4},{9,5},{10,6},{11,7},{12,8},{13,9},{1... | collective-permute-start | bytes 589832 | tf_op jit(solution)/shard_map/ppermute | solution.py:307
  156.0 19.3 %copy-start.4 = (bf16[2,384,512]{2,1,0:T(8,128)(2,1)}, bf16[2,384,512]{2,1,0:T(8,128)(2,1)S(1)}, u32[]{:S(2)}) copy-start(bf16[2,384,512]{2,1,0:T(8,128)(2,1)S(1)} %collective-permute-done.10.refs_8_) | copy-start | bytes 2359300
  156.0 34.9 %collective-permute-start.7 = (bf16[2,128,384]{2,1,0:T(8,128)(2,1)S(1)}, bf16[2,128,384]{2,1,0:T(8,128)(2,1)S(1)}, u32[]{:S(2)}, u32[]{:S(2)}) collective-permute-start(bf16[2,128,384]{2,1,0:T(8,128)(2,1)S(1)} %get-tuple-element.29), channel_id=1, source_target_pairs={{0,2},{1,3},{2,4},{3,5},{4,6},{5,7},{6,8},{7,9},{8,10},{9,11},{10,... | collective-permute-start | bytes 589832 | tf_op jit(solution)/shard_map/ppermute | solution.py:307
  161.8 29.1 %collective-permute-start.8 = (bf16[2,128,384]{2,1,0:T(8,128)(2,1)S(1)}, bf16[2,128,384]{2,1,0:T(8,128)(2,1)}, u32[]{:S(2)}, u32[]{:S(2)}) collective-permute-start(bf16[2,128,384]{2,1,0:T(8,128)(2,1)S(1)} %get-tuple-element.30), channel_id=1, source_target_pairs={{2,0},{3,1},{4,2},{5,3},{6,4},{7,5},{8,6},{9,7},{10,8},{11,9},{12,... | collective-permute-start | bytes 589832 | tf_op jit(solution)/shard_map/ppermute | solution.py:307
  175.3 13.6 %copy-start.19 = (bf16[384,384]{1,0:T(8,128)(2,1)S(1)}, bf16[384,384]{1,0:T(8,128)(2,1)}, u32[]{:S(2)}) copy-start(bf16[384,384]{1,0:T(8,128)(2,1)} %get-tuple-element.44) | copy-start | bytes 884740
  188.7 2.2 %copy-start.14 = (bf16[2,128,384]{2,1,0:T(8,128)(2,1)}, bf16[2,128,384]{2,1,0:T(8,128)(2,1)S(1)}, u32[]{:S(2)}) copy-start(bf16[2,128,384]{2,1,0:T(8,128)(2,1)S(1)} %collective-permute-done.5.refs_10_) | copy-start | bytes 589828
  188.8 18.6 %collective-permute-start.25 = (bf16[384,512]{1,0:T(8,128)(2,1)}, bf16[384,512]{1,0:T(8,128)(2,1)S(1)}, u32[]{:S(2)}, u32[]{:S(2)}) collective-permute-start(bf16[384,512]{1,0:T(8,128)(2,1)} %get-tuple-element.45), channel_id=1, source_target_pairs={{0,16},{16,0},{1,17},{17,1},{2,18},{18,2},{3,19},{19,3},{4,20},{20... | collective-permute-start | bytes 1179656 | tf_op jit(solution)/shard_map/ppermute | solution.py:316
  188.8 2.1 copy-start.15
  188.9 18.5 %collective-permute-start.24 = (bf16[384,384]{1,0:T(8,128)(2,1)S(1)}, bf16[384,384]{1,0:T(8,128)(2,1)S(1)}, u32[]{:S(2)}, u32[]{:S(2)}) collective-permute-start(bf16[384,384]{1,0:T(8,128)(2,1)S(1)} %copy-done.19), channel_id=1, source_target_pairs={{0,16},{16,0},{1,17},{17,1},{2,18},{18,2},{3,19},{19,3},{4,20},{20... | collective-permute-start | bytes 884744 | tf_op jit(solution)/shard_map/ppermute | solution.py:316
  190.9 0.7 copy-start.16
  202.3 9.9 %collective-permute-start.23 = (bf16[384,384]{1,0:T(8,128)(2,1)}, bf16[384,384]{1,0:T(8,128)(2,1)S(1)}, u32[]{:S(2)}, u32[]{:S(2)}) collective-permute-start(bf16[384,384]{1,0:T(8,128)(2,1)} %get-tuple-element.43), channel_id=1, source_target_pairs={{0,16},{16,0},{1,17},{17,1},{2,18},{18,2},{3,19},{19,3},{4,20},{20... | collective-permute-start | bytes 884744 | tf_op jit(solution)/shard_map/ppermute | solution.py:316
  207.3 0.7 copy-start.6
  207.3 0.8 copy-start.5
  212.1 0.7 copy-start.7

commit v2 on v1

--- a/solution.py
+++ b/solution.py
@@ -27,19 +27,49 @@
     return jnp.where(side == 0, first, second)
 
 
-def distant_kernel(half, low_col, meta, key, value, *rest):
-    count = meta.shape[0] - 1
-    received, outs, sems = rest[: -count - 1], rest[-count - 1 : -1], rest[-1]
-    side_col = meta[0] * (key.shape[1] // 2) + low_col
+def pack_kernel(low, flip, where, key, value, out, sems):
+    side = 1 - where[0] if flip else where[0]
+    first = pl.multiple_of(side * (key.shape[1] // 2) + low, HD)
+    copies = [
+        pltpu.make_async_copy(source.at[:, pl.ds(first, out.shape[2])], out.at[i], sems.at[i])
+        for i, source in enumerate((key, value))
+    ]
+    for copy in copies:
+        copy.start()
+    for copy in copies:
+        copy.wait()
+
+
+def pack(where, key, value, low, width, flip):
+    return pl.pallas_call(
+        functools.partial(pack_kernel, low, flip),
+        out_shape=pltpu.VMEM((2, key.shape[0], width), key.dtype),
+        grid_spec=pltpu.PrefetchScalarGridSpec(
+            num_scalar_prefetch=1,
+            grid=(),
+            in_specs=[anywhere] * 2,
+            out_specs=pl.BlockSpec(memory_space=pltpu.VMEM),
+            scratch_shapes=[pltpu.SemaphoreType.DMA((2,))],
+        ),
+    )(where, key, value)
+
+
+def distant_kernel(half, jobs, lows, chosen, where, here, key, value, *rest):
+    received, outs, sems = rest[: len(lows)], rest[len(lows) : -1], rest[-1]
+    slabs = chosen.shape[0]
+    side_col = where[0] * (key.shape[1] // 2)
     waits = []
-    for i, out in enumerate(outs):
-        slot = meta[1 + i]
+    for i, ((step, members), out) in enumerate(zip(jobs, outs)):
+        reader = here[0] + step
+        reader = jnp.where(reader < 0, reader + slabs, reader)
+        slot = chosen[jnp.where(reader >= slabs, reader - slabs, reader)]
         own = slot < half
-        rows = pl.ds(pl.multiple_of(lax.rem(slot, half) * TILE, TILE), TILE)
+        rows = pl.ds(pl.multiple_of(jnp.where(own, slot, slot - half) * TILE, TILE), TILE)
         first = 0
-        for p, part in enumerate(received):
+        for p in members:
+            part = received[p]
             width = part.shape[2]
-            cols = pl.ds(pl.multiple_of(side_col + first, HD), width)
+            cols = pl.ds(pl.multiple_of(side_col + lows[p], HD), width)
             for j, source in enumerate((key, value)):
                 target, sem = out.at[j, :, first : first + width], sems.at[i, j, p]
                 mine = pltpu.make_async_copy(source.at[rows, cols], target, sem)
@@ -52,21 +82,22 @@
         copy.wait()
 
 
-def select_distant(meta, key, value, received, low_col, half):
-    count = meta.shape[0] - 1
-    width = sum(part.shape[2] for part in received)
-    shape = pltpu.VMEM((2, TILE, width), key.dtype)
+def select_distant(chosen, where, here, key, value, received, lows, jobs, half):
+    shapes = [
+        pltpu.VMEM((2, TILE, sum(received[p].shape[2] for p in members)), key.dtype)
+        for _, members in jobs
+    ]
     return pl.pallas_call(
-        functools.partial(distant_kernel, half, low_col),
-        out_shape=[shape] * count,
+        functools.partial(distant_kernel, half, jobs, lows),
+        out_shape=shapes,
         grid_spec=pltpu.PrefetchScalarGridSpec(
-            num_scalar_prefetch=1,
+            num_scalar_prefetch=3,
             grid=(),
             in_specs=[anywhere] * (2 + len(received)),
-            out_specs=[pl.BlockSpec(memory_space=pltpu.VMEM)] * count,
-            scratch_shapes=[pltpu.SemaphoreType.DMA((count, 2, len(received)))],
+            out_specs=[pl.BlockSpec(memory_space=pltpu.VMEM)] * len(jobs),
+            scratch_shapes=[pltpu.SemaphoreType.DMA((len(jobs), 2, len(received)))],
         ),
-    )(meta, key, value, *received)
+    )(chosen, where, here, key, value, *received)
 
 
 def attend_kernel(allowed, where, q_own, q_rec, k_own, v_own, kv_rec, rim_a, rim_b, *rest):
@@ -89,8 +120,8 @@
         first = last
 
     pairs = [(j, min(j + 2, slots)) for j in range(0, slots, 2)]
-    blocks = [(q_own, o_own, t, t) for t in range(tiles)]
-    blocks += [(q_rec, o_send, t, tiles + t) for t in range(tiles)]
+    blocks = [(q_own, o_own, t, where[0] * tiles + t) for t in range(tiles)]
+    blocks += [(q_rec, o_send, t, (1 - where[0]) * tiles + t) for t in range(tiles)]
     largest, mixed = {}, {}
 
     def score(b, pair):
@@ -142,7 +173,7 @@
             settle(b + 1)
 
 
-def attend(allowed, where, arrays, result, chunk_low, far_low, low, high, heads_here):
+def attend(allowed, where, arrays, result, chunk_low, far_lows, low, high, heads_here):
     queries, q_rec, key, value, kv_rec, rim_a, rim_b, far = arrays
     rows = queries.shape[0]
     slots = allowed.shape[1]
@@ -150,11 +181,14 @@
     flat = pl.BlockSpec((rows, HD), lambda i, a, w: (0, low + i))
     whole = pl.BlockSpec((2, rows, HD), lambda i, a, w: (0, 0, low + i))
     part = pl.BlockSpec((2, rows, HD), lambda i, a, w: (0, 0, low - chunk_low + i))
-    tile = pl.BlockSpec((2, TILE, HD), lambda i, a, w: (0, 0, low - far_low + i))
+    tiles = [
+        pl.BlockSpec((2, TILE, HD), lambda i, a, w, start=low - far_low: (0, 0, start + i))
+        for far_low in far_lows
+    ]
     out = pl.BlockSpec((rows, HD), lambda i, a, w: (0, i))
     shape = jax.ShapeDtypeStruct((rows, (high - low) * HD), queries.dtype)
     inputs = [queries, q_rec, key, value, kv_rec, rim_a, rim_b, *far]
-    specs = [own, flat, own, own, part, whole, part] + [tile] * len(far)
+    specs = [own, flat, own, own, part, whole, part] + tiles
     aliases = {}
     kernel = attend_kernel
     if result is not None:
@@ -186,32 +220,30 @@
 
 def place_kernel(lows, heads_here, where, *refs):
     count = len(lows)
-    pieces, out, held, sems = refs[:count], refs[count + 1], refs[count + 2 : -1], refs[-1]
-    loads, stores = [], []
+    pieces, out, sems = refs[:count], refs[count + 1], refs[-1]
+    stores = []
     for i, low in enumerate(lows):
-        cols = pl.ds(pl.multiple_of(((1 - where[0]) * heads_here + low) * HD, HD), held[i].shape[1])
-        loads.append(pltpu.make_async_copy(pieces[i], held[i], sems.at[0, i]))
-        stores.append(pltpu.make_async_copy(held[i], out.at[:, cols], sems.at[1, i]))
-    for load in loads:
-        load.start()
-    for load, store in zip(loads, stores):
-        load.wait()
+        cols = pl.ds(
+            pl.multiple_of(((1 - where[0]) * heads_here + low) * HD, HD), pieces[i].shape[1]
+        )
+        stores.append(pltpu.make_async_copy(pieces[i], out.at[:, cols], sems.at[i]))
+    for store in stores:
         store.start()
     for store in stores:
         store.wait()
 
 
 def place(where, pieces, lows, result, heads_here):
+    pieces = [pltpu.with_memory_space_constraint(piece, pltpu.VMEM) for piece in pieces]
     return pl.pallas_call(
         functools.partial(place_kernel, lows, heads_here),
         out_shape=jax.ShapeDtypeStruct(result.shape, result.dtype),
         grid_spec=pltpu.PrefetchScalarGridSpec(
             num_scalar_prefetch=1,
             grid=(),
-            in_specs=[pl.BlockSpec(memory_space=pltpu.HBM)] * (len(pieces) + 1),
+            in_specs=[pl.BlockSpec(memory_space=pltpu.VMEM)] * len(pieces) + [anywhere],
             out_specs=anywhere,
-            scratch_shapes=[pltpu.VMEM(piece.shape, piece.dtype) for piece in pieces]
-            + [pltpu.SemaphoreType.DMA((2, len(pieces)))],
+            scratch_shapes=[pltpu.SemaphoreType.DMA((len(pieces),))],
         ),
         input_output_aliases={1 + len(pieces): 0},
     )(where, *pieces, result)
@@ -231,33 +263,26 @@
     for level in range(2, FAR + 1):
         shifts += [(1, slabs // 2**level), (-1, slabs // 2**level)]
     live = jnp.arange(key_tiles.shape[1], dtype=jnp.int32)[None, :] < tile_count[:, None]
-    listed_slab = key_tiles // slab_tiles
-    within = key_tiles % slab_tiles
-    turned = (within + half * side) % slab_tiles
-    mine = jnp.where(live & (listed_slab == slab), turned, 0)
+    turned = (key_tiles % slab_tiles + half * side) % slab_tiles
+    mine = jnp.where(live & (key_tiles // slab_tiles == slab), turned, 0)
     chosen = jnp.max(mine.reshape(slabs, -1), axis=1)
-    readers = [
-        (slab + shifts[0][1]) % slabs if direction == 0 else jnp.clip(slab + direction * far, 0, slabs - 1)
-        for direction, far in shifts
-    ]
-    sent_slots = chosen[jnp.stack(readers)]
     where = side.astype(jnp.int32)[None]
-    meta = jnp.concatenate([where, sent_slots])
-
-    offset = listed_slab - slab
-    slots = jnp.where(offset == 0, turned, -1)
+    here = slab.astype(jnp.int32)[None]
+
+    listed = lax.dynamic_slice_in_dim(key_tiles, slab * slab_tiles, slab_tiles, 0)
+    counts = lax.dynamic_slice_in_dim(tile_count, slab * slab_tiles, slab_tiles, 0)
+    offset = listed // slab_tiles - slab
+    within = listed % slab_tiles
+    slots = (within + half * side) % slab_tiles
     slots = jnp.where(offset == -1, 2 * half + half * (1 - side) + within - half, slots)
     slots = jnp.where(offset == 1, 2 * half + half * side + within, slots)
     for i, (direction, far) in enumerate(shifts):
         hit = (jnp.abs(offset) == far) if direction == 0 else (offset == -direction * far)
         slots = jnp.where(hit, 4 * half + i, slots)
-    slots = jnp.where(live, slots, -1)
-    slots = lax.dynamic_slice_in_dim(slots, slab * slab_tiles, slab_tiles, 0)
-    slots = jnp.where(side == 0, slots, jnp.roll(slots, half, axis=0))
-    slot_total = 4 * half + len(shifts)
-    allowed = jnp.any(
-        slots[:, :, None] == jnp.arange(slot_total, dtype=jnp.int32)[None, None, :], axis=1
-    ).astype(jnp.int32)
+    alive = jnp.arange(listed.shape[1], dtype=jnp.int32)[None, :] < counts[:, None]
+    slots = jnp.where(alive, slots, -1)
+    slot_ids = jnp.arange(4 * half + len(shifts), dtype=jnp.int32)
+    allowed = jnp.max((slots[:, :, None] == slot_ids[None, None, :]).astype(jnp.int32), axis=1)
 
     swap = [(0, 1), (1, 0)]
     chunks = chunk_bounds(heads_here)
@@ -274,15 +299,16 @@
     rim_a = None
     for c, (low, high) in enumerate(chunks):
         width = (high - low) * HD
-        packed = jnp.stack(
-            [columns_of(array, 1 - side, low * HD, width) for array in (key_rows, value_rows)]
-        )
+        if c == 0:
+            packed = pack(where, key_rows, value_rows, low * HD, width, True)
+        else:
+            packed = jnp.stack(
+                [columns_of(array, 1 - side, low * HD, width) for array in (key_rows, value_rows)]
+            )
         kv_rec.append(lax.ppermute(packed, "head", swap))
         if c == 0:
             rim_a = lax.ppermute(
-                jnp.stack(
-                    [columns_of(array, side, 0, group_width) for array in (key_rows, value_rows)]
-                ),
+                pack(where, key_rows, value_rows, 0, group_width, False),
                 ("head", "blk"),
                 outward(1),
             )
@@ -291,27 +317,40 @@
     rim_b = []
     for c in range(len(chunks)):
         rim_b.append(lax.ppermute(kv_rec[c], ("head", "blk"), outward(-1)))
-    far = []
-    for members in far_groups:
-        low = chunks[members[0]][0]
+    lows = [low * HD for low, _ in chunks]
+    far = [[None] * len(shifts) for _ in chunks]
+    for jobs in far_jobs:
+        used = sorted({m for _, members in jobs for m in members})
         tiles = select_distant(
-            meta, key_rows, value_rows, [kv_rec[c] for c in members], low * HD, half
-        )
-        arrived = []
-        for (direction, distance), tile in zip(shifts, tiles):
+            chosen,
+            where,
+            here,
+            key_rows,
+            value_rows,
+            [kv_rec[m] for m in used],
+            [lows[m] for m in used],
+            [
+                ((shifts[i][0] or 1) * shifts[i][1], tuple(used.index(m) for m in members))
+                for i, members in jobs
+            ],
+            half,
+        )
+        for (i, members), tile in zip(jobs, tiles):
+            direction, distance = shifts[i]
             if direction == 0:
                 pairs = [(s, (s + distance) % slabs) for s in range(slabs)]
             else:
                 step = direction * distance
                 pairs = [(s, s + step) for s in range(slabs) if 0 <= s + step < slabs]
-            arrived.append(lax.ppermute(tile, "blk", pairs))
-        far += [(low, arrived)] * len(members)
+            arrived = lax.ppermute(tile, "blk", pairs)
+            for m in members:
+                far[m][i] = (chunks[members[0]][0], arrived)
     result, returned = None, []
     for c, a, b in head_runs(heads_here):
-        far_low, arrived = far[c]
+        far_lows, arrived = zip(*far[c])
         arrays = (queries, q_rec, key_rows, value_rows, kv_rec[c], rim_a, rim_b[c], arrived)
         result, sent = attend(
-            allowed, where, arrays, result, chunks[c][0], far_low, a, b, heads_here
+            allowed, where, arrays, result, chunks[c][0], far_lows, a, b, heads_here
         )
         returned.append((a, lax.ppermute(sent, "head", swap)))
     result = place(
@@ -321,7 +360,7 @@
     return result
 
 
-far_groups = ((0,), (1,), (2,))
+far_jobs = tuple(tuple((i, (c,)) for i in range(2 * FAR - 1)) for c in range(3))
 
 
 def chunk_bounds(heads):

time: 217 us -> 187 us (0.86)
  waiting for transfers between devices: 86.3 us -> 54.4 us
  starting transfers between devices: 66.8 us -> 72.4 us
  other arithmetic: 11.6 us -> 7.13 us
    ppermute x3, waiting for transfers between devices: 46.4 us -> 26.2 us  [on_device(): kv_rec.append(lax.ppermute(packed, 'head', swap))]
    ppermute x16, waiting for transfers between devices: 32.9 us -> 19.7 us  [the longest x15 19.7 us: on_device(): arrived = lax.ppermute(tile, 'blk', pairs)]
    ppermute x16, starting transfers between devices: 45.1 us -> 53.6 us  [the longest x15 51.7 us: on_device(): arrived = lax.ppermute(tile, 'blk', pairs)]
    pallas_call x3 -> x5, Pallas kernels: 6.22 us -> 10.2 us  [the longest x3 7.66 us: select_distant(): pl.pallas_call(functools.partial(distant_kernel, half, jobs, lows), out_s...]
    another operation x2 -> x0, other arithmetic: 3.14 us -> none  [on_device(): jnp.stack([columns_of(array, side, 0, group_width) for array in (key_rows...]
    ppermute x3, starting transfers between devices: 15.4 us -> 12.5 us  [on_device(): rim_b.append(lax.ppermute(kv_rec[c], ('head', 'blk'), outward(-1)))]
    another operation x5 -> x4, other arithmetic: 5.8 us -> 4.62 us  [on_device(): jnp.stack([columns_of(array, 1 - side, low * HD, width) for array in (key...]
  transfers between devices with their start and end apart: 26 -> 26, of which waited for: 9 -> 10; matrix products, arithmetic and copies ran while one was open for 5% -> 4% of each run, Pallas kernels for 20% -> 24%
where the time goes in v2:
time: 187 us; the launch traced here: 185 us
  starting transfers between devices  72.4 us (39%)
  waiting for transfers between devices  54.4 us (29%)
  Pallas kernels  46.6 us (25%)
  other arithmetic  7.13 us (4%)
  local copies, waits for them, and re-layouts  3.93 us (2%)
    ppermute x15, starting transfers between devices, on_device(): arrived = lax.ppermute(tile, 'blk', pairs)  51.7 us
    pallas_call x3, Pallas kernels, attend(): pl.pallas_call(kernel, out_shape=[jax.ShapeDtypeStruct(queries.shape, que...  34.8 us
    ppermute x3, waiting for transfers between devices, on_device(): kv_rec.append(lax.ppermute(packed, 'head', swap))  26.2 us
    ppermute x15, waiting for transfers between devices, on_device(): arrived = lax.ppermute(tile, 'blk', pairs)  19.7 us
    ppermute x3, starting transfers between devices, on_device(): rim_b.append(lax.ppermute(kv_rec[c], ('head', 'blk'), outward(-1)))  12.5 us
    ppermute x3, waiting for transfers between devices, on_device(): returned.append((a, lax.ppermute(sent, 'head', swap)))  8.49 us
    pallas_call x3, Pallas kernels, select_distant(): pl.pallas_call(functools.partial(distant_kernel, half, jobs, lows), out_s...  7.66 us
    another operation x4, other arithmetic, on_device(): jnp.stack([columns_of(array, 1 - side, low * HD, width) for array in (key...  4.62 us
  transfers between devices with their start and end apart: 26, of which 10 were waited for; matrix products, arithmetic and copies ran while one was open for 4% of the time, Pallas kernels for 24%

profile of v2, /device:TPU:12, one launch (start us, length us, event | category | flops | bytes accessed | tf_op | source)
XLA Modules:
  0.0 185.0 jit_solution(13080971794849696188)
XLA Ops:
  0.0 1.1 shard_map.58
  1.1 1.6 collective-permute-start.16
  2.6 1.5 shard_map.55
  4.2 1.9 %collective-permute-start.2 = (bf16[2,384,1280]{2,1,0:T(8,128)(2,1)S(1)}, bf16[2,384,1280]{2,1,0:T(8,128)(2,1)}, u32[]{:S(2)}, u32[]{:S(2)}) collective-permute-start(bf16[2,384,1280]{2,1,0:T(8,128)(2,1)S(1)} %shard_map.55), channel_id=1, source_target_pairs={{1,0},{2,1},{3,2},{4,3},{5,4},{6,5},{7,6},{8,7},{9,8},{10,9},{11,1... | collective-permute-start | bytes 5898248 | tf_op jit(solution)/shard_map/ppermute | solution.py:310
  6.1 1.4 select_bitcast_fusion
  7.6 1.0 pad_maximum_fusion
  9.0 1.3 select_bitcast_fusion.2
  10.4 0.9 pad_maximum_fusion.1
  11.3 1.5 collective-permute-start.1
  12.8 1.0 slice_select_fusion
  15.1 2.3 %collective-permute-done.16.rest_0_.kv_rec = bf16[2,384,384]{2,1,0:T(8,128)(2,1)} collective-permute-done((bf16[2,384,384]{2,1,0:T(8,128)(2,1)S(1)}, bf16[2,384,384]{2,1,0:T(8,128)(2,1)}, u32[]{:S(2)}, u32[]{:S(2)}) %collective-permute-start.16) | collective-permute-done | bytes 589856 | tf_op jit(solution)/shard_map/ppermute | solution.py:308
  17.4 2.8 %shard_map.59 = (bf16[2,128,384]{2,1,0:T(8,128)(2,1)S(1)}, bf16[2,128,384]{2,1,0:T(8,128)(2,1)S(1)}, bf16[2,128,384]{2,1,0:T(8,128)(2,1)S(1)}, bf16[2,128,384]{2,1,0:T(8,128)(2,1)}, bf16[2,128,384]{2,1,0:T(8,128)(2,1)}) custom-call(s32[16]{0:T(128)} %reduce_max.28.chosen, s32[1]{0:T(128)} %bitcast.where.refs_1_, s32[1]{0:T(128)} %bitcast.3.here, ...), custom_call_target="tpu_custom_call" | custom-call | tf_op jit(solution)/shard_map/pallas_call | solution.py:90
  20.3 2.7 %collective-permute-start.18 = (bf16[2,128,384]{2,1,0:T(8,128)(2,1)S(1)}, bf16[2,128,384]{2,1,0:T(8,128)(2,1)S(1)}, u32[]{:S(2)}, u32[]{:S(2)}) collective-permute-start(bf16[2,128,384]{2,1,0:T(8,128)(2,1)S(1)} %get-tuple-element.36), channel_id=1, source_target_pairs={{0,8},{1,9},{2,10},{3,11},{4,12},{5,13},{6,14},{7,15},{8,0},{9,1},... | collective-permute-start | bytes 589832 | tf_op jit(solution)/shard_map/ppermute | solution.py:345
  22.9 23.9 %collective-permute-done.1.rest_0_.refs_6_ = bf16[2,384,384]{2,1,0:T(8,128)(2,1)S(1)} collective-permute-done((bf16[2,384,384]{2,1,0:T(8,128)(2,1)}, bf16[2,384,384]{2,1,0:T(8,128)(2,1)S(1)}, u32[]{:S(2)}, u32[]{:S(2)}) %collective-permute-start.1) | collective-permute-done | bytes 589856 | tf_op jit(solution)/shard_map/ppermute | solution.py:308
  46.8 3.5 %collective-permute-start.19 = (bf16[2,128,384]{2,1,0:T(8,128)(2,1)S(1)}, bf16[2,128,384]{2,1,0:T(8,128)(2,1)S(1)}, u32[]{:S(2)}, u32[]{:S(2)}) collective-permute-start(bf16[2,128,384]{2,1,0:T(8,128)(2,1)S(1)} %get-tuple-element.37), channel_id=1, source_target_pairs={{0,4},{1,5},{2,6},{3,7},{4,8},{5,9},{6,10},{7,11},{8,12},{9,13},{1... | collective-permute-start | bytes 589832 | tf_op jit(solution)/shard_map/ppermute | solution.py:345
  50.3 2.4 %collective-permute-start.20 = (bf16[2,128,384]{2,1,0:T(8,128)(2,1)S(1)}, bf16[2,128,384]{2,1,0:T(8,128)(2,1)S(1)}, u32[]{:S(2)}, u32[]{:S(2)}) collective-permute-start(bf16[2,128,384]{2,1,0:T(8,128)(2,1)S(1)} %get-tuple-element.38), channel_id=1, source_target_pairs={{4,0},{5,1},{6,2},{7,3},{8,4},{9,5},{10,6},{11,7},{12,8},{13,9},{1... | collective-permute-start | bytes 589832 | tf_op jit(solution)/shard_map/ppermute | solution.py:345
  52.7 1.7 collective-permute-done.19.rest_1_
  54.4 3.4 %collective-permute-start.21 = (bf16[2,128,384]{2,1,0:T(8,128)(2,1)}, bf16[2,128,384]{2,1,0:T(8,128)(2,1)}, u32[]{:S(2)}, u32[]{:S(2)}) collective-permute-start(bf16[2,128,384]{2,1,0:T(8,128)(2,1)} %get-tuple-element.39), channel_id=1, source_target_pairs={{0,2},{1,3},{2,4},{3,5},{4,6},{5,7},{6,8},{7,9},{8,10},{9,11},{10,... | collective-permute-start | bytes 589832 | tf_op jit(solution)/shard_map/ppermute | solution.py:345
  58.6 2.4 %collective-permute-start.22 = (bf16[2,128,384]{2,1,0:T(8,128)(2,1)}, bf16[2,128,384]{2,1,0:T(8,128)(2,1)}, u32[]{:S(2)}, u32[]{:S(2)}) collective-permute-start(bf16[2,128,384]{2,1,0:T(8,128)(2,1)} %get-tuple-element.40), channel_id=1, source_target_pairs={{2,0},{3,1},{4,2},{5,3},{6,4},{7,5},{8,6},{9,7},{10,8},{11,9},{12,... | collective-permute-start | bytes 589832 | tf_op jit(solution)/shard_map/ppermute | solution.py:345
  61.0 2.7 %shard_map.56 = (bf16[2,128,384]{2,1,0:T(8,128)(2,1)}, bf16[2,128,384]{2,1,0:T(8,128)(2,1)S(1)}, bf16[2,128,384]{2,1,0:T(8,128)(2,1)S(1)}, bf16[2,128,384]{2,1,0:T(8,128)(2,1)S(1)}, bf16[2,128,384]{2,1,0:T(8,128)(2,1)S(1)}) custom-call(s32[16]{0:T(128)} %reduce_max.28.chosen, s32[1]{0:T(128)} %bitcast.where.refs_1_, s32[1]{0:T(128)} %bitcast.3.here, ...), custom_call_target="tpu_custom_call" | custom-call | tf_op jit(solution)/shard_map/pallas_call | solution.py:90
  64.4 0.7 copy-done.1
  65.1 0.7 copy-done.2
  65.8 3.2 %collective-permute-start.4 = (bf16[2,128,384]{2,1,0:T(8,128)(2,1)}, bf16[2,128,384]{2,1,0:T(8,128)(2,1)}, u32[]{:S(2)}, u32[]{:S(2)}) collective-permute-start(bf16[2,128,384]{2,1,0:T(8,128)(2,1)} %get-tuple-element.26), channel_id=1, source_target_pairs={{0,8},{1,9},{2,10},{3,11},{4,12},{5,13},{6,14},{7,15},{8,0},{9,1},... | collective-permute-start | bytes 589832 | tf_op jit(solution)/shard_map/ppermute | solution.py:345
  69.0 2.1 %shard_map.57 = (bf16[2,128,512]{2,1,0:T(8,128)(2,1)S(1)}, bf16[2,128,512]{2,1,0:T(8,128)(2,1)S(1)}, bf16[2,128,512]{2,1,0:T(8,128)(2,1)S(1)}, bf16[2,128,512]{2,1,0:T(8,128)(2,1)S(1)}, bf16[2,128,512]{2,1,0:T(8,128)(2,1)S(1)}) custom-call(s32[16]{0:T(128)} %reduce_max.28.chosen, s32[1]{0:T(128)} %bitcast.where.refs_1_, s32[1]{0:T(128)} %bitcast.3.here, ...), custom_call_target="tpu_custom_call" | custom-call | tf_op jit(solution)/shard_map/pallas_call | solution.py:90
  71.3 3.2 %collective-permute-start.12 = (bf16[2,128,512]{2,1,0:T(8,128)(2,1)S(1)}, bf16[2,128,512]{2,1,0:T(8,128)(2,1)S(1)}, u32[]{:S(2)}, u32[]{:S(2)}) collective-permute-start(bf16[2,128,512]{2,1,0:T(8,128)(2,1)S(1)} %get-tuple-element.32), channel_id=1, source_target_pairs={{0,4},{1,5},{2,6},{3,7},{4,8},{5,9},{6,10},{7,11},{8,12},{9,13},{1... | collective-permute-start | bytes 786440 | tf_op jit(solution)/shard_map/ppermute | solution.py:345
  74.5 5.0 %collective-permute-done.4.refs_9_ = bf16[2,128,384]{2,1,0:T(8,128)(2,1)} collective-permute-done((bf16[2,128,384]{2,1,0:T(8,128)(2,1)}, bf16[2,128,384]{2,1,0:T(8,128)(2,1)}, u32[]{:S(2)}, u32[]{:S(2)}) %collective-permute-start.4) | collective-permute-done | bytes 196640 | tf_op jit(solution)/shard_map/ppermute | solution.py:345
  79.5 1.9 %collective-permute-start.10 = (bf16[2,384,512]{2,1,0:T(8,128)(2,1)}, bf16[2,384,512]{2,1,0:T(8,128)(2,1)}, u32[]{:S(2)}, u32[]{:S(2)}) collective-permute-start(bf16[2,384,512]{2,1,0:T(8,128)(2,1)} %collective-permute-done.9.rest_0_.refs_6_), channel_id=1, source_target_pairs={{0,1},{1,2},{2,3},{3,4},{4,5},{5,6},{6,7},{7,8},{8,9},{9,10},{10,1... | collective-permute-start | bytes 2359304 | tf_op jit(solution)/shard_map/ppermute | solution.py:319
  81.4 5.5 %collective-permute-start.13 = (bf16[2,128,512]{2,1,0:T(8,128)(2,1)S(1)}, bf16[2,128,512]{2,1,0:T(8,128)(2,1)S(1)}, u32[]{:S(2)}, u32[]{:S(2)}) collective-permute-start(bf16[2,128,512]{2,1,0:T(8,128)(2,1)S(1)} %get-tuple-element.33), channel_id=1, source_target_pairs={{4,0},{5,1},{6,2},{7,3},{8,4},{9,5},{10,6},{11,7},{12,8},{13,9},{1... | collective-permute-start | bytes 786440 | tf_op jit(solution)/shard_map/ppermute | solution.py:345
  86.9 1.9 %collective-permute-start.14 = (bf16[2,128,512]{2,1,0:T(8,128)(2,1)S(1)}, bf16[2,128,512]{2,1,0:T(8,128)(2,1)S(1)}, u32[]{:S(2)}, u32[]{:S(2)}) collective-permute-start(bf16[2,128,512]{2,1,0:T(8,128)(2,1)S(1)} %get-tuple-element.34), channel_id=1, source_target_pairs={{0,2},{1,3},{2,4},{3,5},{4,6},{5,7},{6,8},{7,9},{8,10},{9,11},{10,... | collective-permute-start | bytes 786440 | tf_op jit(solution)/shard_map/ppermute | solution.py:345
  88.8 1.8 collective-permute-done.12.refs_10_
  90.6 1.9 %collective-permute-start.17 = (bf16[2,384,384]{2,1,0:T(8,128)(2,1)}, bf16[2,384,384]{2,1,0:T(8,128)(2,1)}, u32[]{:S(2)}, u32[]{:S(2)}) collective-permute-start(bf16[2,384,384]{2,1,0:T(8,128)(2,1)} %collective-permute-done.16.rest_0_.kv_rec), channel_id=1, source_target_pairs={{0,1},{1,2},{2,3},{3,4},{4,5},{5,6},{6,7},{7,8},{8,9},{9,10},{10,1... | collective-permute-start | bytes 1769480 | tf_op jit(solution)/shard_map/ppermute | solution.py:319
  92.5 4.1 %collective-permute-start.15 = (bf16[2,128,512]{2,1,0:T(8,128)(2,1)S(1)}, bf16[2,128,512]{2,1,0:T(8,128)(2,1)}, u32[]{:S(2)}, u32[]{:S(2)}) collective-permute-start(bf16[2,128,512]{2,1,0:T(8,128)(2,1)S(1)} %get-tuple-element.35), channel_id=1, source_target_pairs={{2,0},{3,1},{4,2},{5,3},{6,4},{7,5},{8,6},{9,7},{10,8},{11,9},{12,... | collective-permute-start | bytes 786440 | tf_op jit(solution)/shard_map/ppermute | solution.py:345
  96.6 1.4 collective-permute-done.14.refs_12_
  98.0 8.6 %collective-permute-start.3 = (bf16[2,384,384]{2,1,0:T(8,128)(2,1)}, bf16[2,384,384]{2,1,0:T(8,128)(2,1)S(1)}, u32[]{:S(2)}, u32[]{:S(2)}) collective-permute-start(bf16[2,384,384]{2,1,0:T(8,128)(2,1)} %copy-done.4), channel_id=1, source_target_pairs={{0,1},{1,2},{2,3},{3,4},{4,5},{5,6},{6,7},{7,8},{8,9},{9,10},{10,1... | collective-permute-start | bytes 1769480 | tf_op jit(solution)/shard_map/ppermute | solution.py:319
  106.7 9.8 %collective-permute-done.15.refs_13_ = bf16[2,128,512]{2,1,0:T(8,128)(2,1)} collective-permute-done((bf16[2,128,512]{2,1,0:T(8,128)(2,1)S(1)}, bf16[2,128,512]{2,1,0:T(8,128)(2,1)}, u32[]{:S(2)}, u32[]{:S(2)}) %collective-permute-start.15) | collective-permute-done | bytes 262176 | tf_op jit(solution)/shard_map/ppermute | solution.py:345
  116.5 9.7 %collective-permute-start.5 = (bf16[2,128,384]{2,1,0:T(8,128)(2,1)}, bf16[2,128,384]{2,1,0:T(8,128)(2,1)S(1)}, u32[]{:S(2)}, u32[]{:S(2)}) collective-permute-start(bf16[2,128,384]{2,1,0:T(8,128)(2,1)} %copy-done.2), channel_id=1, source_target_pairs={{0,4},{1,5},{2,6},{3,7},{4,8},{5,9},{6,10},{7,11},{8,12},{9,13},{1... | collective-permute-start | bytes 589832 | tf_op jit(solution)/shard_map/ppermute | solution.py:345
  126.4 1.9 %collective-permute-start.6 = (bf16[2,128,384]{2,1,0:T(8,128)(2,1)}, bf16[2,128,384]{2,1,0:T(8,128)(2,1)S(1)}, u32[]{:S(2)}, u32[]{:S(2)}) collective-permute-start(bf16[2,128,384]{2,1,0:T(8,128)(2,1)} %copy-done.1), channel_id=1, source_target_pairs={{4,0},{5,1},{6,2},{7,3},{8,4},{9,5},{10,6},{11,7},{12,8},{13,9},{1... | collective-permute-start | bytes 589832 | tf_op jit(solution)/shard_map/ppermute | solution.py:345
  128.3 5.9 %collective-permute-start.7 = (bf16[2,128,384]{2,1,0:T(8,128)(2,1)}, bf16[2,128,384]{2,1,0:T(8,128)(2,1)}, u32[]{:S(2)}, u32[]{:S(2)}) collective-permute-start(bf16[2,128,384]{2,1,0:T(8,128)(2,1)} %copy-done), channel_id=1, source_target_pairs={{0,2},{1,3},{2,4},{3,5},{4,6},{5,7},{6,8},{7,9},{8,10},{9,11},{10,... | collective-permute-start | bytes 589832 | tf_op jit(solution)/shard_map/ppermute | solution.py:345
  134.3 1.9 %collective-permute-start.8 = (bf16[2,128,384]{2,1,0:T(8,128)(2,1)S(1)}, bf16[2,128,384]{2,1,0:T(8,128)(2,1)S(1)}, u32[]{:S(2)}, u32[]{:S(2)}) collective-permute-start(bf16[2,128,384]{2,1,0:T(8,128)(2,1)S(1)} %get-tuple-element.30), channel_id=1, source_target_pairs={{2,0},{3,1},{4,2},{5,3},{6,4},{7,5},{8,6},{9,7},{10,8},{11,9},{12,... | collective-permute-start | bytes 589832 | tf_op jit(solution)/shard_map/ppermute | solution.py:345
  136.2 0.7 convert_reduce_fusion.allowed.refs_0_
  136.9 10.6 %shard_map.60 = (bf16[384,2560]{1,0:T(8,128)(2,1)}, bf16[384,384]{1,0:T(8,128)(2,1)}) custom-call(s32[6,17]{1,0:T(8,128)} %convert_reduce_fusion.allowed.refs_0_, s32[1]{0:T(128)} %bitcast.where.refs_1_, bf16[384,2560]{1,0:T(8,128)(2,1)} %refs_2_.3, bf16[384,1280]{1,0:T(8,128)(2,1)} %collective-permute-done.q_rec.refs_3_, bf16[384,2560]{1,0:T(8,128)(2,1)} %refs_4_.3, ...), custom_call_target="tpu_custom_call" | custom-call | tf_op jit(solution)/shard_map/pallas_call | solution.py:198
  147.5 13.5 %shard_map.61 = (bf16[384,2560]{1,0:T(8,128)(2,1)}, bf16[384,512]{1,0:T(8,128)(2,1)}) custom-call(s32[6,17]{1,0:T(8,128)} %convert_reduce_fusion.allowed.refs_0_, s32[1]{0:T(128)} %bitcast.where.refs_1_, bf16[384,2560]{1,0:T(8,128)(2,1)} %refs_2_.3, bf16[384,1280]{1,0:T(8,128)(2,1)} %collective-permute-done.q_rec.refs_3_, ...), custom_call_target="tpu_custom_call", output_to_operand_aliasing={{0}: (14, {})} | custom-call | tf_op jit(solution)/shard_map/pallas_call | solution.py:198
  161.2 2.1 %collective-permute-start.24 = (bf16[384,384]{1,0:T(8,128)(2,1)S(1)}, bf16[384,384]{1,0:T(8,128)(2,1)S(1)}, u32[]{:S(2)}, u32[]{:S(2)}) collective-permute-start(bf16[384,384]{1,0:T(8,128)(2,1)S(1)} %copy-done.18), channel_id=1, source_target_pairs={{0,16},{16,0},{1,17},{17,1},{2,18},{18,2},{3,19},{19,3},{4,20},{20... | collective-permute-start | bytes 884744 | tf_op jit(solution)/shard_map/ppermute | solution.py:355
  164.1 10.7 %shard_map.62 = (bf16[384,2560]{1,0:T(8,128)(2,1)}, bf16[384,384]{1,0:T(8,128)(2,1)}) custom-call(s32[6,17]{1,0:T(8,128)} %convert_reduce_fusion.allowed.refs_0_, s32[1]{0:T(128)} %bitcast.where.refs_1_, bf16[384,2560]{1,0:T(8,128)(2,1)} %refs_2_.3, bf16[384,1280]{1,0:T(8,128)(2,1)} %collective-permute-done.q_rec.refs_3_, ...), custom_call_target="tpu_custom_call", output_to_operand_aliasing={{0}: (14, {})} | custom-call | tf_op jit(solution)/shard_map/pallas_call | solution.py:198
  174.9 4.6 %collective-permute-done.24.refs_0_ = bf16[384,384]{1,0:T(8,128)(2,1)S(1)} collective-permute-done((bf16[384,384]{1,0:T(8,128)(2,1)S(1)}, bf16[384,384]{1,0:T(8,128)(2,1)S(1)}, u32[]{:S(2)}, u32[]{:S(2)}) %collective-permute-start.24) | collective-permute-done | bytes 294944 | tf_op jit(solution)/shard_map/ppermute | solution.py:355
  179.5 0.9 shard_map.63.refs_1_
  180.4 3.9 %collective-permute-done.23.refs_0_ = bf16[384,384]{1,0:T(8,128)(2,1)S(1)} collective-permute-done((bf16[384,384]{1,0:T(8,128)(2,1)}, bf16[384,384]{1,0:T(8,128)(2,1)S(1)}, u32[]{:S(2)}, u32[]{:S(2)}) %collective-permute-start.23) | collective-permute-done | bytes 294944 | tf_op jit(solution)/shard_map/ppermute | solution.py:355
  184.3 0.7 shard_map.64
  (64 shorter events, 4.7 us)
Async XLA Ops:
  1.1 16.4 %collective-permute-start.16 = (bf16[2,384,384]{2,1,0:T(8,128)(2,1)S(1)}, bf16[2,384,384]{2,1,0:T(8,128)(2,1)}, u32[]{:S(2)}, u32[]{:S(2)}) collective-permute-start(bf16[2,384,384]{2,1,0:T(8,128)(2,1)S(1)} %shard_map.58), channel_id=1, source_target_pairs={{0,16},{16,0},{1,17},{17,1},{2,18},{18,2},{3,19},{19,3},{4,20},{20... | collective-permute-start | bytes 1769480 | tf_op jit(solution)/shard_map/ppermute | solution.py:308
  4.2 130.1 %collective-permute-start.2 = (bf16[2,384,1280]{2,1,0:T(8,128)(2,1)S(1)}, bf16[2,384,1280]{2,1,0:T(8,128)(2,1)}, u32[]{:S(2)}, u32[]{:S(2)}) collective-permute-start(bf16[2,384,1280]{2,1,0:T(8,128)(2,1)S(1)} %shard_map.55), channel_id=1, source_target_pairs={{1,0},{2,1},{3,2},{4,3},{5,4},{6,5},{7,6},{8,7},{9,8},{10,9},{11,1... | collective-permute-start | bytes 5898248 | tf_op jit(solution)/shard_map/ppermute | solution.py:310
  7.5 5.2 %copy-start.3 = (bf16[384,2560]{1,0:T(8,128)(2,1)S(1)}, bf16[384,2560]{1,0:T(8,128)(2,1)}, u32[]{:S(2)}) copy-start(bf16[384,2560]{1,0:T(8,128)(2,1)} %refs_2_.3) | copy-start | bytes 5898244
  8.5 57.3 %collective-permute-start.9 = (bf16[2,384,512]{2,1,0:T(8,128)(2,1)}, bf16[2,384,512]{2,1,0:T(8,128)(2,1)}, u32[]{:S(2)}, u32[]{:S(2)}) collective-permute-start(bf16[2,384,512]{2,1,0:T(8,128)(2,1)} %pad_maximum_fusion), channel_id=1, source_target_pairs={{0,16},{16,0},{1,17},{17,1},{2,18},{18,2},{3,19},{19,3},{4,20},{20... | collective-permute-start | bytes 2359304 | tf_op jit(solution)/shard_map/ppermute | solution.py:308
  10.4 4.0 %copy-start.16 = (s32[96,16]{0,1:T(8,128)S(1)}, s32[96,16]{0,1:T(8,128)}, u32[]{:S(2)}) copy-start(s32[96,16]{0,1:T(8,128)} %param.8) | copy-start | bytes 18436
  10.4 4.0 %copy-start.17 = (s32[96]{0:T(128)S(1)}, s32[96]{0:T(128)}, u32[]{:S(2)}) copy-start(s32[96]{0:T(128)} %param.9) | copy-start | bytes 1156
  11.3 35.5 %collective-permute-start.1 = (bf16[2,384,384]{2,1,0:T(8,128)(2,1)}, bf16[2,384,384]{2,1,0:T(8,128)(2,1)S(1)}, u32[]{:S(2)}, u32[]{:S(2)}) collective-permute-start(bf16[2,384,384]{2,1,0:T(8,128)(2,1)} %pad_maximum_fusion.1), channel_id=1, source_target_pairs={{0,16},{16,0},{1,17},{17,1},{2,18},{18,2},{3,19},{19,3},{4,20},{20... | collective-permute-start | bytes 1769480 | tf_op jit(solution)/shard_map/ppermute | solution.py:308
  13.8 67.6 %collective-permute-start = (bf16[384,1280]{1,0:T(8,128)(2,1)}, bf16[384,1280]{1,0:T(8,128)(2,1)}, u32[]{:S(2)}, u32[]{:S(2)}) collective-permute-start(bf16[384,1280]{1,0:T(8,128)(2,1)} %slice_select_fusion), channel_id=1, source_target_pairs={{0,16},{16,0},{1,17},{17,1},{2,18},{18,2},{3,19},{19,3},{4,20},{20... | collective-permute-start | bytes 2949128 | tf_op jit(solution)/shard_map/ppermute | solution.py:315
  20.3 30.1 %collective-permute-start.18 = (bf16[2,128,384]{2,1,0:T(8,128)(2,1)S(1)}, bf16[2,128,384]{2,1,0:T(8,128)(2,1)S(1)}, u32[]{:S(2)}, u32[]{:S(2)}) collective-permute-start(bf16[2,128,384]{2,1,0:T(8,128)(2,1)S(1)} %get-tuple-element.36), channel_id=1, source_target_pairs={{0,8},{1,9},{2,10},{3,11},{4,12},{5,13},{6,14},{7,15},{8,0},{9,1},... | collective-permute-start | bytes 589832 | tf_op jit(solution)/shard_map/ppermute | solution.py:345
  46.8 14.2 %copy-start.4 = (bf16[2,384,384]{2,1,0:T(8,128)(2,1)}, bf16[2,384,384]{2,1,0:T(8,128)(2,1)S(1)}, u32[]{:S(2)}) copy-start(bf16[2,384,384]{2,1,0:T(8,128)(2,1)S(1)} %collective-permute-done.1.rest_0_.refs_6_) | copy-start | bytes 1769476
  46.8 7.6 %collective-permute-start.19 = (bf16[2,128,384]{2,1,0:T(8,128)(2,1)S(1)}, bf16[2,128,384]{2,1,0:T(8,128)(2,1)S(1)}, u32[]{:S(2)}, u32[]{:S(2)}) collective-permute-start(bf16[2,128,384]{2,1,0:T(8,128)(2,1)S(1)} %get-tuple-element.37), channel_id=1, source_target_pairs={{0,4},{1,5},{2,6},{3,7},{4,8},{5,9},{6,10},{7,11},{8,12},{9,13},{1... | collective-permute-start | bytes 589832 | tf_op jit(solution)/shard_map/ppermute | solution.py:345
  50.3 7.6 %copy-start.10 = (bf16[2,128,384]{2,1,0:T(8,128)(2,1)}, bf16[2,128,384]{2,1,0:T(8,128)(2,1)S(1)}, u32[]{:S(2)}) copy-start(bf16[2,128,384]{2,1,0:T(8,128)(2,1)S(1)} %collective-permute-done.18.rest_0_) | copy-start | bytes 589828
  50.3 7.6 %collective-permute-start.20 = (bf16[2,128,384]{2,1,0:T(8,128)(2,1)S(1)}, bf16[2,128,384]{2,1,0:T(8,128)(2,1)S(1)}, u32[]{:S(2)}, u32[]{:S(2)}) collective-permute-start(bf16[2,128,384]{2,1,0:T(8,128)(2,1)S(1)} %get-tuple-element.38), channel_id=1, source_target_pairs={{4,0},{5,1},{6,2},{7,3},{8,4},{9,5},{10,6},{11,7},{12,8},{13,9},{1... | collective-permute-start | bytes 589832 | tf_op jit(solution)/shard_map/ppermute | solution.py:345
  54.4 3.5 %copy-start.11 = (bf16[2,128,384]{2,1,0:T(8,128)(2,1)}, bf16[2,128,384]{2,1,0:T(8,128)(2,1)S(1)}, u32[]{:S(2)}) copy-start(bf16[2,128,384]{2,1,0:T(8,128)(2,1)S(1)} %collective-permute-done.19.rest_1_) | copy-start | bytes 589828
  54.4 16.8 %collective-permute-start.21 = (bf16[2,128,384]{2,1,0:T(8,128)(2,1)}, bf16[2,128,384]{2,1,0:T(8,128)(2,1)}, u32[]{:S(2)}, u32[]{:S(2)}) collective-permute-start(bf16[2,128,384]{2,1,0:T(8,128)(2,1)} %get-tuple-element.39), channel_id=1, source_target_pairs={{0,2},{1,3},{2,4},{3,5},{4,6},{5,7},{6,8},{7,9},{8,10},{9,11},{10,... | collective-permute-start | bytes 589832 | tf_op jit(solution)/shard_map/ppermute | solution.py:345
  57.9 0.7 copy-start.12
  58.6 12.7 %collective-permute-start.22 = (bf16[2,128,384]{2,1,0:T(8,128)(2,1)}, bf16[2,128,384]{2,1,0:T(8,128)(2,1)}, u32[]{:S(2)}, u32[]{:S(2)}) collective-permute-start(bf16[2,128,384]{2,1,0:T(8,128)(2,1)} %get-tuple-element.40), channel_id=1, source_target_pairs={{2,0},{3,1},{4,2},{5,3},{6,4},{7,5},{8,6},{9,7},{10,8},{11,9},{12,... | collective-permute-start | bytes 589832 | tf_op jit(solution)/shard_map/ppermute | solution.py:345
  63.7 0.7 copy-start
  64.4 0.7 copy-start.1
  65.1 0.7 copy-start.2
  65.8 13.6 %collective-permute-start.4 = (bf16[2,128,384]{2,1,0:T(8,128)(2,1)}, bf16[2,128,384]{2,1,0:T(8,128)(2,1)}, u32[]{:S(2)}, u32[]{:S(2)}) collective-permute-start(bf16[2,128,384]{2,1,0:T(8,128)(2,1)} %get-tuple-element.26), channel_id=1, source_target_pairs={{0,8},{1,9},{2,10},{3,11},{4,12},{5,13},{6,14},{7,15},{8,0},{9,1},... | collective-permute-start | bytes 589832 | tf_op jit(solution)/shard_map/ppermute | solution.py:345
  71.2 15.7 %collective-permute-start.11 = (bf16[2,128,512]{2,1,0:T(8,128)(2,1)S(1)}, bf16[2,128,512]{2,1,0:T(8,128)(2,1)S(1)}, u32[]{:S(2)}, u32[]{:S(2)}) collective-permute-start(bf16[2,128,512]{2,1,0:T(8,128)(2,1)S(1)} %get-tuple-element.31), channel_id=1, source_target_pairs={{0,8},{1,9},{2,10},{3,11},{4,12},{5,13},{6,14},{7,15},{8,0},{9,1},... | collective-permute-start | bytes 786440 | tf_op jit(solution)/shard_map/ppermute | solution.py:345
  71.3 19.3 %collective-permute-start.12 = (bf16[2,128,512]{2,1,0:T(8,128)(2,1)S(1)}, bf16[2,128,512]{2,1,0:T(8,128)(2,1)S(1)}, u32[]{:S(2)}, u32[]{:S(2)}) collective-permute-start(bf16[2,128,512]{2,1,0:T(8,128)(2,1)S(1)} %get-tuple-element.32), channel_id=1, source_target_pairs={{0,4},{1,5},{2,6},{3,7},{4,8},{5,9},{6,10},{7,11},{8,12},{9,13},{1... | collective-permute-start | bytes 786440 | tf_op jit(solution)/shard_map/ppermute | solution.py:345
  79.5 48.8 %collective-permute-start.10 = (bf16[2,384,512]{2,1,0:T(8,128)(2,1)}, bf16[2,384,512]{2,1,0:T(8,128)(2,1)}, u32[]{:S(2)}, u32[]{:S(2)}) collective-permute-start(bf16[2,384,512]{2,1,0:T(8,128)(2,1)} %collective-permute-done.9.rest_0_.refs_6_), channel_id=1, source_target_pairs={{0,1},{1,2},{2,3},{3,4},{4,5},{5,6},{6,7},{7,8},{8,9},{9,10},{10,1... | collective-permute-start | bytes 2359304 | tf_op jit(solution)/shard_map/ppermute | solution.py:319
  81.4 11.1 %collective-permute-start.13 = (bf16[2,128,512]{2,1,0:T(8,128)(2,1)S(1)}, bf16[2,128,512]{2,1,0:T(8,128)(2,1)S(1)}, u32[]{:S(2)}, u32[]{:S(2)}) collective-permute-start(bf16[2,128,512]{2,1,0:T(8,128)(2,1)S(1)} %get-tuple-element.33), channel_id=1, source_target_pairs={{4,0},{5,1},{6,2},{7,3},{8,4},{9,5},{10,6},{11,7},{12,8},{13,9},{1... | collective-permute-start | bytes 786440 | tf_op jit(solution)/shard_map/ppermute | solution.py:345
  86.9 11.1 %copy-start.6 = (bf16[2,128,512]{2,1,0:T(8,128)(2,1)}, bf16[2,128,512]{2,1,0:T(8,128)(2,1)S(1)}, u32[]{:S(2)}) copy-start(bf16[2,128,512]{2,1,0:T(8,128)(2,1)S(1)} %collective-permute-done.11.refs_9_) | copy-start | bytes 786436
  86.9 11.1 %collective-permute-start.14 = (bf16[2,128,512]{2,1,0:T(8,128)(2,1)S(1)}, bf16[2,128,512]{2,1,0:T(8,128)(2,1)S(1)}, u32[]{:S(2)}, u32[]{:S(2)}) collective-permute-start(bf16[2,128,512]{2,1,0:T(8,128)(2,1)S(1)} %get-tuple-element.34), channel_id=1, source_target_pairs={{0,2},{1,3},{2,4},{3,5},{4,6},{5,7},{6,8},{7,9},{8,10},{9,11},{10,... | collective-permute-start | bytes 786440 | tf_op jit(solution)/shard_map/ppermute | solution.py:345
  90.6 7.4 %copy-start.7 = (bf16[2,128,512]{2,1,0:T(8,128)(2,1)}, bf16[2,128,512]{2,1,0:T(8,128)(2,1)S(1)}, u32[]{:S(2)}) copy-start(bf16[2,128,512]{2,1,0:T(8,128)(2,1)S(1)} %collective-permute-done.12.refs_10_) | copy-start | bytes 786436
  90.6 35.8 %collective-permute-start.17 = (bf16[2,384,384]{2,1,0:T(8,128)(2,1)}, bf16[2,384,384]{2,1,0:T(8,128)(2,1)}, u32[]{:S(2)}, u32[]{:S(2)}) collective-permute-start(bf16[2,384,384]{2,1,0:T(8,128)(2,1)} %collective-permute-done.16.rest_0_.kv_rec), channel_id=1, source_target_pairs={{0,1},{1,2},{2,3},{3,4},{4,5},{5,6},{6,7},{7,8},{8,9},{9,10},{10,1... | collective-permute-start | bytes 1769480 | tf_op jit(solution)/shard_map/ppermute | solution.py:319
  92.5 5.5 %copy-start.8 = (bf16[2,128,512]{2,1,0:T(8,128)(2,1)}, bf16[2,128,512]{2,1,0:T(8,128)(2,1)S(1)}, u32[]{:S(2)}) copy-start(bf16[2,128,512]{2,1,0:T(8,128)(2,1)S(1)} %collective-permute-done.13.refs_11_) | copy-start | bytes 786436
  92.5 23.9 %collective-permute-start.15 = (bf16[2,128,512]{2,1,0:T(8,128)(2,1)S(1)}, bf16[2,128,512]{2,1,0:T(8,128)(2,1)}, u32[]{:S(2)}, u32[]{:S(2)}) collective-permute-start(bf16[2,128,512]{2,1,0:T(8,128)(2,1)S(1)} %get-tuple-element.35), channel_id=1, source_target_pairs={{2,0},{3,1},{4,2},{5,3},{6,4},{7,5},{8,6},{9,7},{10,8},{11,9},{12,... | collective-permute-start | bytes 786440 | tf_op jit(solution)/shard_map/ppermute | solution.py:345
  98.0 49.5 %copy-start.9 = (bf16[2,128,512]{2,1,0:T(8,128)(2,1)}, bf16[2,128,512]{2,1,0:T(8,128)(2,1)S(1)}, u32[]{:S(2)}) copy-start(bf16[2,128,512]{2,1,0:T(8,128)(2,1)S(1)} %collective-permute-done.14.refs_12_) | copy-start | bytes 786436
  98.0 65.2 %collective-permute-start.3 = (bf16[2,384,384]{2,1,0:T(8,128)(2,1)}, bf16[2,384,384]{2,1,0:T(8,128)(2,1)S(1)}, u32[]{:S(2)}, u32[]{:S(2)}) collective-permute-start(bf16[2,384,384]{2,1,0:T(8,128)(2,1)} %copy-done.4), channel_id=1, source_target_pairs={{0,1},{1,2},{2,3},{3,4},{4,5},{5,6},{6,7},{7,8},{8,9},{9,10},{10,1... | collective-permute-start | bytes 1769480 | tf_op jit(solution)/shard_map/ppermute | solution.py:319
  116.5 44.6 %collective-permute-start.5 = (bf16[2,128,384]{2,1,0:T(8,128)(2,1)}, bf16[2,128,384]{2,1,0:T(8,128)(2,1)S(1)}, u32[]{:S(2)}, u32[]{:S(2)}) collective-permute-start(bf16[2,128,384]{2,1,0:T(8,128)(2,1)} %copy-done.2), channel_id=1, source_target_pairs={{0,4},{1,5},{2,6},{3,7},{4,8},{5,9},{6,10},{7,11},{8,12},{9,13},{1... | collective-permute-start | bytes 589832 | tf_op jit(solution)/shard_map/ppermute | solution.py:345
  126.4 34.8 %collective-permute-start.6 = (bf16[2,128,384]{2,1,0:T(8,128)(2,1)}, bf16[2,128,384]{2,1,0:T(8,128)(2,1)S(1)}, u32[]{:S(2)}, u32[]{:S(2)}) collective-permute-start(bf16[2,128,384]{2,1,0:T(8,128)(2,1)} %copy-done.1), channel_id=1, source_target_pairs={{4,0},{5,1},{6,2},{7,3},{8,4},{9,5},{10,6},{11,7},{12,8},{13,9},{1... | collective-permute-start | bytes 589832 | tf_op jit(solution)/shard_map/ppermute | solution.py:345
  128.3 34.9 %collective-permute-start.7 = (bf16[2,128,384]{2,1,0:T(8,128)(2,1)}, bf16[2,128,384]{2,1,0:T(8,128)(2,1)}, u32[]{:S(2)}, u32[]{:S(2)}) collective-permute-start(bf16[2,128,384]{2,1,0:T(8,128)(2,1)} %copy-done), channel_id=1, source_target_pairs={{0,2},{1,3},{2,4},{3,5},{4,6},{5,7},{6,8},{7,9},{8,10},{9,11},{10,... | collective-permute-start | bytes 589832 | tf_op jit(solution)/shard_map/ppermute | solution.py:345
  134.3 29.0 %collective-permute-start.8 = (bf16[2,128,384]{2,1,0:T(8,128)(2,1)S(1)}, bf16[2,128,384]{2,1,0:T(8,128)(2,1)S(1)}, u32[]{:S(2)}, u32[]{:S(2)}) collective-permute-start(bf16[2,128,384]{2,1,0:T(8,128)(2,1)S(1)} %get-tuple-element.30), channel_id=1, source_target_pairs={{2,0},{3,1},{4,2},{5,3},{6,4},{7,5},{8,6},{9,7},{10,8},{11,9},{12,... | collective-permute-start | bytes 589832 | tf_op jit(solution)/shard_map/ppermute | solution.py:345
  147.5 13.6 %copy-start.18 = (bf16[384,384]{1,0:T(8,128)(2,1)S(1)}, bf16[384,384]{1,0:T(8,128)(2,1)}, u32[]{:S(2)}) copy-start(bf16[384,384]{1,0:T(8,128)(2,1)} %get-tuple-element.44) | copy-start | bytes 884740
  161.0 2.2 %copy-start.13 = (bf16[2,128,384]{2,1,0:T(8,128)(2,1)}, bf16[2,128,384]{2,1,0:T(8,128)(2,1)S(1)}, u32[]{:S(2)}) copy-start(bf16[2,128,384]{2,1,0:T(8,128)(2,1)S(1)} %collective-permute-done.5.refs_10_) | copy-start | bytes 589828
  161.1 18.4 %collective-permute-start.25 = (bf16[384,512]{1,0:T(8,128)(2,1)}, bf16[384,512]{1,0:T(8,128)(2,1)S(1)}, u32[]{:S(2)}, u32[]{:S(2)}) collective-permute-start(bf16[384,512]{1,0:T(8,128)(2,1)} %get-tuple-element.45), channel_id=1, source_target_pairs={{0,16},{16,0},{1,17},{17,1},{2,18},{18,2},{3,19},{19,3},{4,20},{20... | collective-permute-start | bytes 1179656 | tf_op jit(solution)/shard_map/ppermute | solution.py:355
  161.1 2.1 %copy-start.14 = (bf16[2,128,384]{2,1,0:T(8,128)(2,1)}, bf16[2,128,384]{2,1,0:T(8,128)(2,1)S(1)}, u32[]{:S(2)}) copy-start(bf16[2,128,384]{2,1,0:T(8,128)(2,1)S(1)} %collective-permute-done.6.refs_11_) | copy-start | bytes 589828
  161.2 18.3 %collective-permute-start.24 = (bf16[384,384]{1,0:T(8,128)(2,1)S(1)}, bf16[384,384]{1,0:T(8,128)(2,1)S(1)}, u32[]{:S(2)}, u32[]{:S(2)}) collective-permute-start(bf16[384,384]{1,0:T(8,128)(2,1)S(1)} %copy-done.18), channel_id=1, source_target_pairs={{0,16},{16,0},{1,17},{17,1},{2,18},{18,2},{3,19},{19,3},{4,20},{20... | collective-permute-start | bytes 884744 | tf_op jit(solution)/shard_map/ppermute | solution.py:355
  163.2 0.7 copy-start.15
  163.2 0.9 copy-start.5
  174.8 9.5 %collective-permute-start.23 = (bf16[384,384]{1,0:T(8,128)(2,1)}, bf16[384,384]{1,0:T(8,128)(2,1)S(1)}, u32[]{:S(2)}, u32[]{:S(2)}) collective-permute-start(bf16[384,384]{1,0:T(8,128)(2,1)} %get-tuple-element.43), channel_id=1, source_target_pairs={{0,16},{16,0},{1,17},{17,1},{2,18},{18,2},{3,19},{19,3},{4,20},{20... | collective-permute-start | bytes 884744 | tf_op jit(solution)/shard_map/ppermute | solution.py:355

commit v3 on v2

--- a/solution.py
+++ b/solution.py
@@ -54,15 +54,28 @@
     )(where, key, value)
 
 
+def across_from(slab, distance, near):
+    forth = 1 - 2 * lax.rem(lax.div(slab, distance), 2)
+    return slab + distance * forth if near else slab - distance * forth
+
+
+def exchange(slabs, distance, near):
+    pairs = []
+    for s in range(slabs):
+        forth = 1 - 2 * ((s // distance) % 2)
+        other = s + distance * forth if near else s - distance * forth
+        pairs.append((s, other if 0 <= other < slabs else s ^ 1))
+    return pairs
+
+
 def distant_kernel(half, jobs, lows, chosen, where, here, key, value, *rest):
     received, outs, sems = rest[: len(lows)], rest[len(lows) : -1], rest[-1]
     slabs = chosen.shape[0]
     side_col = where[0] * (key.shape[1] // 2)
     waits = []
     for i, ((step, members), out) in enumerate(zip(jobs, outs)):
-        reader = here[0] + step
-        reader = jnp.where(reader < 0, reader + slabs, reader)
-        slot = chosen[jnp.where(reader >= slabs, reader - slabs, reader)]
+        reader = across_from(here[0], *step)
+        slot = chosen[jnp.clip(reader, 0, slabs - 1)]
         own = slot < half
         rows = pl.ds(pl.multiple_of(jnp.where(own, slot, slot - half) * TILE, TILE), TILE)
         first = 0
@@ -70,13 +83,27 @@
             part = received[p]
             width = part.shape[2]
             cols = pl.ds(pl.multiple_of(side_col + lows[p], HD), width)
-            for j, source in enumerate((key, value)):
-                target, sem = out.at[j, :, first : first + width], sems.at[i, j, p]
-                mine = pltpu.make_async_copy(source.at[rows, cols], target, sem)
-                theirs = pltpu.make_async_copy(part.at[j, rows, :], target, sem)
-                pl.when(own)(mine.start)
-                pl.when(jnp.logical_not(own))(theirs.start)
-                waits.append(theirs)
+            target = out.at[:, :, first : first + width]
+            mine = [
+                pltpu.make_async_copy(source.at[rows, cols], target.at[j], sems.at[i, j, p])
+                for j, source in enumerate((key, value))
+            ]
+            theirs = [
+                pltpu.make_async_copy(part.at[j, rows, :], target.at[j], sems.at[i, j, p])
+                for j in range(2)
+            ]
+            waits += theirs
+
+            @pl.when(own)
+            def from_own(copies=mine):
+                for copy in copies:
+                    copy.start()
+
+            @pl.when(jnp.logical_not(own))
+            def from_received(copies=theirs):
+                for copy in copies:
+                    copy.start()
+
             first += width
     for copy in waits:
         copy.wait()
@@ -100,7 +127,7 @@
     )(chosen, where, here, key, value, *received)
 
 
-def attend_kernel(allowed, where, q_own, q_rec, k_own, v_own, kv_rec, rim_a, rim_b, *rest):
+def attend_kernel(where, allowed, q_own, q_rec, k_own, v_own, kv_rec, rim_a, rim_b, *rest):
     far, (o_own, o_send, keys, values, scores, tops) = rest[:-6], rest[-6:]
     rows = q_own.shape[0]
     tiles = rows // TILE
@@ -177,29 +204,30 @@
     queries, q_rec, key, value, kv_rec, rim_a, rim_b, far = arrays
     rows = queries.shape[0]
     slots = allowed.shape[1]
-    own = pl.BlockSpec((rows, HD), lambda i, a, w: (0, w[0] * heads_here + low + i))
-    flat = pl.BlockSpec((rows, HD), lambda i, a, w: (0, low + i))
-    whole = pl.BlockSpec((2, rows, HD), lambda i, a, w: (0, 0, low + i))
-    part = pl.BlockSpec((2, rows, HD), lambda i, a, w: (0, 0, low - chunk_low + i))
+    own = pl.BlockSpec((rows, HD), lambda i, w: (0, w[0] * heads_here + low + i))
+    flat = pl.BlockSpec((rows, HD), lambda i, w: (0, low + i))
+    whole = pl.BlockSpec((2, rows, HD), lambda i, w: (0, 0, low + i))
+    part = pl.BlockSpec((2, rows, HD), lambda i, w: (0, 0, low - chunk_low + i))
     tiles = [
-        pl.BlockSpec((2, TILE, HD), lambda i, a, w, start=low - far_low: (0, 0, start + i))
+        pl.BlockSpec((2, TILE, HD), lambda i, w, start=low - far_low: (0, 0, start + i))
         for far_low in far_lows
     ]
-    out = pl.BlockSpec((rows, HD), lambda i, a, w: (0, i))
+    out = pl.BlockSpec((rows, HD), lambda i, w: (0, i))
     shape = jax.ShapeDtypeStruct((rows, (high - low) * HD), queries.dtype)
-    inputs = [queries, q_rec, key, value, kv_rec, rim_a, rim_b, *far]
-    specs = [own, flat, own, own, part, whole, part] + tiles
+    inputs = [allowed, queries, q_rec, key, value, kv_rec, rim_a, rim_b, *far]
+    specs = [pl.BlockSpec(memory_space=pltpu.SMEM)]
+    specs += [own, flat, own, own, part, whole, part] + tiles
     aliases = {}
     kernel = attend_kernel
     if result is not None:
-        kernel = functools.partial(skip_operand, attend_kernel, 2 + len(inputs))
-        aliases = {2 + len(inputs): 0}
+        kernel = functools.partial(skip_operand, attend_kernel, 1 + len(inputs))
+        aliases = {1 + len(inputs): 0}
         inputs, specs = inputs + [result], specs + [anywhere]
     return pl.pallas_call(
         kernel,
         out_shape=[jax.ShapeDtypeStruct(queries.shape, queries.dtype), shape],
         grid_spec=pltpu.PrefetchScalarGridSpec(
-            num_scalar_prefetch=2,
+            num_scalar_prefetch=1,
             grid=(high - low,),
             in_specs=specs,
             out_specs=[own, out],
@@ -211,7 +239,7 @@
             ],
         ),
         input_output_aliases=aliases,
-    )(allowed, where, *inputs)
+    )(where, *inputs)
 
 
 def skip_operand(kernel, index, *refs):
@@ -259,9 +287,9 @@
     half = tok_rows // TILE
     slab_tiles = 2 * half
 
-    shifts = [(0, slabs // 2)]
+    shifts = [(slabs // 2, True)]
     for level in range(2, FAR + 1):
-        shifts += [(1, slabs // 2**level), (-1, slabs // 2**level)]
+        shifts += [(slabs // 2**level, True), (slabs // 2**level, False)]
     live = jnp.arange(key_tiles.shape[1], dtype=jnp.int32)[None, :] < tile_count[:, None]
     turned = (key_tiles % slab_tiles + half * side) % slab_tiles
     mine = jnp.where(live & (key_tiles // slab_tiles == slab), turned, 0)
@@ -276,9 +304,8 @@
     slots = (within + half * side) % slab_tiles
     slots = jnp.where(offset == -1, 2 * half + half * (1 - side) + within - half, slots)
     slots = jnp.where(offset == 1, 2 * half + half * side + within, slots)
-    for i, (direction, far) in enumerate(shifts):
-        hit = (jnp.abs(offset) == far) if direction == 0 else (offset == -direction * far)
-        slots = jnp.where(hit, 4 * half + i, slots)
+    for i, shift in enumerate(shifts):
+        slots = jnp.where(listed // slab_tiles == across_from(slab, *shift), 4 * half + i, slots)
     alive = jnp.arange(listed.shape[1], dtype=jnp.int32)[None, :] < counts[:, None]
     slots = jnp.where(alive, slots, -1)
     slot_ids = jnp.arange(4 * half + len(shifts), dtype=jnp.int32)
@@ -289,10 +316,9 @@
 
     def outward(direction):
         return [
-            (g * slabs + s, g * slabs + s + step)
+            (g * slabs + s, g * slabs + (s + step) % slabs)
             for g, step in ((0, -direction), (1, direction))
             for s in range(slabs)
-            if 0 <= s + step < slabs
         ]
 
     kv_rec = []
@@ -330,19 +356,13 @@
             [kv_rec[m] for m in used],
             [lows[m] for m in used],
             [
-                ((shifts[i][0] or 1) * shifts[i][1], tuple(used.index(m) for m in members))
+                (shifts[i], tuple(used.index(m) for m in members))
                 for i, members in jobs
             ],
             half,
         )
         for (i, members), tile in zip(jobs, tiles):
-            direction, distance = shifts[i]
-            if direction == 0:
-                pairs = [(s, (s + distance) % slabs) for s in range(slabs)]
-            else:
-                step = direction * distance
-                pairs = [(s, s + step) for s in range(slabs) if 0 <= s + step < slabs]
-            arrived = lax.ppermute(tile, "blk", pairs)
+            arrived = lax.ppermute(tile, "blk", exchange(slabs, *shifts[i]))
             for m in members:
                 far[m][i] = (chunks[members[0]][0], arrived)
     result, returned = None, []
@@ -369,7 +389,8 @@
 
 
 def head_runs(heads):
-    return [(c, low, high) for c, (low, high) in enumerate(chunk_bounds(heads))]
+    first, second, (low, high) = chunk_bounds(heads)
+    return [(0, *first), (1, *second), (2, low, high - 1), (2, high - 1, high)]
 
 
 def solution(mesh):

time: 187 us -> 168 us (0.90)
  starting transfers between devices: 72.4 us -> 32.9 us
  waiting for transfers between devices: 54.4 us -> 74.5 us
    ppermute x15, starting transfers between devices: 51.7 us -> 24.3 us  [on_device(): arrived = lax.ppermute(tile, 'blk', exchange(slabs, *shifts[i]))]
    ppermute x15, waiting for transfers between devices: 19.7 us -> 41 us  [on_device(): arrived = lax.ppermute(tile, 'blk', exchange(slabs, *shifts[i]))]
    ppermute x3, starting transfers between devices: 12.5 us -> 0.15 us  [on_device(): rim_b.append(lax.ppermute(kv_rec[c], ('head', 'blk'), outward(-1)))]
    ppermute x3 -> x4, waiting for transfers between devices: 8.49 us -> 5.36 us  [on_device(): returned.append((a, lax.ppermute(sent, 'head', swap)))]
    ppermute x3 -> x4, starting transfers between devices: 2.21 us -> 4.24 us  [on_device(): returned.append((a, lax.ppermute(sent, 'head', swap)))]
    unnamed x38 -> x42, local copies, waits for them, and re-layouts: 3.69 us -> 4.93 us
    pallas_call x3 -> x4, Pallas kernels: 34.8 us -> 34.6 us  [attend(): pl.pallas_call(kernel, out_shape=[jax.ShapeDtypeStruct(queries.shape, que...]
  transfers between devices with their start and end apart: 26 -> 27, of which waited for: 10 -> 11; matrix products, arithmetic and copies ran while one was open for 4% -> 4% of each run, Pallas kernels for 24% -> 27%
where the time goes in v3:
time: 168 us; the launch traced here: 167 us
  waiting for transfers between devices  74.5 us (44%)
  Pallas kernels  46.4 us (28%)
  starting transfers between devices  32.9 us (20%)
  other arithmetic  7.17 us (4%)
  local copies, waits for them, and re-layouts  5.17 us (3%)
    ppermute x15, waiting for transfers between devices, on_device(): arrived = lax.ppermute(tile, 'blk', exchange(slabs, *shifts[i]))  41 us
    pallas_call x4, Pallas kernels, attend(): pl.pallas_call(kernel, out_shape=[jax.ShapeDtypeStruct(queries.shape, que...  34.6 us
    ppermute x3, waiting for transfers between devices, on_device(): kv_rec.append(lax.ppermute(packed, 'head', swap))  28.1 us
    ppermute x15, starting transfers between devices, on_device(): arrived = lax.ppermute(tile, 'blk', exchange(slabs, *shifts[i]))  24.3 us
    pallas_call x3, Pallas kernels, select_distant(): pl.pallas_call(functools.partial(distant_kernel, half, jobs, lows), out_s...  7.7 us
    ppermute x4, waiting for transfers between devices, on_device(): returned.append((a, lax.ppermute(sent, 'head', swap)))  5.36 us
    unnamed x42, local copies, waits for them, and re-layouts  4.93 us
    another operation x4, other arithmetic, on_device(): jnp.stack([columns_of(array, 1 - side, low * HD, width) for array in (key...  4.63 us
  transfers between devices with their start and end apart: 27, of which 11 were waited for; matrix products, arithmetic and copies ran while one was open for 4% of the time, Pallas kernels for 27%

profile of v3, /device:TPU:12, one launch (start us, length us, event | category | flops | bytes accessed | tf_op | source)
XLA Modules:
  0.0 166.5 jit_solution(15935649116738479843)
XLA Ops:
  0.0 1.1 shard_map.58
  1.1 1.6 collective-permute-start.16
  2.6 1.5 shard_map.55
  4.2 1.4 select_bitcast_fusion
  5.7 1.0 pad_maximum_fusion
  7.2 1.3 select_bitcast_fusion.2
  8.5 0.9 pad_maximum_fusion.1
  9.4 1.5 collective-permute-start.1
  10.9 1.0 slice_select_fusion
  12.6 0.7 reduce_max.28.chosen
  13.3 4.1 %collective-permute-done.16.rest_0_.kv_rec = bf16[2,384,384]{2,1,0:T(8,128)(2,1)} collective-permute-done((bf16[2,384,384]{2,1,0:T(8,128)(2,1)S(1)}, bf16[2,384,384]{2,1,0:T(8,128)(2,1)}, u32[]{:S(2)}, u32[]{:S(2)}) %collective-permute-start.16) | collective-permute-done | bytes 589856 | tf_op jit(solution)/shard_map/ppermute | solution.py:334
  17.4 2.8 %shard_map.59 = (bf16[2,128,384]{2,1,0:T(8,128)(2,1)S(1)}, bf16[2,128,384]{2,1,0:T(8,128)(2,1)S(1)}, bf16[2,128,384]{2,1,0:T(8,128)(2,1)S(1)}, bf16[2,128,384]{2,1,0:T(8,128)(2,1)}, bf16[2,128,384]{2,1,0:T(8,128)(2,1)}) custom-call(s32[16]{0:T(128)} %reduce_max.28.chosen, s32[1]{0:T(128)} %bitcast.where.refs_0_, s32[1]{0:T(128)} %bitcast.3.here, ...), custom_call_target="tpu_custom_call" | custom-call | tf_op jit(solution)/shard_map/pallas_call | solution.py:117
  20.3 2.7 %collective-permute-start.18 = (bf16[2,128,384]{2,1,0:T(8,128)(2,1)S(1)}, bf16[2,128,384]{2,1,0:T(8,128)(2,1)S(1)}, u32[]{:S(2)}, u32[]{:S(2)}) collective-permute-start(bf16[2,128,384]{2,1,0:T(8,128)(2,1)S(1)} %get-tuple-element.38), channel_id=1, source_target_pairs={{0,8},{1,9},{2,10},{3,11},{4,12},{5,13},{6,14},{7,15},{8,0},{9,1},... | collective-permute-start | bytes 589832 | tf_op jit(solution)/shard_map/ppermute | solution.py:365
  22.9 23.9 %collective-permute-done.1.rest_0_.refs_6_ = bf16[2,384,384]{2,1,0:T(8,128)(2,1)S(1)} collective-permute-done((bf16[2,384,384]{2,1,0:T(8,128)(2,1)}, bf16[2,384,384]{2,1,0:T(8,128)(2,1)S(1)}, u32[]{:S(2)}, u32[]{:S(2)}) %collective-permute-start.1) | collective-permute-done | bytes 589856 | tf_op jit(solution)/shard_map/ppermute | solution.py:334
  47.3 2.7 %collective-permute-start.20 = (bf16[2,128,384]{2,1,0:T(8,128)(2,1)S(1)}, bf16[2,128,384]{2,1,0:T(8,128)(2,1)S(1)}, u32[]{:S(2)}, u32[]{:S(2)}) collective-permute-start(bf16[2,128,384]{2,1,0:T(8,128)(2,1)S(1)} %get-tuple-element.40), channel_id=1, source_target_pairs={{0,1},{1,0},{2,3},{3,2},{4,8},{5,9},{6,10},{7,11},{8,4},{9,5},{10,... | collective-permute-start | bytes 589832 | tf_op jit(solution)/shard_map/ppermute | solution.py:365
  50.0 2.5 %collective-permute-done.19.rest_1_ = bf16[2,128,384]{2,1,0:T(8,128)(2,1)S(1)} collective-permute-done((bf16[2,128,384]{2,1,0:T(8,128)(2,1)S(1)}, bf16[2,128,384]{2,1,0:T(8,128)(2,1)S(1)}, u32[]{:S(2)}, u32[]{:S(2)}) %collective-permute-start.19) | collective-permute-done | bytes 196640 | tf_op jit(solution)/shard_map/ppermute | solution.py:365
  53.0 0.6 collective-permute-done.20.rest_2_
  53.7 0.7 copy-done.17
  54.3 2.0 %collective-permute-start.22 = (bf16[2,128,384]{2,1,0:T(8,128)(2,1)}, bf16[2,128,384]{2,1,0:T(8,128)(2,1)}, u32[]{:S(2)}, u32[]{:S(2)}) collective-permute-start(bf16[2,128,384]{2,1,0:T(8,128)(2,1)} %get-tuple-element.42), channel_id=1, source_target_pairs={{0,1},{1,0},{2,4},{3,5},{4,2},{5,3},{6,8},{7,9},{8,6},{9,7},{10,12... | collective-permute-start | bytes 589832 | tf_op jit(solution)/shard_map/ppermute | solution.py:365
  56.3 2.8 %shard_map.56 = (bf16[2,128,384]{2,1,0:T(8,128)(2,1)}, bf16[2,128,384]{2,1,0:T(8,128)(2,1)S(1)}, bf16[2,128,384]{2,1,0:T(8,128)(2,1)S(1)}, bf16[2,128,384]{2,1,0:T(8,128)(2,1)S(1)}, bf16[2,128,384]{2,1,0:T(8,128)(2,1)S(1)}) custom-call(s32[16]{0:T(128)} %reduce_max.28.chosen, s32[1]{0:T(128)} %bitcast.where.refs_0_, s32[1]{0:T(128)} %bitcast.3.here, ...), custom_call_target="tpu_custom_call" | custom-call | tf_op jit(solution)/shard_map/pallas_call | solution.py:117
  59.1 0.7 copy-done
  59.7 0.7 copy-done.1
  60.4 0.7 copy-done.2
  61.1 2.1 %shard_map.57 = (bf16[2,128,512]{2,1,0:T(8,128)(2,1)S(1)}, bf16[2,128,512]{2,1,0:T(8,128)(2,1)S(1)}, bf16[2,128,512]{2,1,0:T(8,128)(2,1)S(1)}, bf16[2,128,512]{2,1,0:T(8,128)(2,1)S(1)}, bf16[2,128,512]{2,1,0:T(8,128)(2,1)S(1)}) custom-call(s32[16]{0:T(128)} %reduce_max.28.chosen, s32[1]{0:T(128)} %bitcast.where.refs_0_, s32[1]{0:T(128)} %bitcast.3.here, ...), custom_call_target="tpu_custom_call" | custom-call | tf_op jit(solution)/shard_map/pallas_call | solution.py:117
  63.3 3.0 %collective-permute-start.11 = (bf16[2,128,512]{2,1,0:T(8,128)(2,1)S(1)}, bf16[2,128,512]{2,1,0:T(8,128)(2,1)S(1)}, u32[]{:S(2)}, u32[]{:S(2)}) collective-permute-start(bf16[2,128,512]{2,1,0:T(8,128)(2,1)S(1)} %get-tuple-element.33), channel_id=1, source_target_pairs={{0,8},{1,9},{2,10},{3,11},{4,12},{5,13},{6,14},{7,15},{8,0},{9,1},... | collective-permute-start | bytes 786440 | tf_op jit(solution)/shard_map/ppermute | solution.py:365
  66.7 8.0 %collective-permute-done.4.refs_9_ = bf16[2,128,384]{2,1,0:T(8,128)(2,1)} collective-permute-done((bf16[2,128,384]{2,1,0:T(8,128)(2,1)}, bf16[2,128,384]{2,1,0:T(8,128)(2,1)}, u32[]{:S(2)}, u32[]{:S(2)}) %collective-permute-start.4) | collective-permute-done | bytes 196640 | tf_op jit(solution)/shard_map/ppermute | solution.py:365
  74.7 1.7 %collective-permute-start.13 = (bf16[2,128,512]{2,1,0:T(8,128)(2,1)S(1)}, bf16[2,128,512]{2,1,0:T(8,128)(2,1)S(1)}, u32[]{:S(2)}, u32[]{:S(2)}) collective-permute-start(bf16[2,128,512]{2,1,0:T(8,128)(2,1)S(1)} %get-tuple-element.35), channel_id=1, source_target_pairs={{0,1},{1,0},{2,3},{3,2},{4,8},{5,9},{6,10},{7,11},{8,4},{9,5},{10,... | collective-permute-start | bytes 786440 | tf_op jit(solution)/shard_map/ppermute | solution.py:365
  76.4 3.8 %collective-permute-done.11.refs_9_ = bf16[2,128,512]{2,1,0:T(8,128)(2,1)S(1)} collective-permute-done((bf16[2,128,512]{2,1,0:T(8,128)(2,1)S(1)}, bf16[2,128,512]{2,1,0:T(8,128)(2,1)S(1)}, u32[]{:S(2)}, u32[]{:S(2)}) %collective-permute-start.11) | collective-permute-done | bytes 262176 | tf_op jit(solution)/shard_map/ppermute | solution.py:365
  80.3 2.4 %collective-permute-start.14 = (bf16[2,128,512]{2,1,0:T(8,128)(2,1)S(1)}, bf16[2,128,512]{2,1,0:T(8,128)(2,1)S(1)}, u32[]{:S(2)}, u32[]{:S(2)}) collective-permute-start(bf16[2,128,512]{2,1,0:T(8,128)(2,1)S(1)} %get-tuple-element.36), channel_id=1, source_target_pairs={{0,2},{1,3},{2,0},{3,1},{4,6},{5,7},{6,4},{7,5},{8,10},{9,11},{10,... | collective-permute-start | bytes 786440 | tf_op jit(solution)/shard_map/ppermute | solution.py:365
  82.6 16.9 %collective-permute-done.13.refs_11_ = bf16[2,128,512]{2,1,0:T(8,128)(2,1)S(1)} collective-permute-done((bf16[2,128,512]{2,1,0:T(8,128)(2,1)S(1)}, bf16[2,128,512]{2,1,0:T(8,128)(2,1)S(1)}, u32[]{:S(2)}, u32[]{:S(2)}) %collective-permute-start.13) | collective-permute-done | bytes 262176 | tf_op jit(solution)/shard_map/ppermute | solution.py:365
  99.5 5.1 %collective-permute-done.14.refs_12_ = bf16[2,128,512]{2,1,0:T(8,128)(2,1)S(1)} collective-permute-done((bf16[2,128,512]{2,1,0:T(8,128)(2,1)S(1)}, bf16[2,128,512]{2,1,0:T(8,128)(2,1)S(1)}, u32[]{:S(2)}, u32[]{:S(2)}) %collective-permute-start.14) | collective-permute-done | bytes 262176 | tf_op jit(solution)/shard_map/ppermute | solution.py:365
  104.6 0.7 copy-done.13
  105.5 4.1 %collective-permute-done.15.refs_13_ = bf16[2,128,512]{2,1,0:T(8,128)(2,1)S(1)} collective-permute-done((bf16[2,128,512]{2,1,0:T(8,128)(2,1)S(1)}, bf16[2,128,512]{2,1,0:T(8,128)(2,1)S(1)}, u32[]{:S(2)}, u32[]{:S(2)}) %collective-permute-start.15) | collective-permute-done | bytes 262176 | tf_op jit(solution)/shard_map/ppermute | solution.py:365
  110.3 6.4 %collective-permute-start.6 = (bf16[2,128,384]{2,1,0:T(8,128)(2,1)}, bf16[2,128,384]{2,1,0:T(8,128)(2,1)S(1)}, u32[]{:S(2)}, u32[]{:S(2)}) collective-permute-start(bf16[2,128,384]{2,1,0:T(8,128)(2,1)} %copy-done.1), channel_id=1, source_target_pairs={{0,1},{1,0},{2,3},{3,2},{4,8},{5,9},{6,10},{7,11},{8,4},{9,5},{10,... | collective-permute-start | bytes 589832 | tf_op jit(solution)/shard_map/ppermute | solution.py:365
  116.7 2.2 %collective-permute-start.7 = (bf16[2,128,384]{2,1,0:T(8,128)(2,1)}, bf16[2,128,384]{2,1,0:T(8,128)(2,1)S(1)}, u32[]{:S(2)}, u32[]{:S(2)}) collective-permute-start(bf16[2,128,384]{2,1,0:T(8,128)(2,1)} %copy-done), channel_id=1, source_target_pairs={{0,2},{1,3},{2,0},{3,1},{4,6},{5,7},{6,4},{7,5},{8,10},{9,11},{10,... | collective-permute-start | bytes 589832 | tf_op jit(solution)/shard_map/ppermute | solution.py:365
  118.9 0.7 convert_reduce_fusion.allowed.refs_1_
  119.6 10.0 %shard_map.60 = (bf16[384,2560]{1,0:T(8,128)(2,1)}, bf16[384,384]{1,0:T(8,128)(2,1)}) custom-call(s32[1]{0:T(128)} %bitcast.where.refs_0_, s32[6,17]{1,0:T(8,128)} %convert_reduce_fusion.allowed.refs_1_, bf16[384,2560]{1,0:T(8,128)(2,1)} %refs_2_.5, bf16[384,1280]{1,0:T(8,128)(2,1)} %collective-permute-done.q_rec.refs_3_, bf16[384,2560]{1,0:T(8,128)(2,1)} %refs_4_.5, ...), custom_call_target="tpu_custom_call" | custom-call | tf_op jit(solution)/shard_map/pallas_call | solution.py:226
  129.6 12.7 %shard_map.61 = (bf16[384,2560]{1,0:T(8,128)(2,1)}, bf16[384,512]{1,0:T(8,128)(2,1)}) custom-call(s32[1]{0:T(128)} %bitcast.where.refs_0_, s32[6,17]{1,0:T(8,128)} %convert_reduce_fusion.allowed.refs_1_, bf16[384,2560]{1,0:T(8,128)(2,1)} %refs_2_.5, bf16[384,1280]{1,0:T(8,128)(2,1)} %collective-permute-done.q_rec.refs_3_, ...), custom_call_target="tpu_custom_call", output_to_operand_aliasing={{0}: (14, {})} | custom-call | tf_op jit(solution)/shard_map/pallas_call | solution.py:226
  142.3 0.9 collective-permute-start.25
  143.2 1.2 collective-permute-start.24
  144.6 0.6 copy-done.8
  145.4 7.3 %shard_map.62 = (bf16[384,2560]{1,0:T(8,128)(2,1)}, bf16[384,256]{1,0:T(8,128)(2,1)}) custom-call(s32[1]{0:T(128)} %bitcast.where.refs_0_, s32[6,17]{1,0:T(8,128)} %convert_reduce_fusion.allowed.refs_1_, bf16[384,2560]{1,0:T(8,128)(2,1)} %refs_2_.5, bf16[384,1280]{1,0:T(8,128)(2,1)} %collective-permute-done.q_rec.refs_3_, ...), custom_call_target="tpu_custom_call", output_to_operand_aliasing={{0}: (14, {})} | custom-call | tf_op jit(solution)/shard_map/pallas_call | solution.py:226
  152.7 0.9 collective-permute-start.26
  153.6 4.6 %shard_map.63 = (bf16[384,2560]{1,0:T(8,128)(2,1)}, bf16[384,128]{1,0:T(8,128)(2,1)}) custom-call(s32[1]{0:T(128)} %bitcast.where.refs_0_, s32[6,17]{1,0:T(8,128)} %convert_reduce_fusion.allowed.refs_1_, bf16[384,2560]{1,0:T(8,128)(2,1)} %refs_2_.5, bf16[384,1280]{1,0:T(8,128)(2,1)} %collective-permute-done.q_rec.refs_3_, ...), custom_call_target="tpu_custom_call", output_to_operand_aliasing={{0}: (14, {})} | custom-call | tf_op jit(solution)/shard_map/pallas_call | solution.py:226
  158.2 1.2 collective-permute-start.23
  159.4 5.2 %collective-permute-done.26.refs_2_ = bf16[384,256]{1,0:T(8,128)(2,1)S(1)} collective-permute-done((bf16[384,256]{1,0:T(8,128)(2,1)}, bf16[384,256]{1,0:T(8,128)(2,1)S(1)}, u32[]{:S(2)}, u32[]{:S(2)}) %collective-permute-start.26) | collective-permute-done | bytes 196640 | tf_op jit(solution)/shard_map/ppermute | solution.py:375
  164.7 0.9 shard_map.64.refs_1_
  165.7 0.6 shard_map.65
  (71 shorter events, 4.0 us)
Async XLA Ops:
  1.1 16.4 %collective-permute-start.16 = (bf16[2,384,384]{2,1,0:T(8,128)(2,1)S(1)}, bf16[2,384,384]{2,1,0:T(8,128)(2,1)}, u32[]{:S(2)}, u32[]{:S(2)}) collective-permute-start(bf16[2,384,384]{2,1,0:T(8,128)(2,1)S(1)} %shard_map.58), channel_id=1, source_target_pairs={{0,16},{16,0},{1,17},{17,1},{2,18},{18,2},{3,19},{19,3},{4,20},{20... | collective-permute-start | bytes 1769480 | tf_op jit(solution)/shard_map/ppermute | solution.py:334
  4.2 114.8 %collective-permute-start.2 = (bf16[2,384,1280]{2,1,0:T(8,128)(2,1)S(1)}, bf16[2,384,1280]{2,1,0:T(8,128)(2,1)}, u32[]{:S(2)}, u32[]{:S(2)}) collective-permute-start(bf16[2,384,1280]{2,1,0:T(8,128)(2,1)S(1)} %shard_map.55), channel_id=1, source_target_pairs={{0,15},{1,0},{2,1},{3,2},{4,3},{5,4},{6,5},{7,6},{8,7},{9,8},{10,9... | collective-permute-start | bytes 5898248 | tf_op jit(solution)/shard_map/ppermute | solution.py:336
  5.7 5.3 %copy-start.3 = (bf16[384,2560]{1,0:T(8,128)(2,1)S(1)}, bf16[384,2560]{1,0:T(8,128)(2,1)}, u32[]{:S(2)}) copy-start(bf16[384,2560]{1,0:T(8,128)(2,1)} %refs_2_.5) | copy-start | bytes 5898244
  6.7 54.5 %collective-permute-start.9 = (bf16[2,384,512]{2,1,0:T(8,128)(2,1)}, bf16[2,384,512]{2,1,0:T(8,128)(2,1)}, u32[]{:S(2)}, u32[]{:S(2)}) collective-permute-start(bf16[2,384,512]{2,1,0:T(8,128)(2,1)} %pad_maximum_fusion), channel_id=1, source_target_pairs={{0,16},{16,0},{1,17},{17,1},{2,18},{18,2},{3,19},{19,3},{4,20},{20... | collective-permute-start | bytes 2359304 | tf_op jit(solution)/shard_map/ppermute | solution.py:334
  8.5 4.0 %copy-start.18 = (s32[96,16]{0,1:T(8,128)S(1)}, s32[96,16]{0,1:T(8,128)}, u32[]{:S(2)}) copy-start(s32[96,16]{0,1:T(8,128)} %param.8) | copy-start | bytes 18436
  8.5 4.0 %copy-start.19 = (s32[96]{0:T(128)S(1)}, s32[96]{0:T(128)}, u32[]{:S(2)}) copy-start(s32[96]{0:T(128)} %param.9) | copy-start | bytes 1156
  9.4 37.4 %collective-permute-start.1 = (bf16[2,384,384]{2,1,0:T(8,128)(2,1)}, bf16[2,384,384]{2,1,0:T(8,128)(2,1)S(1)}, u32[]{:S(2)}, u32[]{:S(2)}) collective-permute-start(bf16[2,384,384]{2,1,0:T(8,128)(2,1)} %pad_maximum_fusion.1), channel_id=1, source_target_pairs={{0,16},{16,0},{1,17},{17,1},{2,18},{18,2},{3,19},{19,3},{4,20},{20... | collective-permute-start | bytes 1769480 | tf_op jit(solution)/shard_map/ppermute | solution.py:334
  12.0 62.7 %collective-permute-start = (bf16[384,1280]{1,0:T(8,128)(2,1)}, bf16[384,1280]{1,0:T(8,128)(2,1)}, u32[]{:S(2)}, u32[]{:S(2)}) collective-permute-start(bf16[384,1280]{1,0:T(8,128)(2,1)} %slice_select_fusion), channel_id=1, source_target_pairs={{0,16},{16,0},{1,17},{17,1},{2,18},{18,2},{3,19},{19,3},{4,20},{20... | collective-permute-start | bytes 2949128 | tf_op jit(solution)/shard_map/ppermute | solution.py:341
  20.3 27.0 %collective-permute-start.18 = (bf16[2,128,384]{2,1,0:T(8,128)(2,1)S(1)}, bf16[2,128,384]{2,1,0:T(8,128)(2,1)S(1)}, u32[]{:S(2)}, u32[]{:S(2)}) collective-permute-start(bf16[2,128,384]{2,1,0:T(8,128)(2,1)S(1)} %get-tuple-element.38), channel_id=1, source_target_pairs={{0,8},{1,9},{2,10},{3,11},{4,12},{5,13},{6,14},{7,15},{8,0},{9,1},... | collective-permute-start | bytes 589832 | tf_op jit(solution)/shard_map/ppermute | solution.py:365
  46.8 9.4 %copy-start.4 = (bf16[2,384,384]{2,1,0:T(8,128)(2,1)}, bf16[2,384,384]{2,1,0:T(8,128)(2,1)S(1)}, u32[]{:S(2)}) copy-start(bf16[2,384,384]{2,1,0:T(8,128)(2,1)S(1)} %collective-permute-done.1.rest_0_.refs_6_) | copy-start | bytes 1769476
  46.8 5.7 %collective-permute-start.19 = (bf16[2,128,384]{2,1,0:T(8,128)(2,1)S(1)}, bf16[2,128,384]{2,1,0:T(8,128)(2,1)S(1)}, u32[]{:S(2)}, u32[]{:S(2)}) collective-permute-start(bf16[2,128,384]{2,1,0:T(8,128)(2,1)S(1)} %get-tuple-element.39), channel_id=1, source_target_pairs={{0,4},{1,5},{2,6},{3,7},{4,0},{5,1},{6,2},{7,3},{8,12},{9,13},{10,... | collective-permute-start | bytes 589832 | tf_op jit(solution)/shard_map/ppermute | solution.py:365
  47.3 6.4 %copy-start.15 = (bf16[2,128,384]{2,1,0:T(8,128)(2,1)}, bf16[2,128,384]{2,1,0:T(8,128)(2,1)S(1)}, u32[]{:S(2)}) copy-start(bf16[2,128,384]{2,1,0:T(8,128)(2,1)S(1)} %collective-permute-done.18.rest_0_) | copy-start | bytes 589828
  47.3 6.4 %collective-permute-start.20 = (bf16[2,128,384]{2,1,0:T(8,128)(2,1)S(1)}, bf16[2,128,384]{2,1,0:T(8,128)(2,1)S(1)}, u32[]{:S(2)}, u32[]{:S(2)}) collective-permute-start(bf16[2,128,384]{2,1,0:T(8,128)(2,1)S(1)} %get-tuple-element.40), channel_id=1, source_target_pairs={{0,1},{1,0},{2,3},{3,2},{4,8},{5,9},{6,10},{7,11},{8,4},{9,5},{10,... | collective-permute-start | bytes 589832 | tf_op jit(solution)/shard_map/ppermute | solution.py:365
  52.5 1.1 copy-start.16
  52.5 10.8 %collective-permute-start.21 = (bf16[2,128,384]{2,1,0:T(8,128)(2,1)}, bf16[2,128,384]{2,1,0:T(8,128)(2,1)}, u32[]{:S(2)}, u32[]{:S(2)}) collective-permute-start(bf16[2,128,384]{2,1,0:T(8,128)(2,1)} %get-tuple-element.41), channel_id=1, source_target_pairs={{0,2},{1,3},{2,0},{3,1},{4,6},{5,7},{6,4},{7,5},{8,10},{9,11},{10,... | collective-permute-start | bytes 589832 | tf_op jit(solution)/shard_map/ppermute | solution.py:365
  53.6 0.7 copy-start.17
  54.3 12.0 %collective-permute-start.22 = (bf16[2,128,384]{2,1,0:T(8,128)(2,1)}, bf16[2,128,384]{2,1,0:T(8,128)(2,1)}, u32[]{:S(2)}, u32[]{:S(2)}) collective-permute-start(bf16[2,128,384]{2,1,0:T(8,128)(2,1)} %get-tuple-element.42), channel_id=1, source_target_pairs={{0,1},{1,0},{2,4},{3,5},{4,2},{5,3},{6,8},{7,9},{8,6},{9,7},{10,12... | collective-permute-start | bytes 589832 | tf_op jit(solution)/shard_map/ppermute | solution.py:365
  59.0 0.7 copy-start
  59.7 0.7 copy-start.1
  60.4 0.7 copy-start.2
  61.1 13.5 %collective-permute-start.4 = (bf16[2,128,384]{2,1,0:T(8,128)(2,1)}, bf16[2,128,384]{2,1,0:T(8,128)(2,1)}, u32[]{:S(2)}, u32[]{:S(2)}) collective-permute-start(bf16[2,128,384]{2,1,0:T(8,128)(2,1)} %get-tuple-element.28), channel_id=1, source_target_pairs={{0,8},{1,9},{2,10},{3,11},{4,12},{5,13},{6,14},{7,15},{8,0},{9,1},... | collective-permute-start | bytes 589832 | tf_op jit(solution)/shard_map/ppermute | solution.py:365
  63.3 16.9 %collective-permute-start.11 = (bf16[2,128,512]{2,1,0:T(8,128)(2,1)S(1)}, bf16[2,128,512]{2,1,0:T(8,128)(2,1)S(1)}, u32[]{:S(2)}, u32[]{:S(2)}) collective-permute-start(bf16[2,128,512]{2,1,0:T(8,128)(2,1)S(1)} %get-tuple-element.33), channel_id=1, source_target_pairs={{0,8},{1,9},{2,10},{3,11},{4,12},{5,13},{6,14},{7,15},{8,0},{9,1},... | collective-permute-start | bytes 786440 | tf_op jit(solution)/shard_map/ppermute | solution.py:365
  66.3 14.0 %collective-permute-start.12 = (bf16[2,128,512]{2,1,0:T(8,128)(2,1)S(1)}, bf16[2,128,512]{2,1,0:T(8,128)(2,1)S(1)}, u32[]{:S(2)}, u32[]{:S(2)}) collective-permute-start(bf16[2,128,512]{2,1,0:T(8,128)(2,1)S(1)} %get-tuple-element.34), channel_id=1, source_target_pairs={{0,4},{1,5},{2,6},{3,7},{4,0},{5,1},{6,2},{7,3},{8,12},{9,13},{10,... | collective-permute-start | bytes 786440 | tf_op jit(solution)/shard_map/ppermute | solution.py:365
  74.6 42.1 %collective-permute-start.10 = (bf16[2,384,512]{2,1,0:T(8,128)(2,1)}, bf16[2,384,512]{2,1,0:T(8,128)(2,1)}, u32[]{:S(2)}, u32[]{:S(2)}) collective-permute-start(bf16[2,384,512]{2,1,0:T(8,128)(2,1)} %collective-permute-done.9.rest_0_.refs_6_), channel_id=1, source_target_pairs={{0,1},{1,2},{2,3},{3,4},{4,5},{5,6},{6,7},{7,8},{8,9},{9,10},{10,1... | collective-permute-start | bytes 2359304 | tf_op jit(solution)/shard_map/ppermute | solution.py:345
  74.7 24.8 %collective-permute-start.13 = (bf16[2,128,512]{2,1,0:T(8,128)(2,1)S(1)}, bf16[2,128,512]{2,1,0:T(8,128)(2,1)S(1)}, u32[]{:S(2)}, u32[]{:S(2)}) collective-permute-start(bf16[2,128,512]{2,1,0:T(8,128)(2,1)S(1)} %get-tuple-element.35), channel_id=1, source_target_pairs={{0,1},{1,0},{2,3},{3,2},{4,8},{5,9},{6,10},{7,11},{8,4},{9,5},{10,... | collective-permute-start | bytes 786440 | tf_op jit(solution)/shard_map/ppermute | solution.py:365
  80.2 24.5 %copy-start.10 = (bf16[2,128,512]{2,1,0:T(8,128)(2,1)}, bf16[2,128,512]{2,1,0:T(8,128)(2,1)S(1)}, u32[]{:S(2)}) copy-start(bf16[2,128,512]{2,1,0:T(8,128)(2,1)S(1)} %collective-permute-done.11.refs_9_) | copy-start | bytes 786436
  80.2 29.7 %collective-permute-start.17 = (bf16[2,384,384]{2,1,0:T(8,128)(2,1)}, bf16[2,384,384]{2,1,0:T(8,128)(2,1)}, u32[]{:S(2)}, u32[]{:S(2)}) collective-permute-start(bf16[2,384,384]{2,1,0:T(8,128)(2,1)} %collective-permute-done.16.rest_0_.kv_rec), channel_id=1, source_target_pairs={{0,1},{1,2},{2,3},{3,4},{4,5},{5,6},{6,7},{7,8},{8,9},{9,10},{10,1... | collective-permute-start | bytes 1769480 | tf_op jit(solution)/shard_map/ppermute | solution.py:345
  80.3 24.4 %copy-start.11 = (bf16[2,128,512]{2,1,0:T(8,128)(2,1)}, bf16[2,128,512]{2,1,0:T(8,128)(2,1)S(1)}, u32[]{:S(2)}) copy-start(bf16[2,128,512]{2,1,0:T(8,128)(2,1)S(1)} %collective-permute-done.12.refs_10_) | copy-start | bytes 786436
  80.3 24.4 %collective-permute-start.14 = (bf16[2,128,512]{2,1,0:T(8,128)(2,1)S(1)}, bf16[2,128,512]{2,1,0:T(8,128)(2,1)S(1)}, u32[]{:S(2)}, u32[]{:S(2)}) collective-permute-start(bf16[2,128,512]{2,1,0:T(8,128)(2,1)S(1)} %get-tuple-element.36), channel_id=1, source_target_pairs={{0,2},{1,3},{2,0},{3,1},{4,6},{5,7},{6,4},{7,5},{8,10},{9,11},{10,... | collective-permute-start | bytes 786440 | tf_op jit(solution)/shard_map/ppermute | solution.py:365
  99.5 5.2 %copy-start.12 = (bf16[2,128,512]{2,1,0:T(8,128)(2,1)}, bf16[2,128,512]{2,1,0:T(8,128)(2,1)S(1)}, u32[]{:S(2)}) copy-start(bf16[2,128,512]{2,1,0:T(8,128)(2,1)S(1)} %collective-permute-done.13.refs_11_) | copy-start | bytes 786436
  99.5 10.1 %collective-permute-start.15 = (bf16[2,128,512]{2,1,0:T(8,128)(2,1)S(1)}, bf16[2,128,512]{2,1,0:T(8,128)(2,1)S(1)}, u32[]{:S(2)}, u32[]{:S(2)}) collective-permute-start(bf16[2,128,512]{2,1,0:T(8,128)(2,1)S(1)} %get-tuple-element.37), channel_id=1, source_target_pairs={{0,1},{1,0},{2,4},{3,5},{4,2},{5,3},{6,8},{7,9},{8,6},{9,7},{10,12... | collective-permute-start | bytes 786440 | tf_op jit(solution)/shard_map/ppermute | solution.py:365
  104.6 0.7 copy-start.13
  105.4 39.1 %collective-permute-start.3 = (bf16[2,384,384]{2,1,0:T(8,128)(2,1)}, bf16[2,384,384]{2,1,0:T(8,128)(2,1)S(1)}, u32[]{:S(2)}, u32[]{:S(2)}) collective-permute-start(bf16[2,384,384]{2,1,0:T(8,128)(2,1)} %copy-done.4), channel_id=1, source_target_pairs={{0,1},{1,2},{2,3},{3,4},{4,5},{5,6},{6,7},{7,8},{8,9},{9,10},{10,1... | collective-permute-start | bytes 1769480 | tf_op jit(solution)/shard_map/ppermute | solution.py:345
  109.6 0.7 copy-start.14
  109.6 32.7 %collective-permute-start.5 = (bf16[2,128,384]{2,1,0:T(8,128)(2,1)}, bf16[2,128,384]{2,1,0:T(8,128)(2,1)S(1)}, u32[]{:S(2)}, u32[]{:S(2)}) collective-permute-start(bf16[2,128,384]{2,1,0:T(8,128)(2,1)} %copy-done.2), channel_id=1, source_target_pairs={{0,4},{1,5},{2,6},{3,7},{4,0},{5,1},{6,2},{7,3},{8,12},{9,13},{10,... | collective-permute-start | bytes 589832 | tf_op jit(solution)/shard_map/ppermute | solution.py:365
  110.3 32.9 %collective-permute-start.6 = (bf16[2,128,384]{2,1,0:T(8,128)(2,1)}, bf16[2,128,384]{2,1,0:T(8,128)(2,1)S(1)}, u32[]{:S(2)}, u32[]{:S(2)}) collective-permute-start(bf16[2,128,384]{2,1,0:T(8,128)(2,1)} %copy-done.1), channel_id=1, source_target_pairs={{0,1},{1,0},{2,3},{3,2},{4,8},{5,9},{6,10},{7,11},{8,4},{9,5},{10,... | collective-permute-start | bytes 589832 | tf_op jit(solution)/shard_map/ppermute | solution.py:365
  116.7 27.8 %collective-permute-start.7 = (bf16[2,128,384]{2,1,0:T(8,128)(2,1)}, bf16[2,128,384]{2,1,0:T(8,128)(2,1)S(1)}, u32[]{:S(2)}, u32[]{:S(2)}) collective-permute-start(bf16[2,128,384]{2,1,0:T(8,128)(2,1)} %copy-done), channel_id=1, source_target_pairs={{0,2},{1,3},{2,0},{3,1},{4,6},{5,7},{6,4},{7,5},{8,10},{9,11},{10,... | collective-permute-start | bytes 589832 | tf_op jit(solution)/shard_map/ppermute | solution.py:365
  118.9 25.6 %collective-permute-start.8 = (bf16[2,128,384]{2,1,0:T(8,128)(2,1)S(1)}, bf16[2,128,384]{2,1,0:T(8,128)(2,1)S(1)}, u32[]{:S(2)}, u32[]{:S(2)}) collective-permute-start(bf16[2,128,384]{2,1,0:T(8,128)(2,1)S(1)} %get-tuple-element.32), channel_id=1, source_target_pairs={{0,1},{1,0},{2,4},{3,5},{4,2},{5,3},{6,8},{7,9},{8,6},{9,7},{10,12... | collective-permute-start | bytes 589832 | tf_op jit(solution)/shard_map/ppermute | solution.py:365
  129.6 13.7 %copy-start.20 = (bf16[384,384]{1,0:T(8,128)(2,1)S(1)}, bf16[384,384]{1,0:T(8,128)(2,1)}, u32[]{:S(2)}) copy-start(bf16[384,384]{1,0:T(8,128)(2,1)} %get-tuple-element.47) | copy-start | bytes 884740
  142.3 2.2 %copy-start.6 = (bf16[2,128,384]{2,1,0:T(8,128)(2,1)}, bf16[2,128,384]{2,1,0:T(8,128)(2,1)S(1)}, u32[]{:S(2)}) copy-start(bf16[2,128,384]{2,1,0:T(8,128)(2,1)S(1)} %collective-permute-done.5.refs_10_) | copy-start | bytes 589828
  142.3 22.3 %collective-permute-start.25 = (bf16[384,512]{1,0:T(8,128)(2,1)}, bf16[384,512]{1,0:T(8,128)(2,1)S(1)}, u32[]{:S(2)}, u32[]{:S(2)}) collective-permute-start(bf16[384,512]{1,0:T(8,128)(2,1)} %get-tuple-element.48), channel_id=1, source_target_pairs={{0,16},{16,0},{1,17},{17,1},{2,18},{18,2},{3,19},{19,3},{4,20},{20... | collective-permute-start | bytes 1179656 | tf_op jit(solution)/shard_map/ppermute | solution.py:375
  143.2 1.3 copy-start.7
  143.2 21.4 %collective-permute-start.24 = (bf16[384,384]{1,0:T(8,128)(2,1)S(1)}, bf16[384,384]{1,0:T(8,128)(2,1)S(1)}, u32[]{:S(2)}, u32[]{:S(2)}) collective-permute-start(bf16[384,384]{1,0:T(8,128)(2,1)S(1)} %copy-done.20), channel_id=1, source_target_pairs={{0,16},{16,0},{1,17},{17,1},{2,18},{18,2},{3,19},{19,3},{4,20},{20... | collective-permute-start | bytes 884744 | tf_op jit(solution)/shard_map/ppermute | solution.py:375
  144.5 0.7 copy-start.8
  144.5 0.7 copy-start.9
  144.5 0.9 copy-start.5
  152.7 11.9 %collective-permute-start.26 = (bf16[384,256]{1,0:T(8,128)(2,1)}, bf16[384,256]{1,0:T(8,128)(2,1)S(1)}, u32[]{:S(2)}, u32[]{:S(2)}) collective-permute-start(bf16[384,256]{1,0:T(8,128)(2,1)} %get-tuple-element.49), channel_id=1, source_target_pairs={{0,16},{16,0},{1,17},{17,1},{2,18},{18,2},{3,19},{19,3},{4,20},{20... | collective-permute-start | bytes 589832 | tf_op jit(solution)/shard_map/ppermute | solution.py:375
  158.2 7.5 %collective-permute-start.23 = (bf16[384,128]{1,0:T(8,128)(2,1)}, bf16[384,128]{1,0:T(8,128)(2,1)S(1)}, u32[]{:S(2)}, u32[]{:S(2)}) collective-permute-start(bf16[384,128]{1,0:T(8,128)(2,1)} %get-tuple-element.46), channel_id=1, source_target_pairs={{0,16},{16,0},{1,17},{17,1},{2,18},{18,2},{3,19},{19,3},{4,20},{20... | collective-permute-start | bytes 294920 | tf_op jit(solution)/shard_map/ppermute | solution.py:375

commit v4 on v3

--- a/solution.py
+++ b/solution.py
@@ -200,12 +200,12 @@
             settle(b + 1)
 
 
-def attend(allowed, where, arrays, result, chunk_low, far_lows, low, high, heads_here):
+def attend(allowed, where, arrays, result, chunk_low, q_low, far_lows, low, high, heads_here):
     queries, q_rec, key, value, kv_rec, rim_a, rim_b, far = arrays
     rows = queries.shape[0]
     slots = allowed.shape[1]
     own = pl.BlockSpec((rows, HD), lambda i, w: (0, w[0] * heads_here + low + i))
-    flat = pl.BlockSpec((rows, HD), lambda i, w: (0, low + i))
+    asked = pl.BlockSpec((rows, HD), lambda i, w: (0, low - q_low + i))
     whole = pl.BlockSpec((2, rows, HD), lambda i, w: (0, 0, low + i))
     part = pl.BlockSpec((2, rows, HD), lambda i, w: (0, 0, low - chunk_low + i))
     tiles = [
@@ -216,7 +216,7 @@
     shape = jax.ShapeDtypeStruct((rows, (high - low) * HD), queries.dtype)
     inputs = [allowed, queries, q_rec, key, value, kv_rec, rim_a, rim_b, *far]
     specs = [pl.BlockSpec(memory_space=pltpu.SMEM)]
-    specs += [own, flat, own, own, part, whole, part] + tiles
+    specs += [own, asked, own, own, part, whole, part] + tiles
     aliases = {}
     kernel = attend_kernel
     if result is not None:
@@ -338,7 +338,10 @@
                 ("head", "blk"),
                 outward(1),
             )
-    q_rec = lax.ppermute(columns_of(queries, 1 - side, 0, group_width), "head", swap)
+    q_rec = []
+    for low, high in ((0, chunks[0][1]), (chunks[0][1], heads_here)):
+        asked = columns_of(queries, 1 - side, low * HD, (high - low) * HD)
+        q_rec.append((low, lax.ppermute(asked, "head", swap)))
 
     rim_b = []
     for c in range(len(chunks)):
@@ -368,9 +371,10 @@
     result, returned = None, []
     for c, a, b in head_runs(heads_here):
         far_lows, arrived = zip(*far[c])
-        arrays = (queries, q_rec, key_rows, value_rows, kv_rec[c], rim_a, rim_b[c], arrived)
+        q_low, q_part = q_rec[min(c, 1)]
+        arrays = (queries, q_part, key_rows, value_rows, kv_rec[c], rim_a, rim_b[c], arrived)
         result, sent = attend(
-            allowed, where, arrays, result, chunks[c][0], far_lows, a, b, heads_here
+            allowed, where, arrays, result, chunks[c][0], q_low, far_lows, a, b, heads_here
         )
         returned.append((a, lax.ppermute(sent, "head", swap)))
     result = place(
@@ -380,17 +384,16 @@
     return result
 
 
-far_jobs = tuple(tuple((i, (c,)) for i in range(2 * FAR - 1)) for c in range(3))
+far_jobs = tuple(tuple((i, (c,)) for i in range(2 * FAR - 1)) for c in range(4))
 
 
 def chunk_bounds(heads):
-    cuts = [0, heads * 3 // 10, heads * 7 // 10, heads]
+    cuts = [0, heads * 2 // 10, heads * 5 // 10, heads * 8 // 10, heads]
     return list(zip(cuts[:-1], cuts[1:]))
 
 
 def head_runs(heads):
-    first, second, (low, high) = chunk_bounds(heads)
-    return [(0, *first), (1, *second), (2, low, high - 1), (2, high - 1, high)]
+    return [(c, low, high) for c, (low, high) in enumerate(chunk_bounds(heads))]
 
 
 def solution(mesh):

time: 168 us -> 177 us (1.054)
  the two profiles are of different devices: /device:TPU:12 before, /device:TPU:0 now
where the time goes in v4:
time: 177 us; the launch traced here: 176 us
  starting transfers between devices  55.4 us (31%)
  waiting for transfers between devices  53.3 us (30%)
  Pallas kernels  46.8 us (26%)
  other arithmetic  12.8 us (7%)
  local copies, waits for them, and re-layouts  7.25 us (4%)
    ppermute x20, starting transfers between devices, on_device(): arrived = lax.ppermute(tile, 'blk', exchange(slabs, *shifts[i]))  39.3 us
    ppermute x20, waiting for transfers between devices, on_device(): arrived = lax.ppermute(tile, 'blk', exchange(slabs, *shifts[i]))  37.4 us
    pallas_call x4, Pallas kernels, attend(): pl.pallas_call(kernel, out_shape=[jax.ShapeDtypeStruct(queries.shape, que...  34.7 us
    ppermute x4, waiting for transfers between devices, on_device(): returned.append((a, lax.ppermute(sent, 'head', swap)))  10.6 us
    pallas_call x4, Pallas kernels, select_distant(): pl.pallas_call(functools.partial(distant_kernel, half, jobs, lows), out_s...  7.89 us
    another operation x5, other arithmetic, on_device(): jnp.stack([columns_of(array, 1 - side, low * HD, width) for array in (key...  7.09 us
    unnamed x54, local copies, waits for them, and re-layouts  6.51 us
    ppermute x4, waiting for transfers between devices, on_device(): kv_rec.append(lax.ppermute(packed, 'head', swap))  5.24 us
  transfers between devices with their start and end apart: 35, of which 10 were waited for; matrix products, arithmetic and copies ran while one was open for 8% of the time, Pallas kernels for 26%

profile of v4, /device:TPU:0, one launch (start us, length us, event | category | flops | bytes accessed | tf_op | source)
XLA Modules:
  0.0 176.0 jit_solution(18061986393564866797)
XLA Ops:
  0.0 1.0 shard_map.59
  1.0 3.0 %collective-permute-start.24 = (bf16[2,384,256]{2,1,0:T(8,128)(2,1)S(1)}, bf16[2,384,256]{2,1,0:T(8,128)(2,1)}, u32[]{:S(2)}, u32[]{:S(2)}) collective-permute-start(bf16[2,384,256]{2,1,0:T(8,128)(2,1)S(1)} %shard_map.59), channel_id=1, source_target_pairs={{0,16},{16,0},{1,17},{17,1},{2,18},{18,2},{3,19},{19,3},{4,20},{20... | collective-permute-start | bytes 1179656 | tf_op jit(solution)/shard_map/ppermute | solution.py:334
  4.1 1.5 shard_map.55
  5.6 3.8 %collective-permute-start.2 = (bf16[2,384,1280]{2,1,0:T(8,128)(2,1)S(1)}, bf16[2,384,1280]{2,1,0:T(8,128)(2,1)}, u32[]{:S(2)}, u32[]{:S(2)}) collective-permute-start(bf16[2,384,1280]{2,1,0:T(8,128)(2,1)S(1)} %shard_map.55), channel_id=1, source_target_pairs={{0,15},{1,0},{2,1},{3,2},{4,3},{5,4},{6,5},{7,6},{8,7},{9,8},{10,9... | collective-permute-start | bytes 5898248 | tf_op jit(solution)/shard_map/ppermute | solution.py:336
  9.4 1.2 slice_select_fusion.1
  10.6 1.3 select_bitcast_fusion.4
  11.9 0.8 pad_maximum_fusion.2
  12.7 2.0 %collective-permute-start.1 = (bf16[2,384,256]{2,1,0:T(8,128)(2,1)}, bf16[2,384,256]{2,1,0:T(8,128)(2,1)S(1)}, u32[]{:S(2)}, u32[]{:S(2)}) collective-permute-start(bf16[2,384,256]{2,1,0:T(8,128)(2,1)} %pad_maximum_fusion.2), channel_id=1, source_target_pairs={{0,16},{16,0},{1,17},{17,1},{2,18},{18,2},{3,19},{19,3},{4,20},{20... | collective-permute-start | bytes 1179656 | tf_op jit(solution)/shard_map/ppermute | solution.py:334
  14.7 2.1 %select_bitcast_fusion = (bf16[1,384,384]{2,1,0:T(8,128)(2,1)S(1)}, bf16[1,384,384]{2,1,0:T(8,128)(2,1)S(1)}, bf16[1,384,384]{2,1,0:T(8,128)(2,1)}, bf16[1,384,384]{2,1,0:T(8,128)(2,1)S(1)}) fusion(bf16[384,2560]{1,0:T(8,128)(2,1)} %refs_5_.5, pred[]{:T(512)S(6)} %eq.88, bf16[384,2560]{1,0:T(8,128)(2,1)S(1)} %copy-done.3), kind=kLoop, calls=%fused_computation.4 | loop fusion | flops 589824 | bytes 3538945 | tf_op jit(solution)/shard_map/stack | solution.py:331
  16.9 0.9 pad_maximum_fusion.1
  17.9 0.7 reduce_max.28.chosen
  18.6 1.9 %shard_map.60 = (bf16[2,128,256]{2,1,0:T(8,128)(2,1)S(1)}, bf16[2,128,256]{2,1,0:T(8,128)(2,1)S(1)}, bf16[2,128,256]{2,1,0:T(8,128)(2,1)S(1)}, bf16[2,128,256]{2,1,0:T(8,128)(2,1)S(1)}, bf16[2,128,256]{2,1,0:T(8,128)(2,1)S(1)}) custom-call(s32[16]{0:T(128)} %reduce_max.28.chosen, s32[1]{0:T(128)} %bitcast.where.refs_0_, s32[1]{0:T(128)} %bitcast.3.here, ...), custom_call_target="tpu_custom_call" | custom-call | tf_op jit(solution)/shard_map/pallas_call | solution.py:117
  20.6 1.0 collective-permute-start.27
  21.6 5.2 %collective-permute-done.1.rest_0_.refs_6_ = bf16[2,384,256]{2,1,0:T(8,128)(2,1)S(1)} collective-permute-done((bf16[2,384,256]{2,1,0:T(8,128)(2,1)}, bf16[2,384,256]{2,1,0:T(8,128)(2,1)S(1)}, u32[]{:S(2)}, u32[]{:S(2)}) %collective-permute-start.1) | collective-permute-done | bytes 393248 | tf_op jit(solution)/shard_map/ppermute | solution.py:334
  26.8 2.0 %pad_maximum_fusion = bf16[2,384,384]{2,1,0:T(8,128)(2,1)} fusion(bf16[1,384,384]{2,1,0:T(8,128)(2,1)S(1)} %get-tuple-element.64, bf16[1,384,384]{2,1,0:T(8,128)(2,1)} %get-tuple-element.65), kind=kLoop, calls=%fused_computation.1 | loop fusion | flops 294912 | bytes 1179648 | tf_op jit(solution)/shard_map/stack | solution.py:331
  28.8 9.6 %collective-permute-done.26.rest_0_ = bf16[2,128,256]{2,1,0:T(8,128)(2,1)S(1)} collective-permute-done((bf16[2,128,256]{2,1,0:T(8,128)(2,1)S(1)}, bf16[2,128,256]{2,1,0:T(8,128)(2,1)S(1)}, u32[]{:S(2)}, u32[]{:S(2)}) %collective-permute-start.26) | collective-permute-done | bytes 131104 | tf_op jit(solution)/shard_map/ppermute | solution.py:368
  39.7 2.3 %slice_select_fusion = bf16[384,1024]{1,0:T(8,128)(2,1)} fusion(bf16[384,2560]{1,0:T(8,128)(2,1)} %refs_2_.5, pred[]{:T(512)S(6)} %eq.88), kind=kLoop, calls=%fused_computation | loop fusion | flops 393216 | bytes 2359297 | tf_op jit(solution)/shard_map/jit(_where)/select_n | solution.py:27
  42.1 1.4 collective-permute-done.29.rest_3_
  43.5 1.9 %collective-permute-start = (bf16[384,1024]{1,0:T(8,128)(2,1)}, bf16[384,1024]{1,0:T(8,128)(2,1)}, u32[]{:S(2)}, u32[]{:S(2)}) collective-permute-start(bf16[384,1024]{1,0:T(8,128)(2,1)} %slice_select_fusion), channel_id=1, source_target_pairs={{0,16},{16,0},{1,17},{17,1},{2,18},{18,2},{3,19},{19,3},{4,20},{20... | collective-permute-start | bytes 2359304 | tf_op jit(solution)/shard_map/ppermute | solution.py:344
  45.4 0.7 copy-done.19
  46.1 1.9 %shard_map.56 = (bf16[2,128,256]{2,1,0:T(8,128)(2,1)S(1)}, bf16[2,128,256]{2,1,0:T(8,128)(2,1)S(1)}, bf16[2,128,256]{2,1,0:T(8,128)(2,1)S(1)}, bf16[2,128,256]{2,1,0:T(8,128)(2,1)S(1)}, bf16[2,128,256]{2,1,0:T(8,128)(2,1)S(1)}) custom-call(s32[16]{0:T(128)} %reduce_max.28.chosen, s32[1]{0:T(128)} %bitcast.where.refs_0_, s32[1]{0:T(128)} %bitcast.3.here, ...), custom_call_target="tpu_custom_call" | custom-call | tf_op jit(solution)/shard_map/pallas_call | solution.py:117
  50.0 5.0 %collective-permute-start.4 = (bf16[2,128,256]{2,1,0:T(8,128)(2,1)S(1)}, bf16[2,128,256]{2,1,0:T(8,128)(2,1)S(1)}, u32[]{:S(2)}, u32[]{:S(2)}) collective-permute-start(bf16[2,128,256]{2,1,0:T(8,128)(2,1)S(1)} %get-tuple-element.33), channel_id=1, source_target_pairs={{0,8},{1,9},{2,10},{3,11},{4,12},{5,13},{6,14},{7,15},{8,0},{9,1},... | collective-permute-start | bytes 393224 | tf_op jit(solution)/shard_map/ppermute | solution.py:368
  55.0 2.1 %shard_map.58 = (bf16[2,128,384]{2,1,0:T(8,128)(2,1)S(1)}, bf16[2,128,384]{2,1,0:T(8,128)(2,1)S(1)}, bf16[2,128,384]{2,1,0:T(8,128)(2,1)S(1)}, bf16[2,128,384]{2,1,0:T(8,128)(2,1)S(1)}, bf16[2,128,384]{2,1,0:T(8,128)(2,1)S(1)}) custom-call(s32[16]{0:T(128)} %reduce_max.28.chosen, s32[1]{0:T(128)} %bitcast.where.refs_0_, s32[1]{0:T(128)} %bitcast.3.here, ...), custom_call_target="tpu_custom_call" | custom-call | tf_op jit(solution)/shard_map/pallas_call | solution.py:117
  57.1 4.3 %collective-permute-done.4.refs_9_ = bf16[2,128,256]{2,1,0:T(8,128)(2,1)S(1)} collective-permute-done((bf16[2,128,256]{2,1,0:T(8,128)(2,1)S(1)}, bf16[2,128,256]{2,1,0:T(8,128)(2,1)S(1)}, u32[]{:S(2)}, u32[]{:S(2)}) %collective-permute-start.4) | collective-permute-done | bytes 131104 | tf_op jit(solution)/shard_map/ppermute | solution.py:368
  61.4 5.7 %collective-permute-start.19 = (bf16[2,128,384]{2,1,0:T(8,128)(2,1)S(1)}, bf16[2,128,384]{2,1,0:T(8,128)(2,1)S(1)}, u32[]{:S(2)}, u32[]{:S(2)}) collective-permute-start(bf16[2,128,384]{2,1,0:T(8,128)(2,1)S(1)} %get-tuple-element.44), channel_id=1, source_target_pairs={{0,4},{1,5},{2,6},{3,7},{4,0},{5,1},{6,2},{7,3},{8,12},{9,13},{10,... | collective-permute-start | bytes 589832 | tf_op jit(solution)/shard_map/ppermute | solution.py:368
  67.0 5.8 %collective-permute-done.18.refs_9_ = bf16[2,128,384]{2,1,0:T(8,128)(2,1)S(1)} collective-permute-done((bf16[2,128,384]{2,1,0:T(8,128)(2,1)S(1)}, bf16[2,128,384]{2,1,0:T(8,128)(2,1)S(1)}, u32[]{:S(2)}, u32[]{:S(2)}) %collective-permute-start.18) | collective-permute-done | bytes 196640 | tf_op jit(solution)/shard_map/ppermute | solution.py:368
  73.6 0.7 copy-done.8
  74.3 2.1 %shard_map.57 = (bf16[2,128,384]{2,1,0:T(8,128)(2,1)S(1)}, bf16[2,128,384]{2,1,0:T(8,128)(2,1)S(1)}, bf16[2,128,384]{2,1,0:T(8,128)(2,1)S(1)}, bf16[2,128,384]{2,1,0:T(8,128)(2,1)S(1)}, bf16[2,128,384]{2,1,0:T(8,128)(2,1)S(1)}) custom-call(s32[16]{0:T(128)} %reduce_max.28.chosen, s32[1]{0:T(128)} %bitcast.where.refs_0_, s32[1]{0:T(128)} %bitcast.3.here, ...), custom_call_target="tpu_custom_call" | custom-call | tf_op jit(solution)/shard_map/pallas_call | solution.py:117
  76.3 4.0 %collective-permute-done.21.refs_12_ = bf16[2,128,384]{2,1,0:T(8,128)(2,1)} collective-permute-done((bf16[2,128,384]{2,1,0:T(8,128)(2,1)S(1)}, bf16[2,128,384]{2,1,0:T(8,128)(2,1)}, u32[]{:S(2)}, u32[]{:S(2)}) %collective-permute-start.21) | collective-permute-done | bytes 196640 | tf_op jit(solution)/shard_map/ppermute | solution.py:368
  80.4 13.1 %collective-permute-start.12 = (bf16[2,128,384]{2,1,0:T(8,128)(2,1)S(1)}, bf16[2,128,384]{2,1,0:T(8,128)(2,1)S(1)}, u32[]{:S(2)}, u32[]{:S(2)}) collective-permute-start(bf16[2,128,384]{2,1,0:T(8,128)(2,1)S(1)} %get-tuple-element.39), channel_id=1, source_target_pairs={{0,4},{1,5},{2,6},{3,7},{4,0},{5,1},{6,2},{7,3},{8,12},{9,13},{10,... | collective-permute-start | bytes 589832 | tf_op jit(solution)/shard_map/ppermute | solution.py:368
  93.9 3.7 %collective-permute-done.12.refs_10_ = bf16[2,128,384]{2,1,0:T(8,128)(2,1)S(1)} collective-permute-done((bf16[2,128,384]{2,1,0:T(8,128)(2,1)S(1)}, bf16[2,128,384]{2,1,0:T(8,128)(2,1)S(1)}, u32[]{:S(2)}, u32[]{:S(2)}) %collective-permute-start.12) | collective-permute-done | bytes 196640 | tf_op jit(solution)/shard_map/ppermute | solution.py:368
  97.6 0.7 copy-done.11
  98.3 3.0 %collective-permute-start.15 = (bf16[2,128,384]{2,1,0:T(8,128)(2,1)S(1)}, bf16[2,128,384]{2,1,0:T(8,128)(2,1)S(1)}, u32[]{:S(2)}, u32[]{:S(2)}) collective-permute-start(bf16[2,128,384]{2,1,0:T(8,128)(2,1)S(1)} %get-tuple-element.42), channel_id=1, source_target_pairs={{0,1},{1,0},{2,4},{3,5},{4,2},{5,3},{6,8},{7,9},{8,6},{9,7},{10,12... | collective-permute-start | bytes 589832 | tf_op jit(solution)/shard_map/ppermute | solution.py:368
  102.0 8.6 %collective-permute-done.14.refs_12_ = bf16[2,128,384]{2,1,0:T(8,128)(2,1)S(1)} collective-permute-done((bf16[2,128,384]{2,1,0:T(8,128)(2,1)S(1)}, bf16[2,128,384]{2,1,0:T(8,128)(2,1)S(1)}, u32[]{:S(2)}, u32[]{:S(2)}) %collective-permute-start.14) | collective-permute-done | bytes 196640 | tf_op jit(solution)/shard_map/ppermute | solution.py:368
  110.6 5.5 %collective-permute-start.5 = (bf16[2,128,256]{2,1,0:T(8,128)(2,1)}, bf16[2,128,256]{2,1,0:T(8,128)(2,1)S(1)}, u32[]{:S(2)}, u32[]{:S(2)}) collective-permute-start(bf16[2,128,256]{2,1,0:T(8,128)(2,1)} %copy-done.2), channel_id=1, source_target_pairs={{0,4},{1,5},{2,6},{3,7},{4,0},{5,1},{6,2},{7,3},{8,12},{9,13},{10,... | collective-permute-start | bytes 393224 | tf_op jit(solution)/shard_map/ppermute | solution.py:368
  116.6 0.8 fusion.7
  117.5 5.6 %collective-permute-start.8 = (bf16[2,128,256]{2,1,0:T(8,128)(2,1)S(1)}, bf16[2,128,256]{2,1,0:T(8,128)(2,1)S(1)}, u32[]{:S(2)}, u32[]{:S(2)}) collective-permute-start(bf16[2,128,256]{2,1,0:T(8,128)(2,1)S(1)} %get-tuple-element.37), channel_id=1, source_target_pairs={{0,1},{1,0},{2,4},{3,5},{4,2},{5,3},{6,8},{7,9},{8,6},{9,7},{10,12... | collective-permute-start | bytes 393224 | tf_op jit(solution)/shard_map/ppermute | solution.py:368
  123.0 0.7 convert_reduce_fusion.allowed.refs_1_
  123.7 7.3 %shard_map.61 = (bf16[384,2560]{1,0:T(8,128)(2,1)}, bf16[384,256]{1,0:T(8,128)(2,1)}) custom-call(s32[1]{0:T(128)} %bitcast.where.refs_0_, s32[6,17]{1,0:T(8,128)} %convert_reduce_fusion.allowed.refs_1_, bf16[384,2560]{1,0:T(8,128)(2,1)} %refs_2_.5, bf16[384,256]{1,0:T(8,128)(2,1)} %collective-permute-done.23.q_rec, bf16[384,2560]{1,0:T(8,128)(2,1)} %refs_4_.5, ...), custom_call_target="tpu_custom_call" | custom-call | tf_op jit(solution)/shard_map/pallas_call | solution.py:226
  131.0 10.0 %shard_map.62 = (bf16[384,2560]{1,0:T(8,128)(2,1)}, bf16[384,384]{1,0:T(8,128)(2,1)}) custom-call(s32[1]{0:T(128)} %bitcast.where.refs_0_, s32[6,17]{1,0:T(8,128)} %convert_reduce_fusion.allowed.refs_1_, bf16[384,2560]{1,0:T(8,128)(2,1)} %refs_2_.5, bf16[384,1024]{1,0:T(8,128)(2,1)} %collective-permute-done.refs_3_, ...), custom_call_target="tpu_custom_call", output_to_operand_aliasing={{0}: (14, {})} | custom-call | tf_op jit(solution)/shard_map/pallas_call | solution.py:226
  141.1 10.1 %shard_map.63 = (bf16[384,2560]{1,0:T(8,128)(2,1)}, bf16[384,384]{1,0:T(8,128)(2,1)}) custom-call(s32[1]{0:T(128)} %bitcast.where.refs_0_, s32[6,17]{1,0:T(8,128)} %convert_reduce_fusion.allowed.refs_1_, bf16[384,2560]{1,0:T(8,128)(2,1)} %refs_2_.5, bf16[384,1024]{1,0:T(8,128)(2,1)} %collective-permute-done.refs_3_, ...), custom_call_target="tpu_custom_call", output_to_operand_aliasing={{0}: (14, {})} | custom-call | tf_op jit(solution)/shard_map/pallas_call | solution.py:226
  151.3 2.1 %collective-permute-start.33 = (bf16[384,384]{1,0:T(8,128)(2,1)S(1)}, bf16[384,384]{1,0:T(8,128)(2,1)S(1)}, u32[]{:S(2)}, u32[]{:S(2)}) collective-permute-start(bf16[384,384]{1,0:T(8,128)(2,1)S(1)} %copy-done.25), channel_id=1, source_target_pairs={{0,16},{16,0},{1,17},{17,1},{2,18},{18,2},{3,19},{19,3},{4,20},{20... | collective-permute-start | bytes 884744 | tf_op jit(solution)/shard_map/ppermute | solution.py:379
  154.3 7.3 %shard_map.64 = (bf16[384,2560]{1,0:T(8,128)(2,1)}, bf16[384,256]{1,0:T(8,128)(2,1)}) custom-call(s32[1]{0:T(128)} %bitcast.where.refs_0_, s32[6,17]{1,0:T(8,128)} %convert_reduce_fusion.allowed.refs_1_, bf16[384,2560]{1,0:T(8,128)(2,1)} %refs_2_.5, bf16[384,1024]{1,0:T(8,128)(2,1)} %collective-permute-done.refs_3_, ...), custom_call_target="tpu_custom_call", output_to_operand_aliasing={{0}: (14, {})} | custom-call | tf_op jit(solution)/shard_map/pallas_call | solution.py:226
  161.6 2.0 %collective-permute-start.31 = (bf16[384,256]{1,0:T(8,128)(2,1)}, bf16[384,256]{1,0:T(8,128)(2,1)S(1)}, u32[]{:S(2)}, u32[]{:S(2)}) collective-permute-start(bf16[384,256]{1,0:T(8,128)(2,1)} %get-tuple-element.56), channel_id=1, source_target_pairs={{0,16},{16,0},{1,17},{17,1},{2,18},{18,2},{3,19},{19,3},{4,20},{20... | collective-permute-start | bytes 589832 | tf_op jit(solution)/shard_map/ppermute | solution.py:379
  163.6 8.3 %collective-permute-done.32.refs_0_ = bf16[384,256]{1,0:T(8,128)(2,1)S(1)} collective-permute-done((bf16[384,256]{1,0:T(8,128)(2,1)S(1)}, bf16[384,256]{1,0:T(8,128)(2,1)S(1)}, u32[]{:S(2)}, u32[]{:S(2)}) %collective-permute-start.32) | collective-permute-done | bytes 196640 | tf_op jit(solution)/shard_map/ppermute | solution.py:379
  171.9 0.9 shard_map.65.refs_1_
  172.8 2.3 %collective-permute-done.31.refs_0_ = bf16[384,256]{1,0:T(8,128)(2,1)S(1)} collective-permute-done((bf16[384,256]{1,0:T(8,128)(2,1)}, bf16[384,256]{1,0:T(8,128)(2,1)S(1)}, u32[]{:S(2)}, u32[]{:S(2)}) %collective-permute-start.31) | collective-permute-done | bytes 196640 | tf_op jit(solution)/shard_map/ppermute | solution.py:379
  175.2 0.7 shard_map.66
  (102 shorter events, 7.0 us)
Async XLA Ops:
  1.0 17.6 %collective-permute-start.24 = (bf16[2,384,256]{2,1,0:T(8,128)(2,1)S(1)}, bf16[2,384,256]{2,1,0:T(8,128)(2,1)}, u32[]{:S(2)}, u32[]{:S(2)}) collective-permute-start(bf16[2,384,256]{2,1,0:T(8,128)(2,1)S(1)} %shard_map.59), channel_id=1, source_target_pairs={{0,16},{16,0},{1,17},{17,1},{2,18},{18,2},{3,19},{19,3},{4,20},{20... | collective-permute-start | bytes 1179656 | tf_op jit(solution)/shard_map/ppermute | solution.py:334
  5.6 111.9 %collective-permute-start.2 = (bf16[2,384,1280]{2,1,0:T(8,128)(2,1)S(1)}, bf16[2,384,1280]{2,1,0:T(8,128)(2,1)}, u32[]{:S(2)}, u32[]{:S(2)}) collective-permute-start(bf16[2,384,1280]{2,1,0:T(8,128)(2,1)S(1)} %shard_map.55), channel_id=1, source_target_pairs={{0,15},{1,0},{2,1},{3,2},{4,3},{5,4},{6,5},{7,6},{8,7},{9,8},{10,9... | collective-permute-start | bytes 5898248 | tf_op jit(solution)/shard_map/ppermute | solution.py:336
  9.4 5.3 %copy-start.3 = (bf16[384,2560]{1,0:T(8,128)(2,1)S(1)}, bf16[384,2560]{1,0:T(8,128)(2,1)}, u32[]{:S(2)}) copy-start(bf16[384,2560]{1,0:T(8,128)(2,1)} %refs_4_.5) | copy-start | bytes 5898244
  10.6 10.0 %collective-permute-start.23 = (bf16[384,256]{1,0:T(8,128)(2,1)S(1)}, bf16[384,256]{1,0:T(8,128)(2,1)}, u32[]{:S(2)}, u32[]{:S(2)}) collective-permute-start(bf16[384,256]{1,0:T(8,128)(2,1)S(1)} %slice_select_fusion.1), channel_id=1, source_target_pairs={{0,16},{16,0},{1,17},{17,1},{2,18},{18,2},{3,19},{19,3},{4,20},{20... | collective-permute-start | bytes 589832 | tf_op jit(solution)/shard_map/ppermute | solution.py:344
  12.7 5.1 %copy-start.23 = (s32[96,16]{0,1:T(8,128)S(1)}, s32[96,16]{0,1:T(8,128)}, u32[]{:S(2)}) copy-start(s32[96,16]{0,1:T(8,128)} %param.8) | copy-start | bytes 18436
  12.7 5.1 %copy-start.24 = (s32[96]{0:T(128)S(1)}, s32[96]{0:T(128)}, u32[]{:S(2)}) copy-start(s32[96]{0:T(128)} %param.9) | copy-start | bytes 1156
  12.7 14.1 %collective-permute-start.1 = (bf16[2,384,256]{2,1,0:T(8,128)(2,1)}, bf16[2,384,256]{2,1,0:T(8,128)(2,1)S(1)}, u32[]{:S(2)}, u32[]{:S(2)}) collective-permute-start(bf16[2,384,256]{2,1,0:T(8,128)(2,1)} %pad_maximum_fusion.2), channel_id=1, source_target_pairs={{0,16},{16,0},{1,17},{17,1},{2,18},{18,2},{3,19},{19,3},{4,20},{20... | collective-permute-start | bytes 1179656 | tf_op jit(solution)/shard_map/ppermute | solution.py:334
  17.7 32.2 %collective-permute-start.16 = (bf16[2,384,384]{2,1,0:T(8,128)(2,1)}, bf16[2,384,384]{2,1,0:T(8,128)(2,1)}, u32[]{:S(2)}, u32[]{:S(2)}) collective-permute-start(bf16[2,384,384]{2,1,0:T(8,128)(2,1)} %pad_maximum_fusion.1), channel_id=1, source_target_pairs={{0,16},{16,0},{1,17},{17,1},{2,18},{18,2},{3,19},{19,3},{4,20},{20... | collective-permute-start | bytes 1769480 | tf_op jit(solution)/shard_map/ppermute | solution.py:334
  20.5 17.9 %collective-permute-start.26 = (bf16[2,128,256]{2,1,0:T(8,128)(2,1)S(1)}, bf16[2,128,256]{2,1,0:T(8,128)(2,1)S(1)}, u32[]{:S(2)}, u32[]{:S(2)}) collective-permute-start(bf16[2,128,256]{2,1,0:T(8,128)(2,1)S(1)} %get-tuple-element.48), channel_id=1, source_target_pairs={{0,8},{1,9},{2,10},{3,11},{4,12},{5,13},{6,14},{7,15},{8,0},{9,1},... | collective-permute-start | bytes 393224 | tf_op jit(solution)/shard_map/ppermute | solution.py:368
  20.6 17.8 %collective-permute-start.27 = (bf16[2,128,256]{2,1,0:T(8,128)(2,1)S(1)}, bf16[2,128,256]{2,1,0:T(8,128)(2,1)S(1)}, u32[]{:S(2)}, u32[]{:S(2)}) collective-permute-start(bf16[2,128,256]{2,1,0:T(8,128)(2,1)S(1)} %get-tuple-element.49), channel_id=1, source_target_pairs={{0,4},{1,5},{2,6},{3,7},{4,0},{5,1},{6,2},{7,3},{8,12},{9,13},{10,... | collective-permute-start | bytes 393224 | tf_op jit(solution)/shard_map/ppermute | solution.py:368
  26.8 19.3 %copy-start.4 = (bf16[2,384,256]{2,1,0:T(8,128)(2,1)}, bf16[2,384,256]{2,1,0:T(8,128)(2,1)S(1)}, u32[]{:S(2)}) copy-start(bf16[2,384,256]{2,1,0:T(8,128)(2,1)S(1)} %collective-permute-done.1.rest_0_.refs_6_) | copy-start | bytes 1179652
  26.8 11.9 %collective-permute-start.28 = (bf16[2,128,256]{2,1,0:T(8,128)(2,1)S(1)}, bf16[2,128,256]{2,1,0:T(8,128)(2,1)S(1)}, u32[]{:S(2)}, u32[]{:S(2)}) collective-permute-start(bf16[2,128,256]{2,1,0:T(8,128)(2,1)S(1)} %get-tuple-element.50), channel_id=1, source_target_pairs={{0,1},{1,0},{2,3},{3,2},{4,8},{5,9},{6,10},{7,11},{8,4},{9,5},{10,... | collective-permute-start | bytes 393224 | tf_op jit(solution)/shard_map/ppermute | solution.py:368
  38.4 22.9 %collective-permute-start.9 = (bf16[2,384,384]{2,1,0:T(8,128)(2,1)}, bf16[2,384,384]{2,1,0:T(8,128)(2,1)}, u32[]{:S(2)}, u32[]{:S(2)}) collective-permute-start(bf16[2,384,384]{2,1,0:T(8,128)(2,1)} %pad_maximum_fusion), channel_id=1, source_target_pairs={{0,16},{16,0},{1,17},{17,1},{2,18},{18,2},{3,19},{19,3},{4,20},{20... | collective-permute-start | bytes 1769480 | tf_op jit(solution)/shard_map/ppermute | solution.py:334
  38.5 5.0 %collective-permute-start.29 = (bf16[2,128,256]{2,1,0:T(8,128)(2,1)S(1)}, bf16[2,128,256]{2,1,0:T(8,128)(2,1)S(1)}, u32[]{:S(2)}, u32[]{:S(2)}) collective-permute-start(bf16[2,128,256]{2,1,0:T(8,128)(2,1)S(1)} %get-tuple-element.51), channel_id=1, source_target_pairs={{0,2},{1,3},{2,0},{3,1},{4,6},{5,7},{6,4},{7,5},{8,10},{9,11},{10,... | collective-permute-start | bytes 393224 | tf_op jit(solution)/shard_map/ppermute | solution.py:368
  39.7 5.7 %collective-permute-start.30 = (bf16[2,128,256]{2,1,0:T(8,128)(2,1)S(1)}, bf16[2,128,256]{2,1,0:T(8,128)(2,1)S(1)}, u32[]{:S(2)}, u32[]{:S(2)}) collective-permute-start(bf16[2,128,256]{2,1,0:T(8,128)(2,1)S(1)} %get-tuple-element.52), channel_id=1, source_target_pairs={{0,1},{1,0},{2,4},{3,5},{4,2},{5,3},{6,8},{7,9},{8,6},{9,7},{10,12... | collective-permute-start | bytes 393224 | tf_op jit(solution)/shard_map/ppermute | solution.py:368
  43.5 49.9 %collective-permute-start = (bf16[384,1024]{1,0:T(8,128)(2,1)}, bf16[384,1024]{1,0:T(8,128)(2,1)}, u32[]{:S(2)}, u32[]{:S(2)}) collective-permute-start(bf16[384,1024]{1,0:T(8,128)(2,1)} %slice_select_fusion), channel_id=1, source_target_pairs={{0,16},{16,0},{1,17},{17,1},{2,18},{18,2},{3,19},{19,3},{4,20},{20... | collective-permute-start | bytes 2359304 | tf_op jit(solution)/shard_map/ppermute | solution.py:344
  46.1 20.9 %collective-permute-start.25 = (bf16[2,384,256]{2,1,0:T(8,128)(2,1)}, bf16[2,384,256]{2,1,0:T(8,128)(2,1)}, u32[]{:S(2)}, u32[]{:S(2)}) collective-permute-start(bf16[2,384,256]{2,1,0:T(8,128)(2,1)} %collective-permute-done.24.rest_0_.kv_rec), channel_id=1, source_target_pairs={{0,1},{1,2},{2,3},{3,4},{4,5},{5,6},{6,7},{7,8},{8,9},{9,10},{10,1... | collective-permute-start | bytes 1179656 | tf_op jit(solution)/shard_map/ppermute | solution.py:348
  50.0 11.4 %collective-permute-start.4 = (bf16[2,128,256]{2,1,0:T(8,128)(2,1)S(1)}, bf16[2,128,256]{2,1,0:T(8,128)(2,1)S(1)}, u32[]{:S(2)}, u32[]{:S(2)}) collective-permute-start(bf16[2,128,256]{2,1,0:T(8,128)(2,1)S(1)} %get-tuple-element.33), channel_id=1, source_target_pairs={{0,8},{1,9},{2,10},{3,11},{4,12},{5,13},{6,14},{7,15},{8,0},{9,1},... | collective-permute-start | bytes 393224 | tf_op jit(solution)/shard_map/ppermute | solution.py:368
  61.4 11.5 %copy-start.16 = (bf16[2,128,256]{2,1,0:T(8,128)(2,1)}, bf16[2,128,256]{2,1,0:T(8,128)(2,1)S(1)}, u32[]{:S(2)}) copy-start(bf16[2,128,256]{2,1,0:T(8,128)(2,1)S(1)} %collective-permute-done.4.refs_9_) | copy-start | bytes 393220
  61.4 11.4 %collective-permute-start.18 = (bf16[2,128,384]{2,1,0:T(8,128)(2,1)S(1)}, bf16[2,128,384]{2,1,0:T(8,128)(2,1)S(1)}, u32[]{:S(2)}, u32[]{:S(2)}) collective-permute-start(bf16[2,128,384]{2,1,0:T(8,128)(2,1)S(1)} %get-tuple-element.43), channel_id=1, source_target_pairs={{0,8},{1,9},{2,10},{3,11},{4,12},{5,13},{6,14},{7,15},{8,0},{9,1},... | collective-permute-start | bytes 589832 | tf_op jit(solution)/shard_map/ppermute | solution.py:368
  61.4 11.4 %collective-permute-start.19 = (bf16[2,128,384]{2,1,0:T(8,128)(2,1)S(1)}, bf16[2,128,384]{2,1,0:T(8,128)(2,1)S(1)}, u32[]{:S(2)}, u32[]{:S(2)}) collective-permute-start(bf16[2,128,384]{2,1,0:T(8,128)(2,1)S(1)} %get-tuple-element.44), channel_id=1, source_target_pairs={{0,4},{1,5},{2,6},{3,7},{4,0},{5,1},{6,2},{7,3},{8,12},{9,13},{10,... | collective-permute-start | bytes 589832 | tf_op jit(solution)/shard_map/ppermute | solution.py:368
  67.0 5.9 %collective-permute-start.20 = (bf16[2,128,384]{2,1,0:T(8,128)(2,1)S(1)}, bf16[2,128,384]{2,1,0:T(8,128)(2,1)S(1)}, u32[]{:S(2)}, u32[]{:S(2)}) collective-permute-start(bf16[2,128,384]{2,1,0:T(8,128)(2,1)S(1)} %get-tuple-element.45), channel_id=1, source_target_pairs={{0,1},{1,0},{2,3},{3,2},{4,8},{5,9},{6,10},{7,11},{8,4},{9,5},{10,... | collective-permute-start | bytes 589832 | tf_op jit(solution)/shard_map/ppermute | solution.py:368
  72.8 7.6 %collective-permute-start.21 = (bf16[2,128,384]{2,1,0:T(8,128)(2,1)S(1)}, bf16[2,128,384]{2,1,0:T(8,128)(2,1)}, u32[]{:S(2)}, u32[]{:S(2)}) collective-permute-start(bf16[2,128,384]{2,1,0:T(8,128)(2,1)S(1)} %get-tuple-element.46), channel_id=1, source_target_pairs={{0,2},{1,3},{2,0},{3,1},{4,6},{5,7},{6,4},{7,5},{8,10},{9,11},{10,... | collective-permute-start | bytes 589832 | tf_op jit(solution)/shard_map/ppermute | solution.py:368
  72.8 7.5 %collective-permute-start.22 = (bf16[2,128,384]{2,1,0:T(8,128)(2,1)S(1)}, bf16[2,128,384]{2,1,0:T(8,128)(2,1)}, u32[]{:S(2)}, u32[]{:S(2)}) collective-permute-start(bf16[2,128,384]{2,1,0:T(8,128)(2,1)S(1)} %get-tuple-element.47), channel_id=1, source_target_pairs={{0,1},{1,0},{2,4},{3,5},{4,2},{5,3},{6,8},{7,9},{8,6},{9,7},{10,12... | collective-permute-start | bytes 589832 | tf_op jit(solution)/shard_map/ppermute | solution.py:368
  74.3 41.8 %collective-permute-start.17 = (bf16[2,384,384]{2,1,0:T(8,128)(2,1)}, bf16[2,384,384]{2,1,0:T(8,128)(2,1)}, u32[]{:S(2)}, u32[]{:S(2)}) collective-permute-start(bf16[2,384,384]{2,1,0:T(8,128)(2,1)} %collective-permute-done.16.rest_0_.refs_6_), channel_id=1, source_target_pairs={{0,1},{1,2},{2,3},{3,4},{4,5},{5,6},{6,7},{7,8},{8,9},{9,10},{10,1... | collective-permute-start | bytes 1769480 | tf_op jit(solution)/shard_map/ppermute | solution.py:348
  80.4 13.1 %collective-permute-start.11 = (bf16[2,128,384]{2,1,0:T(8,128)(2,1)S(1)}, bf16[2,128,384]{2,1,0:T(8,128)(2,1)S(1)}, u32[]{:S(2)}, u32[]{:S(2)}) collective-permute-start(bf16[2,128,384]{2,1,0:T(8,128)(2,1)S(1)} %get-tuple-element.38), channel_id=1, source_target_pairs={{0,8},{1,9},{2,10},{3,11},{4,12},{5,13},{6,14},{7,15},{8,0},{9,1},... | collective-permute-start | bytes 589832 | tf_op jit(solution)/shard_map/ppermute | solution.py:368
  80.4 17.2 %collective-permute-start.12 = (bf16[2,128,384]{2,1,0:T(8,128)(2,1)S(1)}, bf16[2,128,384]{2,1,0:T(8,128)(2,1)S(1)}, u32[]{:S(2)}, u32[]{:S(2)}) collective-permute-start(bf16[2,128,384]{2,1,0:T(8,128)(2,1)S(1)} %get-tuple-element.39), channel_id=1, source_target_pairs={{0,4},{1,5},{2,6},{3,7},{4,0},{5,1},{6,2},{7,3},{8,12},{9,13},{10,... | collective-permute-start | bytes 589832 | tf_op jit(solution)/shard_map/ppermute | solution.py:368
  93.4 4.2 %collective-permute-start.13 = (bf16[2,128,384]{2,1,0:T(8,128)(2,1)S(1)}, bf16[2,128,384]{2,1,0:T(8,128)(2,1)S(1)}, u32[]{:S(2)}, u32[]{:S(2)}) collective-permute-start(bf16[2,128,384]{2,1,0:T(8,128)(2,1)S(1)} %get-tuple-element.40), channel_id=1, source_target_pairs={{0,1},{1,0},{2,3},{3,2},{4,8},{5,9},{6,10},{7,11},{8,4},{9,5},{10,... | collective-permute-start | bytes 589832 | tf_op jit(solution)/shard_map/ppermute | solution.py:368
  93.4 37.6 %copy-start.9 = (bf16[2,128,384]{2,1,0:T(8,128)(2,1)}, bf16[2,128,384]{2,1,0:T(8,128)(2,1)S(1)}, u32[]{:S(2)}) copy-start(bf16[2,128,384]{2,1,0:T(8,128)(2,1)S(1)} %collective-permute-done.11.refs_9_) | copy-start | bytes 589828
  93.4 24.0 %collective-permute-start.10 = (bf16[2,384,384]{2,1,0:T(8,128)(2,1)}, bf16[2,384,384]{2,1,0:T(8,128)(2,1)}, u32[]{:S(2)}, u32[]{:S(2)}) collective-permute-start(bf16[2,384,384]{2,1,0:T(8,128)(2,1)} %collective-permute-done.9.rest_0_.refs_6_), channel_id=1, source_target_pairs={{0,1},{1,2},{2,3},{3,4},{4,5},{5,6},{6,7},{7,8},{8,9},{9,10},{10,1... | collective-permute-start | bytes 1769480 | tf_op jit(solution)/shard_map/ppermute | solution.py:348
  97.6 33.4 %copy-start.10 = (bf16[2,128,384]{2,1,0:T(8,128)(2,1)}, bf16[2,128,384]{2,1,0:T(8,128)(2,1)S(1)}, u32[]{:S(2)}) copy-start(bf16[2,128,384]{2,1,0:T(8,128)(2,1)S(1)} %collective-permute-done.12.refs_10_) | copy-start | bytes 589828
  97.6 13.0 %collective-permute-start.14 = (bf16[2,128,384]{2,1,0:T(8,128)(2,1)S(1)}, bf16[2,128,384]{2,1,0:T(8,128)(2,1)S(1)}, u32[]{:S(2)}, u32[]{:S(2)}) collective-permute-start(bf16[2,128,384]{2,1,0:T(8,128)(2,1)S(1)} %get-tuple-element.41), channel_id=1, source_target_pairs={{0,2},{1,3},{2,0},{3,1},{4,6},{5,7},{6,4},{7,5},{8,10},{9,11},{10,... | collective-permute-start | bytes 589832 | tf_op jit(solution)/shard_map/ppermute | solution.py:368
  98.3 17.7 %collective-permute-start.15 = (bf16[2,128,384]{2,1,0:T(8,128)(2,1)S(1)}, bf16[2,128,384]{2,1,0:T(8,128)(2,1)S(1)}, u32[]{:S(2)}, u32[]{:S(2)}) collective-permute-start(bf16[2,128,384]{2,1,0:T(8,128)(2,1)S(1)} %get-tuple-element.42), channel_id=1, source_target_pairs={{0,1},{1,0},{2,4},{3,5},{4,2},{5,3},{6,8},{7,9},{8,6},{9,7},{10,12... | collective-permute-start | bytes 589832 | tf_op jit(solution)/shard_map/ppermute | solution.py:368
  110.6 20.4 %copy-start.12 = (bf16[2,128,384]{2,1,0:T(8,128)(2,1)}, bf16[2,128,384]{2,1,0:T(8,128)(2,1)S(1)}, u32[]{:S(2)}) copy-start(bf16[2,128,384]{2,1,0:T(8,128)(2,1)S(1)} %collective-permute-done.14.refs_12_) | copy-start | bytes 589828
  110.6 40.6 %collective-permute-start.5 = (bf16[2,128,256]{2,1,0:T(8,128)(2,1)}, bf16[2,128,256]{2,1,0:T(8,128)(2,1)S(1)}, u32[]{:S(2)}, u32[]{:S(2)}) collective-permute-start(bf16[2,128,256]{2,1,0:T(8,128)(2,1)} %copy-done.2), channel_id=1, source_target_pairs={{0,4},{1,5},{2,6},{3,7},{4,0},{5,1},{6,2},{7,3},{8,12},{9,13},{10,... | collective-permute-start | bytes 393224 | tf_op jit(solution)/shard_map/ppermute | solution.py:368
  116.1 15.0 %copy-start.13 = (bf16[2,128,384]{2,1,0:T(8,128)(2,1)}, bf16[2,128,384]{2,1,0:T(8,128)(2,1)S(1)}, u32[]{:S(2)}) copy-start(bf16[2,128,384]{2,1,0:T(8,128)(2,1)S(1)} %collective-permute-done.15.refs_13_) | copy-start | bytes 589828
  116.1 35.2 %collective-permute-start.6 = (bf16[2,128,256]{2,1,0:T(8,128)(2,1)}, bf16[2,128,256]{2,1,0:T(8,128)(2,1)S(1)}, u32[]{:S(2)}, u32[]{:S(2)}) collective-permute-start(bf16[2,128,256]{2,1,0:T(8,128)(2,1)} %copy-done.1), channel_id=1, source_target_pairs={{0,1},{1,0},{2,3},{3,2},{4,8},{5,9},{6,10},{7,11},{8,4},{9,5},{10,... | collective-permute-start | bytes 393224 | tf_op jit(solution)/shard_map/ppermute | solution.py:368
  116.1 37.4 %collective-permute-start.3 = (bf16[2,384,256]{2,1,0:T(8,128)(2,1)}, bf16[2,384,256]{2,1,0:T(8,128)(2,1)S(1)}, u32[]{:S(2)}, u32[]{:S(2)}) collective-permute-start(bf16[2,384,256]{2,1,0:T(8,128)(2,1)} %copy-done.4), channel_id=1, source_target_pairs={{0,1},{1,2},{2,3},{3,4},{4,5},{5,6},{6,7},{7,8},{8,9},{9,10},{10,1... | collective-permute-start | bytes 1179656 | tf_op jit(solution)/shard_map/ppermute | solution.py:348
  117.4 35.9 %collective-permute-start.7 = (bf16[2,128,256]{2,1,0:T(8,128)(2,1)}, bf16[2,128,256]{2,1,0:T(8,128)(2,1)}, u32[]{:S(2)}, u32[]{:S(2)}) collective-permute-start(bf16[2,128,256]{2,1,0:T(8,128)(2,1)} %copy-done), channel_id=1, source_target_pairs={{0,2},{1,3},{2,0},{3,1},{4,6},{5,7},{6,4},{7,5},{8,10},{9,11},{10,... | collective-permute-start | bytes 393224 | tf_op jit(solution)/shard_map/ppermute | solution.py:368
  117.5 36.0 %collective-permute-start.8 = (bf16[2,128,256]{2,1,0:T(8,128)(2,1)S(1)}, bf16[2,128,256]{2,1,0:T(8,128)(2,1)S(1)}, u32[]{:S(2)}, u32[]{:S(2)}) collective-permute-start(bf16[2,128,256]{2,1,0:T(8,128)(2,1)S(1)} %get-tuple-element.37), channel_id=1, source_target_pairs={{0,1},{1,0},{2,4},{3,5},{4,2},{5,3},{6,8},{7,9},{8,6},{9,7},{10,12... | collective-permute-start | bytes 393224 | tf_op jit(solution)/shard_map/ppermute | solution.py:368
  141.1 10.3 %copy-start.25 = (bf16[384,384]{1,0:T(8,128)(2,1)S(1)}, bf16[384,384]{1,0:T(8,128)(2,1)}, u32[]{:S(2)}) copy-start(bf16[384,384]{1,0:T(8,128)(2,1)} %get-tuple-element.58) | copy-start | bytes 884740
  141.1 12.3 %copy-start.26 = (bf16[384,256]{1,0:T(8,128)(2,1)S(1)}, bf16[384,256]{1,0:T(8,128)(2,1)}, u32[]{:S(2)}) copy-start(bf16[384,256]{1,0:T(8,128)(2,1)} %get-tuple-element.57) | copy-start | bytes 589828
  151.2 2.3 %copy-start.20 = (bf16[2,128,256]{2,1,0:T(8,128)(2,1)}, bf16[2,128,256]{2,1,0:T(8,128)(2,1)S(1)}, u32[]{:S(2)}) copy-start(bf16[2,128,256]{2,1,0:T(8,128)(2,1)S(1)} %collective-permute-done.5.refs_10_) | copy-start | bytes 393220
  151.2 20.7 %collective-permute-start.34 = (bf16[384,384]{1,0:T(8,128)(2,1)}, bf16[384,384]{1,0:T(8,128)(2,1)S(1)}, u32[]{:S(2)}, u32[]{:S(2)}) collective-permute-start(bf16[384,384]{1,0:T(8,128)(2,1)} %get-tuple-element.59), channel_id=1, source_target_pairs={{0,16},{16,0},{1,17},{17,1},{2,18},{18,2},{3,19},{19,3},{4,20},{20... | collective-permute-start | bytes 884744 | tf_op jit(solution)/shard_map/ppermute | solution.py:379
  151.3 2.2 %copy-start.21 = (bf16[2,128,256]{2,1,0:T(8,128)(2,1)}, bf16[2,128,256]{2,1,0:T(8,128)(2,1)S(1)}, u32[]{:S(2)}) copy-start(bf16[2,128,256]{2,1,0:T(8,128)(2,1)S(1)} %collective-permute-done.6.refs_11_) | copy-start | bytes 393220
  151.3 20.6 %collective-permute-start.33 = (bf16[384,384]{1,0:T(8,128)(2,1)S(1)}, bf16[384,384]{1,0:T(8,128)(2,1)S(1)}, u32[]{:S(2)}, u32[]{:S(2)}) collective-permute-start(bf16[384,384]{1,0:T(8,128)(2,1)S(1)} %copy-done.25), channel_id=1, source_target_pairs={{0,16},{16,0},{1,17},{17,1},{2,18},{18,2},{3,19},{19,3},{4,20},{20... | collective-permute-start | bytes 884744 | tf_op jit(solution)/shard_map/ppermute | solution.py:379
  153.4 18.5 %collective-permute-start.32 = (bf16[384,256]{1,0:T(8,128)(2,1)S(1)}, bf16[384,256]{1,0:T(8,128)(2,1)S(1)}, u32[]{:S(2)}, u32[]{:S(2)}) collective-permute-start(bf16[384,256]{1,0:T(8,128)(2,1)S(1)} %copy-done.26), channel_id=1, source_target_pairs={{0,16},{16,0},{1,17},{17,1},{2,18},{18,2},{3,19},{19,3},{4,20},{20... | collective-permute-start | bytes 589832 | tf_op jit(solution)/shard_map/ppermute | solution.py:379
  161.6 13.5 %collective-permute-start.31 = (bf16[384,256]{1,0:T(8,128)(2,1)}, bf16[384,256]{1,0:T(8,128)(2,1)S(1)}, u32[]{:S(2)}, u32[]{:S(2)}) collective-permute-start(bf16[384,256]{1,0:T(8,128)(2,1)} %get-tuple-element.56), channel_id=1, source_target_pairs={{0,16},{16,0},{1,17},{17,1},{2,18},{18,2},{3,19},{19,3},{4,20},{20... | collective-permute-start | bytes 589832 | tf_op jit(solution)/shard_map/ppermute | solution.py:379
  (14 other events, 10.9 us)
